TPU v7x, 32 devices: a whole 2x2x4 slice. The times are simulated.
32 devices in a mesh: tile: 8 (over z, x), wave: 4 (over y, core).
Axes of the slice: x: 2, y: 2, z: 4, core: 2. Of those that a mesh axis runs over, the one named last changes fastest.
Arguments:
- fibre_data: bfloat16 [128, 256, 128], P('wave', 'tile'), may hold values from -162 to 162
- kernels: bfloat16 [4, 256, 4, 128, 128], P('wave', 'tile'), may hold values from -0.25 to 0.25
- block_index: int32 [4, 256, 4], P('wave', 'tile'), may hold values from 0 to 127, as said below
- live_count: int32 [8], P('tile'), may hold values from 8 to 32, as said below
Outputs:
- solution: float32 [128, 128, 128], P('wave', 'tile')
- residual: float32 [128, 128, 128], P('wave', 'tile')
Inputs may be any that keep to these rules, and one draw needn't show every extreme that they name: `block_index`: A group of tile t (groups t * 32 to (t + 1) * 32 - 1) names only blocks from max(t * 16 - 4, 0) to min((t + 1) * 16 + 4, 128) - 1; for every kernel set and tile, some live group of that tile names both ends of that range. `live_count`: some tile has all 32 groups live.
All inputs are finite; a program needn't handle non-finite values.
Results may differ from a plain program's by a relative error of at most 0.035.
Values may be sent and summed in bfloat16 or wider, within the bound.
No kernel may reach another device: no remote copies, remote signals or barrier semaphores. Data moves between devices by JAX's collectives and lax.ppermute only.
A program may use at most 64 MiB of HBM per device.

v0:
```python
import jax
import jax.numpy as jnp
from jax import lax
from jax.sharding import PartitionSpec as P

HALO_BLOCKS = 4
BLOCKS_DEV = 16
ITERATIONS = 3


TIKHONOV = 0.5


def from_behind(value, axis, by):
    size = lax.axis_size(axis)
    pairs = [(i, i + by) for i in range(size) if 0 <= i + by < size]
    return lax.ppermute(value, axis, pairs)


def extended(value, sides, width):
    for axis, dim in sides:
        size, length = (lax.axis_size(axis), value.shape[dim])
        up = [(i, (i + 1) % size) for i in range(size - 1)]
        down = [(j, i) for i, j in up]
        last = lax.slice_in_dim(value, length - width, length, axis=dim)
        initial = lax.slice_in_dim(value, 0, width, axis=dim)
        before = lax.ppermute(last, axis, up)
        after = lax.ppermute(initial, axis, down)
        value = jnp.concatenate([before, value, after], axis=dim)
    return value


def select_table(local_index, extent):
    return (local_index[..., None] == jnp.arange(extent, dtype=jnp.int32)).astype(jnp.bfloat16)


def forward_image(window16, kernels, selector16, live_mask):
    kernel_sets = kernels.shape[0]
    shaped = window16.reshape(
        kernel_sets, window16.shape[0] // kernel_sets, window16.shape[1], window16.shape[2]
    )
    picked = jnp.einsum(
        "cgrb,cwbs->cwgrs", selector16, shaped, preferred_element_type=jnp.float32
    ).astype(jnp.bfloat16)
    applied = jnp.einsum("cwgrs,cgrsf->cwgf", picked, kernels, preferred_element_type=jnp.float32)
    return (applied * live_mask[None, None, :, None]).astype(jnp.bfloat16)


def adjoint_image(image16, kernels, selector16):
    spread = jnp.einsum("cwgf,cgrsf->cwgrs", image16, kernels, preferred_element_type=jnp.float32)
    upper_part = spread.astype(jnp.bfloat16)
    lower_part = (spread - upper_part.astype(jnp.float32)).astype(jnp.bfloat16)
    summed = jnp.einsum(
        "cgrb,cwgrs->cwbs", selector16, upper_part, preferred_element_type=jnp.float32
    )
    summed = summed + jnp.einsum(
        "cgrb,cwgrs->cwbs", selector16, lower_part, preferred_element_type=jnp.float32
    )
    return summed.reshape(summed.shape[0] * summed.shape[1], summed.shape[2], summed.shape[3])


def shards(fibre_data, kernels, block_index, live_count):
    extent = BLOCKS_DEV + 2 * HALO_BLOCKS
    first_block = lax.axis_index("tile") * BLOCKS_DEV - HALO_BLOCKS
    selector16 = select_table(block_index - first_block, extent)
    groups = block_index.shape[1]
    live_mask = (jnp.arange(groups, dtype=jnp.int32) < live_count[0]).astype(jnp.float32)
    kernel_sets = kernels.shape[0]
    observed = fibre_data * live_mask.astype(jnp.bfloat16)[None, :, None]
    observed = observed.reshape(
        kernel_sets, fibre_data.shape[0] // kernel_sets, groups, fibre_data.shape[2]
    )
    partial_rhs = adjoint_image(observed, kernels, selector16)
    rim_width = HALO_BLOCKS

    def settle(partial_value):
        owned_part = partial_value[:, rim_width : rim_width + BLOCKS_DEV]
        from_right = from_behind(
            partial_value[:, :rim_width].astype(jnp.bfloat16), "tile", -1
        ).astype(jnp.float32)
        from_left = from_behind(
            partial_value[:, BLOCKS_DEV + rim_width :].astype(jnp.bfloat16), "tile", 1
        ).astype(jnp.float32)
        owned_part = owned_part.at[:, :rim_width].add(from_left)
        return owned_part.at[:, BLOCKS_DEV - rim_width :].add(from_right)

    def operate(vector):
        padded = extended(vector.astype(jnp.bfloat16), (("tile", 1),), HALO_BLOCKS)
        image16 = forward_image(padded, kernels, selector16, live_mask)
        return settle(adjoint_image(image16, kernels, selector16)) + TIKHONOV * vector

    def local_inner(first_vector, second_vector):
        return jnp.sum(first_vector * second_vector)

    rhs = settle(partial_rhs)
    solution = jnp.zeros_like(rhs)
    residual = rhs

    def paired(vector, applied):
        return lax.psum(
            (local_inner(vector, vector), local_inner(vector, applied)), ("tile", "wave")
        )

    applied = operate(residual)
    current, product = paired(residual, applied)
    step_size = current / product
    direction = residual
    applied_dir = applied
    for iteration in range(ITERATIONS):
        solution = solution + step_size * direction
        residual = residual - step_size * applied_dir
        if iteration + 1 < ITERATIONS:
            applied = operate(residual)
            following, product = paired(residual, applied)
            beta_ratio = following / current
            step_size = following / (product - beta_ratio * following / step_size)
            direction = residual + beta_ratio * direction
            applied_dir = applied + beta_ratio * applied_dir
            current = following
    return (solution, residual)


def solution(mesh):
    in_specs = (
        P("wave", "tile", None),
        P("wave", "tile", None, None, None),
        P("wave", "tile", None),
        P("tile"),
    )
    out_specs = (P("wave", "tile", None), P("wave", "tile", None))
    return jax.shard_map(shards, mesh=mesh, in_specs=in_specs, out_specs=out_specs, check_vma=False)
```

profile of v0, /device:TPU:0, one launch (start us, length us, event | category | flops | bytes accessed | tf_op | source)
XLA Modules:
  0.0 242.5 jit_solution(4463199943497567733)
XLA Ops:
  1.3 1.0 multiply_bitcast_fusion
  2.3 3.7 %fusion.12 = f32[32,32,4,128]{3,1,2,0:T(8,128)S(1)} fusion(bf16[1,32,4,128,128]{4,3,2,1,0:T(8,128)(2,1)} %param.21, bf16[32,32,128,1]{2,1,0,3:T(8,128)(2,1)S(1)} %multiply_bitcast_fusion), kind=kOutput, calls=%fused_computation.12 | convolution fusion | flops 134217728 | bytes 6553600 | tf_op jit(solution)/shard_map/cwgf,cgrsf->cwgrs/dot_general | solution.py:50
  6.1 0.3 fusion.71
  6.6 0.4 copy-done.4
  7.0 0.7 convolution_bitcast_fusion.6
  7.7 0.7 fusion.153
  8.4 4.9 %collective-permute-start = (bf16[32,4,128]{2,1,0:T(4,128)(2,1)S(1)}, bf16[32,4,128]{2,1,0:T(4,128)(2,1)S(1)}, u32[]{:S(2)}, u32[]{:S(2)}) collective-permute-start(bf16[32,4,128]{2,1,0:T(4,128)(2,1)S(1)} %get-tuple-element.124), channel_id=1, source_target_pairs={{0,4},{4,8},{8,12},{12,16},{16,20},{20,24},{24,28},{1,5},{5,9},{9,... | collective-permute-start | bytes 98312 | tf_op jit(solution)/shard_map/ppermute | solution.py:17
  13.3 1.3 collective-permute-start.1
  14.9 4.2 %collective-permute-done.1 = bf16[32,4,128]{2,1,0:T(4,128)(2,1)S(1)} collective-permute-done((bf16[32,4,128]{2,1,0:T(4,128)(2,1)S(1)}, bf16[32,4,128]{2,1,0:T(4,128)(2,1)S(1)}, u32[]{:S(2)}, u32[]{:S(2)}) %collective-permute-start.1) | collective-permute-done | bytes 32800 | tf_op jit(solution)/shard_map/ppermute | solution.py:17
  19.2 1.3 collective-permute-start.3
  20.5 5.0 %collective-permute-start.2 = (bf16[32,4,128]{2,1,0:T(4,128)(2,1)S(1)}, bf16[32,4,128]{2,1,0:T(4,128)(2,1)S(1)}, u32[]{:S(2)}, u32[]{:S(2)}) collective-permute-start(bf16[32,4,128]{2,1,0:T(4,128)(2,1)S(1)} %get-tuple-element.129), channel_id=1, source_target_pairs={{0,4},{4,8},{8,12},{12,16},{16,20},{20,24},{24,28},{1,5},{5,9},{9,... | collective-permute-start | bytes 98312 | tf_op jit(solution)/shard_map/ppermute | solution.py:27
  25.6 1.6 collective-permute-done.2
  27.1 0.5 fusion.18
  27.6 6.0 %fusion.8 = f32[32,32,4,128]{3,1,2,0:T(8,128)S(1)} fusion(bf16[1,32,4,128,128]{4,3,2,1,0:T(8,128)(2,1)} %param.21, bf16[32,32,4,128]{3,1,2,0:T(8,128)(2,1)S(1)} %fusion.18, f32[32]{0:T(128)S(1)} %compare_convert_fusion), kind=kOutput, calls=%fused_computation.8 | convolution fusion | flops 268697600 | bytes 7340160 | tf_op jit(solution)/shard_map/cwgf,cgrsf->cwgrs/dot_general | solution.py:50
  33.6 0.3 fusion.72
  34.2 0.7 convolution_bitcast_fusion.4
  34.8 0.7 fusion.154
  35.6 4.8 %collective-permute-start.4 = (bf16[32,4,128]{2,1,0:T(4,128)(2,1)S(1)}, bf16[32,4,128]{2,1,0:T(4,128)(2,1)S(1)}, u32[]{:S(2)}, u32[]{:S(2)}) collective-permute-start(bf16[32,4,128]{2,1,0:T(4,128)(2,1)S(1)} %get-tuple-element.122), channel_id=1, source_target_pairs={{0,4},{4,8},{8,12},{12,16},{16,20},{20,24},{24,28},{1,5},{5,9},{9,... | collective-permute-start | bytes 98312 | tf_op jit(solution)/shard_map/ppermute | solution.py:17
  40.4 1.3 collective-permute-start.5
  42.0 5.4 %collective-permute-done.5 = bf16[32,4,128]{2,1,0:T(4,128)(2,1)S(1)} collective-permute-done((bf16[32,4,128]{2,1,0:T(4,128)(2,1)S(1)}, bf16[32,4,128]{2,1,0:T(4,128)(2,1)S(1)}, u32[]{:S(2)}, u32[]{:S(2)}) %collective-permute-start.5) | collective-permute-done | bytes 32800 | tf_op jit(solution)/shard_map/ppermute | solution.py:17
  47.5 0.7 multiply_reduce_fusion.4
  48.2 42.1 %all-reduce.2 = (f32[]{:T(128)}, f32[]{:T(128)}) all-reduce(f32[]{:T(128)} %get-tuple-element.103, f32[]{:T(128)} %get-tuple-element.102), channel_id=1, replica_groups=mesh['tile'=8,'wave'=4] {'tile','wave'}, use_global_device_ids=true, to_apply=%region_1.0 | all-reduce | flops 2 | bytes 16 | tf_op jit(solution)/shard_map/psum | solution.py:100
  91.7 1.3 collective-permute-start.7
  93.0 5.0 %collective-permute-start.6 = (bf16[32,4,128]{2,1,0:T(4,128)(2,1)S(1)}, bf16[32,4,128]{2,1,0:T(4,128)(2,1)S(1)}, u32[]{:S(2)}, u32[]{:S(2)}) collective-permute-start(bf16[32,4,128]{2,1,0:T(4,128)(2,1)S(1)} %get-tuple-element.127), channel_id=1, source_target_pairs={{0,4},{4,8},{8,12},{12,16},{16,20},{20,24},{24,28},{1,5},{5,9},{9,... | collective-permute-start | bytes 98312 | tf_op jit(solution)/shard_map/ppermute | solution.py:27
  98.0 1.4 collective-permute-done.6
  99.4 1.5 fusion.19
  100.8 6.3 %fusion.4 = f32[32,32,4,128]{3,1,2,0:T(8,128)S(1)} fusion(bf16[1,32,4,128,128]{4,3,2,1,0:T(8,128)(2,1)} %param.21, bf16[32,32,4,128]{3,1,2,0:T(8,128)(2,1)} %fusion.19, f32[32]{0:T(128)S(1)} %compare_convert_fusion), kind=kOutput, calls=%fused_computation.4 | convolution fusion | flops 268697600 | bytes 7340160 | tf_op jit(solution)/shard_map/cwgf,cgrsf->cwgrs/dot_general | solution.py:50
  107.7 0.7 convolution_bitcast_fusion.2
  108.4 0.7 fusion.155
  109.1 4.8 %collective-permute-start.8 = (bf16[32,4,128]{2,1,0:T(4,128)(2,1)S(1)}, bf16[32,4,128]{2,1,0:T(4,128)(2,1)S(1)}, u32[]{:S(2)}, u32[]{:S(2)}) collective-permute-start(bf16[32,4,128]{2,1,0:T(4,128)(2,1)S(1)} %get-tuple-element.120), channel_id=1, source_target_pairs={{0,4},{4,8},{8,12},{12,16},{16,20},{20,24},{24,28},{1,5},{5,9},{9,... | collective-permute-start | bytes 98312 | tf_op jit(solution)/shard_map/ppermute | solution.py:17
  113.9 1.3 collective-permute-start.9
  115.5 5.4 %collective-permute-done.9 = bf16[32,4,128]{2,1,0:T(4,128)(2,1)S(1)} collective-permute-done((bf16[32,4,128]{2,1,0:T(4,128)(2,1)S(1)}, bf16[32,4,128]{2,1,0:T(4,128)(2,1)S(1)}, u32[]{:S(2)}, u32[]{:S(2)}) %collective-permute-start.9) | collective-permute-done | bytes 32800 | tf_op jit(solution)/shard_map/ppermute | solution.py:17
  121.0 0.7 multiply_reduce_fusion.2
  121.7 39.7 %all-reduce.1 = (f32[]{:T(128)}, f32[]{:T(128)}) all-reduce(f32[]{:T(128)} %get-tuple-element.101, f32[]{:T(128)} %get-tuple-element.100), channel_id=1, replica_groups=mesh['tile'=8,'wave'=4] {'tile','wave'}, use_global_device_ids=true, to_apply=%region_5.0 | all-reduce | flops 2 | bytes 16 | tf_op jit(solution)/shard_map/psum | solution.py:100
  166.0 0.9 fusion.144
  166.9 1.3 collective-permute-start.11
  168.2 4.8 %collective-permute-start.10 = (bf16[32,4,128]{2,1,0:T(4,128)(2,1)S(1)}, bf16[32,4,128]{2,1,0:T(4,128)(2,1)S(1)}, u32[]{:S(2)}, u32[]{:S(2)}) collective-permute-start(bf16[32,4,128]{2,1,0:T(4,128)(2,1)S(1)} %get-tuple-element.125), channel_id=1, source_target_pairs={{0,4},{4,8},{8,12},{12,16},{16,20},{20,24},{24,28},{1,5},{5,9},{9,... | collective-permute-start | bytes 98312 | tf_op jit(solution)/shard_map/ppermute | solution.py:27
  173.0 1.6 collective-permute-done.10
  174.6 0.5 fusion.20
  175.1 6.0 %fusion = f32[32,32,4,128]{3,1,2,0:T(8,128)S(1)} fusion(bf16[1,32,4,128,128]{4,3,2,1,0:T(8,128)(2,1)} %param.21, bf16[32,32,4,128]{3,1,2,0:T(8,128)(2,1)S(1)} %fusion.20, f32[32]{0:T(128)S(1)} %compare_convert_fusion), kind=kOutput, calls=%fused_computation | convolution fusion | flops 268697600 | bytes 7340160 | tf_op jit(solution)/shard_map/cwgf,cgrsf->cwgrs/dot_general | solution.py:50
  181.7 0.7 convolution_bitcast_fusion
  182.4 0.7 fusion.156
  183.1 4.8 %collective-permute-start.12 = (bf16[32,4,128]{2,1,0:T(4,128)(2,1)S(1)}, bf16[32,4,128]{2,1,0:T(4,128)(2,1)S(1)}, u32[]{:S(2)}, u32[]{:S(2)}) collective-permute-start(bf16[32,4,128]{2,1,0:T(4,128)(2,1)S(1)} %get-tuple-element.118), channel_id=1, source_target_pairs={{0,4},{4,8},{8,12},{12,16},{16,20},{20,24},{24,28},{1,5},{5,9},{9,... | collective-permute-start | bytes 98312 | tf_op jit(solution)/shard_map/ppermute | solution.py:17
  187.9 1.3 collective-permute-start.13
  189.5 5.4 %collective-permute-done.13 = bf16[32,4,128]{2,1,0:T(4,128)(2,1)S(1)} collective-permute-done((bf16[32,4,128]{2,1,0:T(4,128)(2,1)S(1)}, bf16[32,4,128]{2,1,0:T(4,128)(2,1)S(1)}, u32[]{:S(2)}, u32[]{:S(2)}) %collective-permute-start.13) | collective-permute-done | bytes 32800 | tf_op jit(solution)/shard_map/ppermute | solution.py:17
  195.0 0.7 multiply_reduce_fusion
  195.7 42.1 %all-reduce = (f32[]{:T(128)}, f32[]{:T(128)}) all-reduce(f32[]{:T(128)} %get-tuple-element.99, f32[]{:T(128)} %get-tuple-element.98), channel_id=1, replica_groups=mesh['tile'=8,'wave'=4] {'tile','wave'}, use_global_device_ids=true, to_apply=%region_9.0 | all-reduce | flops 2 | bytes 16 | tf_op jit(solution)/shard_map/psum | solution.py:100
  241.6 0.9 multiply_subtract_fusion
  (46 shorter events, 3.2 us)
Async XLA Ops:
  6.4 0.7 copy-start.4
  8.4 6.5 %collective-permute-start = (bf16[32,4,128]{2,1,0:T(4,128)(2,1)S(1)}, bf16[32,4,128]{2,1,0:T(4,128)(2,1)S(1)}, u32[]{:S(2)}, u32[]{:S(2)}) collective-permute-start(bf16[32,4,128]{2,1,0:T(4,128)(2,1)S(1)} %get-tuple-element.124), channel_id=1, source_target_pairs={{0,4},{4,8},{8,12},{12,16},{16,20},{20,24},{24,28},{1,5},{5,9},{9,... | collective-permute-start | bytes 98312 | tf_op jit(solution)/shard_map/ppermute | solution.py:17
  13.3 5.8 %collective-permute-start.1 = (bf16[32,4,128]{2,1,0:T(4,128)(2,1)S(1)}, bf16[32,4,128]{2,1,0:T(4,128)(2,1)S(1)}, u32[]{:S(2)}, u32[]{:S(2)}) collective-permute-start(bf16[32,4,128]{2,1,0:T(4,128)(2,1)S(1)} %get-tuple-element.123), channel_id=1, source_target_pairs={{4,0},{8,4},{12,8},{16,12},{20,16},{24,20},{28,24},{5,1},{9,5},{13... | collective-permute-start | bytes 98312 | tf_op jit(solution)/shard_map/ppermute | solution.py:17
  19.2 6.3 %collective-permute-start.3 = (bf16[32,4,128]{2,1,0:T(4,128)(2,1)S(1)}, bf16[32,4,128]{2,1,0:T(4,128)(2,1)S(1)}, u32[]{:S(2)}, u32[]{:S(2)}) collective-permute-start(bf16[32,4,128]{2,1,0:T(4,128)(2,1)S(1)} %get-tuple-element.130), channel_id=1, source_target_pairs={{4,0},{8,4},{12,8},{16,12},{20,16},{24,20},{28,24},{5,1},{9,5},{13... | collective-permute-start | bytes 98312 | tf_op jit(solution)/shard_map/ppermute | solution.py:28
  20.5 6.6 %collective-permute-start.2 = (bf16[32,4,128]{2,1,0:T(4,128)(2,1)S(1)}, bf16[32,4,128]{2,1,0:T(4,128)(2,1)S(1)}, u32[]{:S(2)}, u32[]{:S(2)}) collective-permute-start(bf16[32,4,128]{2,1,0:T(4,128)(2,1)S(1)} %get-tuple-element.129), channel_id=1, source_target_pairs={{0,4},{4,8},{8,12},{12,16},{16,20},{20,24},{24,28},{1,5},{5,9},{9,... | collective-permute-start | bytes 98312 | tf_op jit(solution)/shard_map/ppermute | solution.py:27
  35.6 6.4 %collective-permute-start.4 = (bf16[32,4,128]{2,1,0:T(4,128)(2,1)S(1)}, bf16[32,4,128]{2,1,0:T(4,128)(2,1)S(1)}, u32[]{:S(2)}, u32[]{:S(2)}) collective-permute-start(bf16[32,4,128]{2,1,0:T(4,128)(2,1)S(1)} %get-tuple-element.122), channel_id=1, source_target_pairs={{0,4},{4,8},{8,12},{12,16},{16,20},{20,24},{24,28},{1,5},{5,9},{9,... | collective-permute-start | bytes 98312 | tf_op jit(solution)/shard_map/ppermute | solution.py:17
  40.4 7.0 %collective-permute-start.5 = (bf16[32,4,128]{2,1,0:T(4,128)(2,1)S(1)}, bf16[32,4,128]{2,1,0:T(4,128)(2,1)S(1)}, u32[]{:S(2)}, u32[]{:S(2)}) collective-permute-start(bf16[32,4,128]{2,1,0:T(4,128)(2,1)S(1)} %get-tuple-element.121), channel_id=1, source_target_pairs={{4,0},{8,4},{12,8},{16,12},{20,16},{24,20},{28,24},{5,1},{9,5},{13... | collective-permute-start | bytes 98312 | tf_op jit(solution)/shard_map/ppermute | solution.py:17
  91.7 74.3 %copy-start = (f32[32,16,128]{2,1,0:T(8,128)}, f32[32,16,128]{2,1,0:T(8,128)S(1)}, u32[]{:S(2)}) copy-start(f32[32,16,128]{2,1,0:T(8,128)S(1)} %get-tuple-element.114) | copy-start | bytes 786436
  91.7 6.3 %collective-permute-start.7 = (bf16[32,4,128]{2,1,0:T(4,128)(2,1)S(1)}, bf16[32,4,128]{2,1,0:T(4,128)(2,1)S(1)}, u32[]{:S(2)}, u32[]{:S(2)}) collective-permute-start(bf16[32,4,128]{2,1,0:T(4,128)(2,1)S(1)} %get-tuple-element.128), channel_id=1, source_target_pairs={{4,0},{8,4},{12,8},{16,12},{20,16},{24,20},{28,24},{5,1},{9,5},{13... | collective-permute-start | bytes 98312 | tf_op jit(solution)/shard_map/ppermute | solution.py:28
  93.0 6.4 %collective-permute-start.6 = (bf16[32,4,128]{2,1,0:T(4,128)(2,1)S(1)}, bf16[32,4,128]{2,1,0:T(4,128)(2,1)S(1)}, u32[]{:S(2)}, u32[]{:S(2)}) collective-permute-start(bf16[32,4,128]{2,1,0:T(4,128)(2,1)S(1)} %get-tuple-element.127), channel_id=1, source_target_pairs={{0,4},{4,8},{8,12},{12,16},{16,20},{20,24},{24,28},{1,5},{5,9},{9,... | collective-permute-start | bytes 98312 | tf_op jit(solution)/shard_map/ppermute | solution.py:27
  109.1 6.4 %collective-permute-start.8 = (bf16[32,4,128]{2,1,0:T(4,128)(2,1)S(1)}, bf16[32,4,128]{2,1,0:T(4,128)(2,1)S(1)}, u32[]{:S(2)}, u32[]{:S(2)}) collective-permute-start(bf16[32,4,128]{2,1,0:T(4,128)(2,1)S(1)} %get-tuple-element.120), channel_id=1, source_target_pairs={{0,4},{4,8},{8,12},{12,16},{16,20},{20,24},{24,28},{1,5},{5,9},{9,... | collective-permute-start | bytes 98312 | tf_op jit(solution)/shard_map/ppermute | solution.py:17
  113.9 7.0 %collective-permute-start.9 = (bf16[32,4,128]{2,1,0:T(4,128)(2,1)S(1)}, bf16[32,4,128]{2,1,0:T(4,128)(2,1)S(1)}, u32[]{:S(2)}, u32[]{:S(2)}) collective-permute-start(bf16[32,4,128]{2,1,0:T(4,128)(2,1)S(1)} %get-tuple-element.119), channel_id=1, source_target_pairs={{4,0},{8,4},{12,8},{16,12},{20,16},{24,20},{28,24},{5,1},{9,5},{13... | collective-permute-start | bytes 98312 | tf_op jit(solution)/shard_map/ppermute | solution.py:17
  166.9 6.1 %collective-permute-start.11 = (bf16[32,4,128]{2,1,0:T(4,128)(2,1)S(1)}, bf16[32,4,128]{2,1,0:T(4,128)(2,1)S(1)}, u32[]{:S(2)}, u32[]{:S(2)}) collective-permute-start(bf16[32,4,128]{2,1,0:T(4,128)(2,1)S(1)} %get-tuple-element.126), channel_id=1, source_target_pairs={{4,0},{8,4},{12,8},{16,12},{20,16},{24,20},{28,24},{5,1},{9,5},{13... | collective-permute-start | bytes 98312 | tf_op jit(solution)/shard_map/ppermute | solution.py:28
  168.2 6.4 %collective-permute-start.10 = (bf16[32,4,128]{2,1,0:T(4,128)(2,1)S(1)}, bf16[32,4,128]{2,1,0:T(4,128)(2,1)S(1)}, u32[]{:S(2)}, u32[]{:S(2)}) collective-permute-start(bf16[32,4,128]{2,1,0:T(4,128)(2,1)S(1)} %get-tuple-element.125), channel_id=1, source_target_pairs={{0,4},{4,8},{8,12},{12,16},{16,20},{20,24},{24,28},{1,5},{5,9},{9,... | collective-permute-start | bytes 98312 | tf_op jit(solution)/shard_map/ppermute | solution.py:27
  181.7 13.3 %copy-start.2 = (f32[32,16,128]{2,1,0:T(8,128)S(1)}, f32[32,16,128]{2,1,0:T(8,128)}, u32[]{:S(2)}) copy-start(f32[32,16,128]{2,1,0:T(8,128)} %get-tuple-element.111) | copy-start | bytes 786436
  182.3 59.2 %copy-start.1 = (f32[32,16,128]{2,1,0:T(8,128)S(1)}, f32[32,16,128]{2,1,0:T(8,128)}, u32[]{:S(2)}) copy-start(f32[32,16,128]{2,1,0:T(8,128)} %copy-done) | copy-start | bytes 786436
  182.3 59.2 %copy-start.3 = (f32[32,16,128]{2,1,0:T(8,128)S(1)}, f32[32,16,128]{2,1,0:T(8,128)}, u32[]{:S(2)}) copy-start(f32[32,16,128]{2,1,0:T(8,128)} %get-tuple-element.112) | copy-start | bytes 786436
  183.1 6.4 %collective-permute-start.12 = (bf16[32,4,128]{2,1,0:T(4,128)(2,1)S(1)}, bf16[32,4,128]{2,1,0:T(4,128)(2,1)S(1)}, u32[]{:S(2)}, u32[]{:S(2)}) collective-permute-start(bf16[32,4,128]{2,1,0:T(4,128)(2,1)S(1)} %get-tuple-element.118), channel_id=1, source_target_pairs={{0,4},{4,8},{8,12},{12,16},{16,20},{20,24},{24,28},{1,5},{5,9},{9,... | collective-permute-start | bytes 98312 | tf_op jit(solution)/shard_map/ppermute | solution.py:17
  187.9 7.0 %collective-permute-start.13 = (bf16[32,4,128]{2,1,0:T(4,128)(2,1)S(1)}, bf16[32,4,128]{2,1,0:T(4,128)(2,1)S(1)}, u32[]{:S(2)}, u32[]{:S(2)}) collective-permute-start(bf16[32,4,128]{2,1,0:T(4,128)(2,1)S(1)} %get-tuple-element.117), channel_id=1, source_target_pairs={{4,0},{8,4},{12,8},{16,12},{20,16},{24,20},{28,24},{5,1},{9,5},{13... | collective-permute-start | bytes 98312 | tf_op jit(solution)/shard_map/ppermute | solution.py:17
where the time goes:
time: 244 us; the launch traced here: 243 us
  blocking collectives  124 us (51%)
  starting transfers between devices  43.2 us (18%)
  matrix products  29.9 us (12%)
  waiting for transfers between devices  26 us (11%)
  between operations  11.3 us (5%)
  other arithmetic  7.49 us (3%)
    psum x3, blocking collectives, paired(): lax.psum((local_inner(vector, vector), local_inner(vector, applied)), ('t...  124 us
    ppermute x8, starting transfers between devices, from_behind(): return lax.ppermute(value, axis, pairs)  24.5 us
    dot_general x4, matrix products, adjoint_image(): jnp.einsum('cwgf,cgrsf->cwgrs', image16, kernels, preferred_element_type=...  22 us
    ppermute x8, waiting for transfers between devices, from_behind(): return lax.ppermute(value, axis, pairs)  21.5 us
    ppermute x3, starting transfers between devices, extended(): before = lax.ppermute(last, axis, up)  14.8 us
  transfers between devices with their start and end apart: 14, of which 11 were waited for; matrix products, arithmetic and copies ran while one was open for 0% of the time, Pallas kernels for 0%

commit v1 on v0

v1 whole, which is shorter than its diff:
```python
import functools

import jax
import jax.numpy as jnp
from jax import lax
from jax.experimental import pallas as pl
from jax.experimental.pallas import tpu as pltpu
from jax.sharding import PartitionSpec as P

HALO_BLOCKS = 4
BLOCKS_DEV = 16
EXTENT = BLOCKS_DEV + 2 * HALO_BLOCKS
RIM = 2 * HALO_BLOCKS
TIKHONOV = 0.5
UNROLL = 4
MOMENT_ROWS = 8
VMEM_LIMIT = 24 * 1024 * 1024


def split(value):
    upper = value.astype(jnp.bfloat16)
    lower = (value - upper.astype(jnp.float32)).astype(jnp.bfloat16)
    return upper, lower


def halves_sum(value):
    half = value.shape[0] // 2
    return value[:half] + value[half:]


def row_of(value):
    total = jnp.sum(value, axis=0, keepdims=True)
    return total if total.ndim == 2 else jnp.sum(total, axis=1)


def scatter(spread, index_ref, group, slots, partial_ref):
    lanes = partial_ref.shape[2]
    for slot in range(slots):
        block = index_ref[group * slots + slot]
        partial_ref[block] += spread[:, slot * lanes : (slot + 1) * lanes]


def emit_rims(place_ref, partial_ref, even_ref, odd_ref):
    width = even_ref.shape[0]
    top = EXTENT - width
    is_even = lax.rem(place_ref[0], 2) == 0
    even_ref[...] = partial_ref[pl.ds(jnp.where(is_even, top, 0), width)]
    odd_ref[...] = partial_ref[pl.ds(jnp.where(is_even, 0, top), width)]


def rhs_kernel(place_ref, index_ref, data_ref, kernels_ref, partial_ref, even_ref, odd_ref):
    groups, slots, spaxels, fibres = kernels_ref.shape
    partial_ref[...] = jnp.zeros_like(partial_ref)
    live = place_ref[1]

    def body(step, carry):
        for inner in range(UNROLL):
            group = step * UNROLL + inner
            weights = kernels_ref[group].reshape(slots * spaxels, fibres)
            data = data_ref[group]
            data = jnp.where(group < live, data, jnp.zeros_like(data))
            spread = lax.dot_general(
                data, weights, (((1,), (1,)), ((), ())), preferred_element_type=jnp.float32
            )
            scatter(spread, index_ref, group, slots, partial_ref)
        return carry

    lax.fori_loop(0, groups // UNROLL, body, 0)
    emit_rims(place_ref, partial_ref, even_ref, odd_ref)


def step_kernel(
    power,
    final,
    place_ref,
    index_ref,
    held_ref,
    even_in_ref,
    odd_in_ref,
    moments_in_ref,
    kernels_ref,
    vector_ref,
    partial_ref,
    even_ref,
    odd_ref,
    moments_ref,
    operand_ref,
):
    groups, slots, spaxels, fibres = kernels_ref.shape
    waves = held_ref.shape[1]
    live = place_ref[1]
    is_even = lax.rem(place_ref[0], 2) == 0
    top = EXTENT - RIM
    vector_ref[...] = held_ref[...]
    vector_ref[pl.ds(jnp.where(is_even, top, 0), RIM)] += even_in_ref[...]
    vector_ref[pl.ds(jnp.where(is_even, 0, top), RIM)] += odd_in_ref[...]
    square = jnp.zeros(vector_ref.shape[1:], jnp.float32)
    for block in range(EXTENT):
        value = vector_ref[block]
        operand_ref[block, :waves], operand_ref[block, waves:] = split(value)
        if HALO_BLOCKS <= block < HALO_BLOCKS + BLOCKS_DEV:
            square = square + value * value
    partial_ref[...] = jnp.zeros_like(partial_ref)

    def body(step, energy):
        for inner in range(UNROLL):
            group = step * UNROLL + inner
            weights = kernels_ref[group].reshape(slots * spaxels, fibres)
            picked = jnp.concatenate(
                [operand_ref[index_ref[group * slots + slot]] for slot in range(slots)], axis=1
            )
            image = halves_sum(jnp.dot(picked, weights, preferred_element_type=jnp.float32))
            image = jnp.where(group < live, image, 0.0)
            energy = energy + image * image
            spread = lax.dot_general(
                jnp.concatenate(split(image), axis=0),
                weights,
                (((1,), (1,)), ((), ())),
                preferred_element_type=jnp.float32,
            )
            scatter(halves_sum(spread), index_ref, group, slots, partial_ref)
        return energy

    energy = lax.fori_loop(
        0, groups // UNROLL, body, jnp.zeros((waves, fibres), jnp.float32)
    )
    emit_rims(place_ref, partial_ref, even_ref, odd_ref)
    for block in range(EXTENT):
        partial_ref[block] += TIKHONOV * vector_ref[block]
    square_row = jnp.sum(square, axis=0, keepdims=True)
    energy_row = jnp.sum(energy, axis=0, keepdims=True) + TIKHONOV * square_row
    rows = lax.broadcasted_iota(jnp.int32, moments_in_ref.shape, 0)
    moments = jnp.where(
        rows == 2 * power,
        square_row,
        jnp.where(rows == 2 * power + 1, energy_row, moments_in_ref[...]),
    )
    moments_ref[...] = jnp.broadcast_to(moments, moments_ref.shape) if final else moments


def coefficients(moments, steps):
    def inner(first, second, shift):
        total = 0.0
        for i, a in enumerate(first):
            for j, b in enumerate(second):
                if a is not None and b is not None:
                    total = total + a * b * moments[i + j + shift]
        return total

    one = jnp.ones_like(moments[0])
    residual, direction = [one], [one]
    answer = []
    current = inner(residual, residual, 0)
    for step in range(steps):
        size = current / inner(direction, direction, 1)
        answer = [
            size * d + (answer[i] if i < len(answer) else 0.0) for i, d in enumerate(direction)
        ]
        shifted = [0.0] + [-size * d for d in direction]
        residual = [
            s + (residual[i] if i < len(residual) else 0.0) for i, s in enumerate(shifted)
        ]
        if step + 1 < steps:
            following = inner(residual, residual, 0)
            ratio = following / current
            direction = [
                r + (ratio * direction[i] if i < len(direction) else 0.0)
                for i, r in enumerate(residual)
            ]
            current = following
    return answer, residual


def final_kernel(
    place_ref,
    moments_ref,
    first_ref,
    second_ref,
    third_ref,
    held_ref,
    even_in_ref,
    odd_in_ref,
    solution_ref,
    residual_ref,
    last_ref,
):
    sums = moments_ref[0]
    for source in range(1, moments_ref.shape[0]):
        sums = sums + moments_ref[source]
    sums = jnp.sum(sums, axis=1, keepdims=True)
    lanes = first_ref.shape[2]
    raw = [jnp.broadcast_to(sums[row : row + 1], (1, lanes)) for row in range(6)]
    unit = raw[0] / raw[1]
    scaled, factor = [], 1.0 / raw[0]
    for row in range(6):
        scaled.append(raw[row] * factor)
        factor = factor * unit
    answer, residual = coefficients(scaled, 3)
    power = jnp.ones_like(unit)
    answer_scaled, residual_scaled = [], []
    for row in range(4):
        residual_scaled.append(residual[row] * power)
        power = power * unit
        if row < 3:
            answer_scaled.append(answer[row] * power)
    is_even = lax.rem(place_ref[0], 2) == 0
    last_ref[...] = held_ref[pl.ds(HALO_BLOCKS, BLOCKS_DEV)]
    low, high = 0, BLOCKS_DEV - HALO_BLOCKS
    last_ref[pl.ds(jnp.where(is_even, high, low), HALO_BLOCKS)] += even_in_ref[...]
    last_ref[pl.ds(jnp.where(is_even, low, high), HALO_BLOCKS)] += odd_in_ref[...]
    for block in range(BLOCKS_DEV):
        first = first_ref[HALO_BLOCKS + block]
        second = second_ref[HALO_BLOCKS + block]
        third = third_ref[HALO_BLOCKS + block]
        last = last_ref[block]
        solution_ref[:, block, :] = (
            answer_scaled[0] * first + answer_scaled[1] * second + answer_scaled[2] * third
        )
        residual_ref[:, block, :] = (
            first
            + residual_scaled[1] * second
            + residual_scaled[2] * third
            + residual_scaled[3] * last
        )


def vmem(count):
    return [pl.BlockSpec(memory_space=pltpu.VMEM)] * count


def smem(count):
    return [pl.BlockSpec(memory_space=pltpu.SMEM)] * count


def shards(fibre_data, kernels, block_index, live_count):
    tiles, devices = lax.axis_size("tile"), lax.axis_size("tile") * lax.axis_size("wave")
    _, groups, slots, spaxels, fibres = kernels.shape
    waves = fibre_data.shape[0]
    tile = lax.axis_index("tile")
    first_block = tile * BLOCKS_DEV - HALO_BLOCKS
    index = (block_index - first_block).reshape(groups * slots)
    place = jnp.stack([tile, live_count[0]])
    weights = kernels.reshape(groups, slots, spaxels, fibres)
    data = jnp.swapaxes(fibre_data, 0, 1)
    window = jax.ShapeDtypeStruct((EXTENT, waves, spaxels), jnp.float32)
    rim = jax.ShapeDtypeStruct((RIM, waves, spaxels), jnp.float32)
    half_rim = jax.ShapeDtypeStruct((HALO_BLOCKS, waves, spaxels), jnp.float32)
    moment = jax.ShapeDtypeStruct((MOMENT_ROWS, spaxels), jnp.float32)
    moment_all = jax.ShapeDtypeStruct((devices, MOMENT_ROWS, spaxels), jnp.float32)
    params = pltpu.CompilerParams(vmem_limit_bytes=VMEM_LIMIT)
    even_pairs = [(i, i ^ 1) for i in range(tiles) if (i ^ 1) < tiles]
    odd_pairs = [
        (i, j) for i in range(tiles) for j in [((i + 1) ^ 1) - 1] if 0 <= j < tiles
    ]

    def swap(even, odd):
        return lax.ppermute(even, "tile", even_pairs), lax.ppermute(odd, "tile", odd_pairs)

    held, even, odd = pl.pallas_call(
        rhs_kernel,
        out_shape=(window, rim, rim),
        in_specs=smem(2) + vmem(2),
        out_specs=tuple(vmem(3)),
        compiler_params=params,
        name="rhs",
    )(place, index, data, weights)
    moments = jnp.zeros(moment.shape, jnp.float32)
    vectors = []
    for power in range(3):
        final = power == 2
        even, odd = swap(even, odd)
        out_rim = half_rim if final else rim
        vector, held, even, odd, moments = pl.pallas_call(
            functools.partial(step_kernel, power, final),
            out_shape=(window, window, out_rim, out_rim, moment_all if final else moment),
            in_specs=smem(2) + vmem(5),
            out_specs=tuple(vmem(5)),
            scratch_shapes=[pltpu.VMEM((EXTENT, 2 * waves, spaxels), jnp.bfloat16)],
            compiler_params=params,
            name=f"step{power}",
        )(place, index, held, even, odd, moments, weights)
        vectors.append(vector)
    even, odd = swap(even, odd)
    moments = lax.all_to_all(moments, ("tile", "wave"), 0, 0)
    out = jax.ShapeDtypeStruct((waves, BLOCKS_DEV, spaxels), jnp.float32)
    return pl.pallas_call(
        final_kernel,
        out_shape=(out, out),
        in_specs=smem(1) + vmem(7),
        out_specs=tuple(vmem(2)),
        scratch_shapes=[pltpu.VMEM((BLOCKS_DEV, waves, spaxels), jnp.float32)],
        compiler_params=params,
        name="combine",
    )(place, moments, *vectors, held, even, odd)


def solution(mesh):
    in_specs = (
        P("wave", "tile", None),
        P("wave", "tile", None, None, None),
        P("wave", "tile", None),
        P("tile"),
    )
    out_specs = (P("wave", "tile", None), P("wave", "tile", None))
    return jax.shard_map(shards, mesh=mesh, in_specs=in_specs, out_specs=out_specs, check_vma=False)
```

time: 244 us -> 72.7 us (0.30)
  blocking collectives: 124 us -> 0 us
  matrix products: 29.9 us -> 0 us
  Pallas kernels: 0 us -> 26.3 us
  starting transfers between devices: 43.2 us -> 25.4 us
  waiting for transfers between devices: 26 us -> 15 us
  between operations: 11.3 us -> 1.36 us
  other arithmetic: 7.49 us -> 0.76 us
  local copies, waits for them, and re-layouts: 0.74 us -> 3.44 us
    psum x3 -> x0, blocking collectives: 124 us -> none  [paired(): lax.psum((local_inner(vector, vector), local_inner(vector, applied)), ('t...]
    dot_general x15 -> x0, matrix products: 29.9 us -> none  [the longest x4 22 us: adjoint_image(): jnp.einsum('cwgf,cgrsf->cwgrs', image16, kernels, preferred_element_type=...]
    ppermute x14 -> x8, starting transfers between devices: 43.2 us -> 16.3 us  [the longest x4 13.7 us: swap(): lax.ppermute(even, 'tile', even_pairs)]
    pallas_call x0 -> x5, Pallas kernels: none -> 26.3 us  [the longest x3 21.5 us: shards(): pl.pallas_call(functools.partial(step_kernel, power, final), out_shape=(w...]
    ppermute x14 -> x8, waiting for transfers between devices: 26 us -> 11.9 us  [the longest x4 11.9 us: swap(): lax.ppermute(even, 'tile', even_pairs)]
    all_to_all x0 -> x1, starting transfers between devices: none -> 9.09 us  [shards(): moments = lax.all_to_all(moments, ('tile', 'wave'), 0, 0)]
    all_to_all x0 -> x1, waiting for transfers between devices: none -> 3.13 us  [shards(): moments = lax.all_to_all(moments, ('tile', 'wave'), 0, 0)]
    unnamed x10 -> x5, local copies, waits for them, and re-layouts: 0.43 us -> 3.25 us
  transfers between devices with their start and end apart: 14 -> 9, of which waited for: 11 -> 5; matrix products, arithmetic and copies ran while one was open for 0% -> 0% of each run, Pallas kernels for 0% -> 0%
where the time goes in v1:
time: 72.7 us; the launch traced here: 72.3 us
  Pallas kernels  26.3 us (36%)
  starting transfers between devices  25.4 us (35%)
  waiting for transfers between devices  15 us (21%)
  local copies, waits for them, and re-layouts  3.44 us (5%)
  between operations  1.36 us (2%)
  other arithmetic  0.76 us (1%)
    pallas_call x3, Pallas kernels, shards(): pl.pallas_call(functools.partial(step_kernel, power, final), out_shape=(w...  21.5 us
    ppermute x4, starting transfers between devices, swap(): lax.ppermute(even, 'tile', even_pairs)  13.7 us
    ppermute x4, waiting for transfers between devices, swap(): lax.ppermute(even, 'tile', even_pairs)  11.9 us
    all_to_all x1, starting transfers between devices, shards(): moments = lax.all_to_all(moments, ('tile', 'wave'), 0, 0)  9.09 us
    unnamed x5, local copies, waits for them, and re-layouts  3.25 us
    all_to_all x1, waiting for transfers between devices, shards(): moments = lax.all_to_all(moments, ('tile', 'wave'), 0, 0)  3.13 us
    pallas_call x1, Pallas kernels, shards(): pl.pallas_call(rhs_kernel, out_shape=(window, rim, rim), in_specs=smem(2)...  2.9 us
    ppermute x4, starting transfers between devices, swap(): lax.ppermute(odd, 'tile', odd_pairs)  2.62 us
  transfers between devices with their start and end apart: 9, of which 5 were waited for; matrix products, arithmetic and copies ran while one was open for 0% of the time, Pallas kernels for 0%

profile of v1, /device:TPU:0, one launch (start us, length us, event | category | flops | bytes accessed | tf_op | source)
XLA Modules:
  0.0 72.3 jit_solution(793382472076231049)
XLA Ops:
  1.3 0.7 broadcast_subtract_fusion
  2.0 0.1 copy.8
  2.1 0.1 reshape.10.index_ref
  2.2 1.1 %copy.11 = bf16[32,32,128]{2,0,1:T(8,128)(2,1)S(1)} copy(bf16[32,32,128]{2,1,0:T(8,128)(2,1)} %param.4) | data formatting | bytes 524288 | tf_op args[0]
  3.2 0.1 pad_add_fusion.place_ref
  3.3 0.0 copy-start
  3.3 2.2 %copy-done = bf16[1,32,4,128,128]{4,3,2,1,0:T(8,128)(2,1)S(1)} copy-done((bf16[1,32,4,128,128]{4,3,2,1,0:T(8,128)(2,1)S(1)}, bf16[1,32,4,128,128]{4,3,2,1,0:T(8,128)(2,1)}, u32[]{:S(2)}) %copy-start) | copy-done | bytes 4194328
  5.5 0.0 copy-start.1
  5.5 2.9 %rhs.1 = (f32[24,32,128]{2,1,0:T(8,128)S(1)}, f32[8,32,128]{2,1,0:T(8,128)S(1)}, f32[8,32,128]{2,1,0:T(8,128)S(1)}) custom-call(s32[2]{0:T(128)S(1)} %pad_add_fusion.place_ref, s32[128]{0:T(128)S(1)} %reshape.10.index_ref, bf16[32,32,128]{2,1,0:T(8,128)(2,1)S(1)} %bitcast.9, bf16[32,4,128,128]{3,2,1,0:T(8,128)(2,1)S(1)} %bitcast.5), custom_call_target="tpu_custom_call" | custom-call | tf_op jit(solution)/shard_map/rhs/pallas_call | solution.py:259
  8.4 3.0 %collective-permute-start = (f32[8,32,128]{2,1,0:T(8,128)S(1)}, f32[8,32,128]{2,1,0:T(8,128)S(1)}, u32[]{:S(2)}, u32[]{:S(2)}) collective-permute-start(f32[8,32,128]{2,1,0:T(8,128)S(1)} %get-tuple-element.21), channel_id=1, source_target_pairs={{0,4},{4,0},{8,12},{12,8},{16,20},{20,16},{24,28},{28,24},{1,5},{5... | collective-permute-start | bytes 393224 | tf_op jit(solution)/shard_map/ppermute | solution.py:257
  11.4 0.7 collective-permute-start.1
  12.1 2.8 %collective-permute-done.even_in_ref = f32[8,32,128]{2,1,0:T(8,128)S(1)} collective-permute-done((f32[8,32,128]{2,1,0:T(8,128)S(1)}, f32[8,32,128]{2,1,0:T(8,128)S(1)}, u32[]{:S(2)}, u32[]{:S(2)}) %collective-permute-start) | collective-permute-done | bytes 131104 | tf_op jit(solution)/shard_map/ppermute | solution.py:257
  14.9 0.0 collective-permute-done.1.odd_in_ref
  14.9 0.0 copy-done.1
  14.9 6.9 %step0.1 = (f32[24,32,128]{2,1,0:T(8,128)S(1)}, f32[24,32,128]{2,1,0:T(8,128)S(1)}, f32[8,32,128]{2,1,0:T(8,128)S(1)}, f32[8,32,128]{2,1,0:T(8,128)S(1)}, f32[8,128]{1,0:T(8,128)S(1)}) custom-call(s32[2]{0:T(128)S(1)} %pad_add_fusion.place_ref, s32[128]{0:T(128)S(1)} %reshape.10.index_ref, f32[24,32,128]{2,1,0:T(8,128)S(1)} %get-tuple-element.20.held_ref, ...), custom_call_target="tpu_custom_call" | custom-call | tf_op jit(solution)/shard_map/step0/pallas_call | solution.py:273
  21.9 4.7 %collective-permute-start.2 = (f32[8,32,128]{2,1,0:T(8,128)S(1)}, f32[8,32,128]{2,1,0:T(8,128)S(1)}, u32[]{:S(2)}, u32[]{:S(2)}) collective-permute-start(f32[8,32,128]{2,1,0:T(8,128)S(1)} %get-tuple-element.24), channel_id=1, source_target_pairs={{0,4},{4,0},{8,12},{12,8},{16,20},{20,16},{24,28},{28,24},{1,5},{5... | collective-permute-start | bytes 393224 | tf_op jit(solution)/shard_map/ppermute | solution.py:257
  26.6 0.7 collective-permute-start.3
  27.3 3.3 %collective-permute-done.2.even_in_ref = f32[8,32,128]{2,1,0:T(8,128)S(1)} collective-permute-done((f32[8,32,128]{2,1,0:T(8,128)S(1)}, f32[8,32,128]{2,1,0:T(8,128)S(1)}, u32[]{:S(2)}, u32[]{:S(2)}) %collective-permute-start.2) | collective-permute-done | bytes 131104 | tf_op jit(solution)/shard_map/ppermute | solution.py:257
  30.5 0.0 collective-permute-done.3.odd_in_ref
  30.5 6.9 %step1.1 = (f32[24,32,128]{2,1,0:T(8,128)S(1)}, f32[24,32,128]{2,1,0:T(8,128)S(1)}, f32[8,32,128]{2,1,0:T(8,128)S(1)}, f32[8,32,128]{2,1,0:T(8,128)S(1)}, f32[8,128]{1,0:T(8,128)S(1)}) custom-call(s32[2]{0:T(128)S(1)} %pad_add_fusion.place_ref, s32[128]{0:T(128)S(1)} %reshape.10.index_ref, f32[24,32,128]{2,1,0:T(8,128)S(1)} %get-tuple-element.23.held_ref, ...), custom_call_target="tpu_custom_call" | custom-call | tf_op jit(solution)/shard_map/step1/pallas_call | solution.py:273
  37.5 4.1 %collective-permute-start.4 = (f32[8,32,128]{2,1,0:T(8,128)S(1)}, f32[8,32,128]{2,1,0:T(8,128)S(1)}, u32[]{:S(2)}, u32[]{:S(2)}) collective-permute-start(f32[8,32,128]{2,1,0:T(8,128)S(1)} %get-tuple-element.28), channel_id=1, source_target_pairs={{0,4},{4,0},{8,12},{12,8},{16,20},{20,16},{24,28},{28,24},{1,5},{5... | collective-permute-start | bytes 393224 | tf_op jit(solution)/shard_map/ppermute | solution.py:257
  41.6 0.7 collective-permute-start.5
  42.3 3.2 %collective-permute-done.4.even_in_ref = f32[8,32,128]{2,1,0:T(8,128)S(1)} collective-permute-done((f32[8,32,128]{2,1,0:T(8,128)S(1)}, f32[8,32,128]{2,1,0:T(8,128)S(1)}, u32[]{:S(2)}, u32[]{:S(2)}) %collective-permute-start.4) | collective-permute-done | bytes 131104 | tf_op jit(solution)/shard_map/ppermute | solution.py:257
  45.5 0.0 collective-permute-done.5.odd_in_ref
  45.5 7.6 %step2.1 = (f32[24,32,128]{2,1,0:T(8,128)S(1)}, f32[24,32,128]{2,1,0:T(8,128)S(1)}, f32[4,32,128]{2,1,0:T(8,128)S(1)}, f32[4,32,128]{2,1,0:T(8,128)S(1)}, f32[32,8,128]{2,1,0:T(8,128)}) custom-call(s32[2]{0:T(128)S(1)} %pad_add_fusion.place_ref, s32[128]{0:T(128)S(1)} %reshape.10.index_ref, f32[24,32,128]{2,1,0:T(8,128)S(1)} %get-tuple-element.27.held_ref, ...), custom_call_target="tpu_custom_call" | custom-call | tf_op jit(solution)/shard_map/step2/pallas_call | solution.py:273
  53.1 9.1 %all-to-all-start = ((f32[32,8,128]{2,1,0:T(8,128)}), f32[32,8,128]{2,1,0:T(8,128)S(1)}, u32[]{:S(2)}, u32[]{:S(2)}) async-start(f32[32,8,128]{2,1,0:T(8,128)} %get-tuple-element.31), calls=%async_computation | async-start | bytes 262144 | tf_op jit(solution)/shard_map/all_to_all | solution.py:284
  62.2 1.8 %collective-permute-start.6 = (f32[4,32,128]{2,1,0:T(8,128)S(1)}, f32[4,32,128]{2,1,0:T(8,128)S(1)}, u32[]{:S(2)}, u32[]{:S(2)}) collective-permute-start(f32[4,32,128]{2,1,0:T(8,128)S(1)} %get-tuple-element.36), channel_id=1, source_target_pairs={{0,4},{4,0},{8,12},{12,8},{16,20},{20,16},{24,28},{28,24},{1,5},{5... | collective-permute-start | bytes 196616 | tf_op jit(solution)/shard_map/ppermute | solution.py:257
  64.0 0.7 collective-permute-start.7
  64.7 2.6 %collective-permute-done.6.even_in_ref = f32[4,32,128]{2,1,0:T(8,128)S(1)} collective-permute-done((f32[4,32,128]{2,1,0:T(8,128)S(1)}, f32[4,32,128]{2,1,0:T(8,128)S(1)}, u32[]{:S(2)}, u32[]{:S(2)}) %collective-permute-start.6) | collective-permute-done | bytes 65568 | tf_op jit(solution)/shard_map/ppermute | solution.py:257
  67.3 0.0 collective-permute-done.7.odd_in_ref
  67.3 3.1 %all-to-all-done.moments_ref = f32[32,8,128]{2,1,0:T(8,128)S(1)} async-done(((f32[32,8,128]{2,1,0:T(8,128)}), f32[32,8,128]{2,1,0:T(8,128)S(1)}, u32[]{:S(2)}, u32[]{:S(2)}) %all-to-all-start) | async-done | bytes 131104 | tf_op jit(solution)/shard_map/all_to_all | solution.py:284
  70.4 1.9 %combine.1 = (f32[32,16,128]{2,1,0:T(8,128)}, f32[32,16,128]{2,1,0:T(8,128)}) custom-call(s32[2]{0:T(128)S(1)} %pad_add_fusion.place_ref, f32[32,8,128]{2,1,0:T(8,128)S(1)} %all-to-all-done.moments_ref, f32[24,32,128]{2,1,0:T(8,128)S(1)} %get-tuple-element.32.first_ref, f32[24,32,128]{2,1,0:T(8,128)S(1)} %get-tuple-element.33.second_ref, ...), custom_call_target="tpu_custom_call" | custom-call | tf_op jit(solution)/shard_map/combine/pallas_call | solution.py:286
  (1 shorter events, 0.0 us)
Async XLA Ops:
  3.3 2.2 %copy-start = (bf16[1,32,4,128,128]{4,3,2,1,0:T(8,128)(2,1)S(1)}, bf16[1,32,4,128,128]{4,3,2,1,0:T(8,128)(2,1)}, u32[]{:S(2)}) copy-start(bf16[1,32,4,128,128]{4,3,2,1,0:T(8,128)(2,1)} %param.5) | copy-start | bytes 12582916
  5.5 9.5 %copy-start.1 = (bf16[1,32,4,128,128]{4,3,2,1,0:T(8,128)(2,1)S(1)}, bf16[1,32,4,128,128]{4,3,2,1,0:T(8,128)(2,1)}, u32[]{:S(2)}) copy-start(bf16[1,32,4,128,128]{4,3,2,1,0:T(8,128)(2,1)} %param.5) | copy-start | bytes 12582916
  8.4 6.5 %collective-permute-start = (f32[8,32,128]{2,1,0:T(8,128)S(1)}, f32[8,32,128]{2,1,0:T(8,128)S(1)}, u32[]{:S(2)}, u32[]{:S(2)}) collective-permute-start(f32[8,32,128]{2,1,0:T(8,128)S(1)} %get-tuple-element.21), channel_id=1, source_target_pairs={{0,4},{4,0},{8,12},{12,8},{16,20},{20,16},{24,28},{28,24},{1,5},{5... | collective-permute-start | bytes 393224 | tf_op jit(solution)/shard_map/ppermute | solution.py:257
  11.4 3.5 %collective-permute-start.1 = (f32[8,32,128]{2,1,0:T(8,128)S(1)}, f32[8,32,128]{2,1,0:T(8,128)S(1)}, u32[]{:S(2)}, u32[]{:S(2)}) collective-permute-start(f32[8,32,128]{2,1,0:T(8,128)S(1)} %get-tuple-element.22), channel_id=1, source_target_pairs={{4,8},{8,4},{12,16},{16,12},{20,24},{24,20},{5,9},{9,5},{13,17},{1... | collective-permute-start | bytes 393224 | tf_op jit(solution)/shard_map/ppermute | solution.py:257
  21.9 8.6 %collective-permute-start.2 = (f32[8,32,128]{2,1,0:T(8,128)S(1)}, f32[8,32,128]{2,1,0:T(8,128)S(1)}, u32[]{:S(2)}, u32[]{:S(2)}) collective-permute-start(f32[8,32,128]{2,1,0:T(8,128)S(1)} %get-tuple-element.24), channel_id=1, source_target_pairs={{0,4},{4,0},{8,12},{12,8},{16,20},{20,16},{24,28},{28,24},{1,5},{5... | collective-permute-start | bytes 393224 | tf_op jit(solution)/shard_map/ppermute | solution.py:257
  26.6 3.9 %collective-permute-start.3 = (f32[8,32,128]{2,1,0:T(8,128)S(1)}, f32[8,32,128]{2,1,0:T(8,128)S(1)}, u32[]{:S(2)}, u32[]{:S(2)}) collective-permute-start(f32[8,32,128]{2,1,0:T(8,128)S(1)} %get-tuple-element.25), channel_id=1, source_target_pairs={{4,8},{8,4},{12,16},{16,12},{20,24},{24,20},{5,9},{9,5},{13,17},{1... | collective-permute-start | bytes 393224 | tf_op jit(solution)/shard_map/ppermute | solution.py:257
  37.5 8.0 %collective-permute-start.4 = (f32[8,32,128]{2,1,0:T(8,128)S(1)}, f32[8,32,128]{2,1,0:T(8,128)S(1)}, u32[]{:S(2)}, u32[]{:S(2)}) collective-permute-start(f32[8,32,128]{2,1,0:T(8,128)S(1)} %get-tuple-element.28), channel_id=1, source_target_pairs={{0,4},{4,0},{8,12},{12,8},{16,20},{20,16},{24,28},{28,24},{1,5},{5... | collective-permute-start | bytes 393224 | tf_op jit(solution)/shard_map/ppermute | solution.py:257
  41.6 3.9 %collective-permute-start.5 = (f32[8,32,128]{2,1,0:T(8,128)S(1)}, f32[8,32,128]{2,1,0:T(8,128)S(1)}, u32[]{:S(2)}, u32[]{:S(2)}) collective-permute-start(f32[8,32,128]{2,1,0:T(8,128)S(1)} %get-tuple-element.29), channel_id=1, source_target_pairs={{4,8},{8,4},{12,16},{16,12},{20,24},{24,20},{5,9},{9,5},{13,17},{1... | collective-permute-start | bytes 393224 | tf_op jit(solution)/shard_map/ppermute | solution.py:257
  53.1 17.3 %all-to-all-start = ((f32[32,8,128]{2,1,0:T(8,128)}), f32[32,8,128]{2,1,0:T(8,128)S(1)}, u32[]{:S(2)}, u32[]{:S(2)}) async-start(f32[32,8,128]{2,1,0:T(8,128)} %get-tuple-element.31), calls=%async_computation | async-start | bytes 262144 | tf_op jit(solution)/shard_map/all_to_all | solution.py:284
  62.2 5.1 %collective-permute-start.6 = (f32[4,32,128]{2,1,0:T(8,128)S(1)}, f32[4,32,128]{2,1,0:T(8,128)S(1)}, u32[]{:S(2)}, u32[]{:S(2)}) collective-permute-start(f32[4,32,128]{2,1,0:T(8,128)S(1)} %get-tuple-element.36), channel_id=1, source_target_pairs={{0,4},{4,0},{8,12},{12,8},{16,20},{20,16},{24,28},{28,24},{1,5},{5... | collective-permute-start | bytes 196616 | tf_op jit(solution)/shard_map/ppermute | solution.py:257
  64.0 3.2 %collective-permute-start.7 = (f32[4,32,128]{2,1,0:T(8,128)S(1)}, f32[4,32,128]{2,1,0:T(8,128)S(1)}, u32[]{:S(2)}, u32[]{:S(2)}) collective-permute-start(f32[4,32,128]{2,1,0:T(8,128)S(1)} %get-tuple-element.37), channel_id=1, source_target_pairs={{4,8},{8,4},{12,16},{16,12},{20,24},{24,20},{5,9},{9,5},{13,17},{1... | collective-permute-start | bytes 196616 | tf_op jit(solution)/shard_map/ppermute | solution.py:257

commit v2 on v1

--- a/solution.py
+++ b/solution.py
@@ -12,7 +12,7 @@
 EXTENT = BLOCKS_DEV + 2 * HALO_BLOCKS
 RIM = 2 * HALO_BLOCKS
 TIKHONOV = 0.5
-UNROLL = 4
+CHUNKS = 8
 MOMENT_ROWS = 8
 VMEM_LIMIT = 24 * 1024 * 1024
 
@@ -28,16 +28,18 @@
     return value[:half] + value[half:]
 
 
-def row_of(value):
-    total = jnp.sum(value, axis=0, keepdims=True)
-    return total if total.ndim == 2 else jnp.sum(total, axis=1)
-
-
-def scatter(spread, index_ref, group, slots, partial_ref):
+def scatter(spread, place_ref, index_ref, group, partial_ref):
     lanes = partial_ref.shape[2]
-    for slot in range(slots):
-        block = index_ref[group * slots + slot]
+    first = place_ref[0] * BLOCKS_DEV - HALO_BLOCKS
+    for slot in range(index_ref.shape[1]):
+        block = index_ref[group, slot] - first
         partial_ref[block] += spread[:, slot * lanes : (slot + 1) * lanes]
+
+
+def spread_of(image, weights):
+    return lax.dot_general(
+        image, weights, (((1,), (1,)), ((), ())), preferred_element_type=jnp.float32
+    )
 
 
 def emit_rims(place_ref, partial_ref, even_ref, odd_ref):
@@ -48,24 +50,43 @@
     odd_ref[...] = partial_ref[pl.ds(jnp.where(is_even, 0, top), width)]
 
 
-def rhs_kernel(place_ref, index_ref, data_ref, kernels_ref, partial_ref, even_ref, odd_ref):
+def rhs_kernel(
+    place_ref,
+    live_ref,
+    index_ref,
+    data_ref,
+    source_ref,
+    kernels_ref,
+    partial_ref,
+    even_ref,
+    odd_ref,
+    narrow_ref,
+    wide_ref,
+    sems,
+    data_sem,
+):
     groups, slots, spaxels, fibres = kernels_ref.shape
+    chunks = sems.shape[0]
+    size = groups // chunks
+
+    def copy(chunk):
+        part = pl.ds(chunk * size, size)
+        return pltpu.make_async_copy(source_ref.at[part], kernels_ref.at[part], sems.at[chunk])
+
+    data_copy = pltpu.make_async_copy(data_ref, narrow_ref, data_sem)
+    data_copy.start()
+    for chunk in range(chunks):
+        copy(chunk).start()
     partial_ref[...] = jnp.zeros_like(partial_ref)
-    live = place_ref[1]
-
-    def body(step, carry):
-        for inner in range(UNROLL):
-            group = step * UNROLL + inner
-            weights = kernels_ref[group].reshape(slots * spaxels, fibres)
-            data = data_ref[group]
-            data = jnp.where(group < live, data, jnp.zeros_like(data))
-            spread = lax.dot_general(
-                data, weights, (((1,), (1,)), ((), ())), preferred_element_type=jnp.float32
-            )
-            scatter(spread, index_ref, group, slots, partial_ref)
-        return carry
-
-    lax.fori_loop(0, groups // UNROLL, body, 0)
+    data_copy.wait()
+    wide_ref[...] = narrow_ref[...].astype(jnp.float32)
+    live = live_ref[0]
+    for chunk in range(chunks):
+        copy(chunk).wait()
+        for group in range(chunk * size, (chunk + 1) * size):
+            data = jnp.where(group < live, wide_ref[:, group, :], 0.0).astype(jnp.bfloat16)
+            spread = spread_of(data, kernels_ref[group].reshape(slots * spaxels, fibres))
+            scatter(spread, place_ref, index_ref, group, partial_ref)
     emit_rims(place_ref, partial_ref, even_ref, odd_ref)
 
 
@@ -73,6 +94,7 @@
     power,
     final,
     place_ref,
+    live_ref,
     index_ref,
     held_ref,
     even_in_ref,
@@ -85,11 +107,13 @@
     odd_ref,
     moments_ref,
     operand_ref,
+    image_ref,
 ):
     groups, slots, spaxels, fibres = kernels_ref.shape
     waves = held_ref.shape[1]
-    live = place_ref[1]
+    live = live_ref[0]
     is_even = lax.rem(place_ref[0], 2) == 0
+    first_block = place_ref[0] * BLOCKS_DEV - HALO_BLOCKS
     top = EXTENT - RIM
     vector_ref[...] = held_ref[...]
     vector_ref[pl.ds(jnp.where(is_even, top, 0), RIM)] += even_in_ref[...]
@@ -101,29 +125,20 @@
         if HALO_BLOCKS <= block < HALO_BLOCKS + BLOCKS_DEV:
             square = square + value * value
     partial_ref[...] = jnp.zeros_like(partial_ref)
-
-    def body(step, energy):
-        for inner in range(UNROLL):
-            group = step * UNROLL + inner
-            weights = kernels_ref[group].reshape(slots * spaxels, fibres)
-            picked = jnp.concatenate(
-                [operand_ref[index_ref[group * slots + slot]] for slot in range(slots)], axis=1
-            )
-            image = halves_sum(jnp.dot(picked, weights, preferred_element_type=jnp.float32))
-            image = jnp.where(group < live, image, 0.0)
-            energy = energy + image * image
-            spread = lax.dot_general(
-                jnp.concatenate(split(image), axis=0),
-                weights,
-                (((1,), (1,)), ((), ())),
-                preferred_element_type=jnp.float32,
-            )
-            scatter(halves_sum(spread), index_ref, group, slots, partial_ref)
-        return energy
-
-    energy = lax.fori_loop(
-        0, groups // UNROLL, body, jnp.zeros((waves, fibres), jnp.float32)
-    )
+    energy = jnp.zeros((waves, fibres), jnp.float32)
+    for group in range(groups):
+        picked = jnp.concatenate(
+            [operand_ref[index_ref[group, slot] - first_block] for slot in range(slots)], axis=1
+        )
+        weights = kernels_ref[group].reshape(slots * spaxels, fibres)
+        image = halves_sum(jnp.dot(picked, weights, preferred_element_type=jnp.float32))
+        image = jnp.where(group < live, image, 0.0)
+        energy = energy + image * image
+        image_ref[group, :waves], image_ref[group, waves:] = split(image)
+    for group in range(groups):
+        weights = kernels_ref[group].reshape(slots * spaxels, fibres)
+        spread = halves_sum(spread_of(image_ref[group], weights))
+        scatter(spread, place_ref, index_ref, group, partial_ref)
     emit_rims(place_ref, partial_ref, even_ref, odd_ref)
     for block in range(EXTENT):
         partial_ref[block] += TIKHONOV * vector_ref[block]
@@ -236,12 +251,9 @@
     tiles, devices = lax.axis_size("tile"), lax.axis_size("tile") * lax.axis_size("wave")
     _, groups, slots, spaxels, fibres = kernels.shape
     waves = fibre_data.shape[0]
-    tile = lax.axis_index("tile")
-    first_block = tile * BLOCKS_DEV - HALO_BLOCKS
-    index = (block_index - first_block).reshape(groups * slots)
-    place = jnp.stack([tile, live_count[0]])
+    place = lax.axis_index("tile").reshape(1)
+    index = block_index.reshape(groups, slots)
     weights = kernels.reshape(groups, slots, spaxels, fibres)
-    data = jnp.swapaxes(fibre_data, 0, 1)
     window = jax.ShapeDtypeStruct((EXTENT, waves, spaxels), jnp.float32)
     rim = jax.ShapeDtypeStruct((RIM, waves, spaxels), jnp.float32)
     half_rim = jax.ShapeDtypeStruct((HALO_BLOCKS, waves, spaxels), jnp.float32)
@@ -256,14 +268,21 @@
     def swap(even, odd):
         return lax.ppermute(even, "tile", even_pairs), lax.ppermute(odd, "tile", odd_pairs)
 
-    held, even, odd = pl.pallas_call(
+    chunks = CHUNKS if groups % CHUNKS == 0 else 1
+    weights, held, even, odd = pl.pallas_call(
         rhs_kernel,
-        out_shape=(window, rim, rim),
-        in_specs=smem(2) + vmem(2),
-        out_specs=tuple(vmem(3)),
+        out_shape=(jax.ShapeDtypeStruct(weights.shape, weights.dtype), window, rim, rim),
+        in_specs=smem(3) + [pl.BlockSpec(memory_space=pltpu.HBM)] * 2,
+        out_specs=tuple(vmem(4)),
+        scratch_shapes=[
+            pltpu.VMEM(fibre_data.shape, fibre_data.dtype),
+            pltpu.VMEM(fibre_data.shape, jnp.float32),
+            pltpu.SemaphoreType.DMA((chunks,)),
+            pltpu.SemaphoreType.DMA,
+        ],
         compiler_params=params,
         name="rhs",
-    )(place, index, data, weights)
+    )(place, live_count, index, fibre_data, weights)
     moments = jnp.zeros(moment.shape, jnp.float32)
     vectors = []
     for power in range(3):
@@ -273,12 +292,15 @@
         vector, held, even, odd, moments = pl.pallas_call(
             functools.partial(step_kernel, power, final),
             out_shape=(window, window, out_rim, out_rim, moment_all if final else moment),
-            in_specs=smem(2) + vmem(5),
+            in_specs=smem(3) + vmem(5),
             out_specs=tuple(vmem(5)),
-            scratch_shapes=[pltpu.VMEM((EXTENT, 2 * waves, spaxels), jnp.bfloat16)],
+            scratch_shapes=[
+                pltpu.VMEM((EXTENT, 2 * waves, spaxels), jnp.bfloat16),
+                pltpu.VMEM((groups, 2 * waves, fibres), jnp.bfloat16),
+            ],
             compiler_params=params,
             name=f"step{power}",
-        )(place, index, held, even, odd, moments, weights)
+        )(place, live_count, index, held, even, odd, moments, weights)
         vectors.append(vector)
     even, odd = swap(even, odd)
     moments = lax.all_to_all(moments, ("tile", "wave"), 0, 0)

time: 72.7 us -> 62 us (0.85)
  Pallas kernels: 26.3 us -> 15.9 us
  other arithmetic: 0.76 us -> 0 us
    pallas_call x3, Pallas kernels: 21.5 us -> 10.8 us  [shards(): pl.pallas_call(functools.partial(step_kernel, power, final), out_shape=(w...]
    pallas_call x1, Pallas kernels: 2.9 us -> 3.7 us  [shards(): pl.pallas_call(rhs_kernel, out_shape=(jax.ShapeDtypeStruct(weights.shape,...]
    unnamed x5 -> x4, local copies, waits for them, and re-layouts: 3.25 us -> 3.14 us
where the time goes in v2:
time: 62 us; the launch traced here: 61.7 us
  starting transfers between devices  25.5 us (41%)
  Pallas kernels  15.9 us (26%)
  waiting for transfers between devices  15 us (24%)
  local copies, waits for them, and re-layouts  3.9 us (6%)
  between operations  1.35 us (2%)
    ppermute x4, starting transfers between devices, swap(): lax.ppermute(even, 'tile', even_pairs)  13.8 us
    ppermute x4, waiting for transfers between devices, swap(): lax.ppermute(even, 'tile', even_pairs)  11.9 us
    pallas_call x3, Pallas kernels, shards(): pl.pallas_call(functools.partial(step_kernel, power, final), out_shape=(w...  10.8 us
    all_to_all x1, starting transfers between devices, shards(): moments = lax.all_to_all(moments, ('tile', 'wave'), 0, 0)  9.15 us
    pallas_call x1, Pallas kernels, shards(): pl.pallas_call(rhs_kernel, out_shape=(jax.ShapeDtypeStruct(weights.shape,...  3.7 us
    unnamed x4, local copies, waits for them, and re-layouts  3.14 us
    all_to_all x1, waiting for transfers between devices, shards(): moments = lax.all_to_all(moments, ('tile', 'wave'), 0, 0)  3.13 us
    ppermute x4, starting transfers between devices, swap(): lax.ppermute(odd, 'tile', odd_pairs)  2.62 us
  transfers between devices with their start and end apart: 9, of which 5 were waited for; matrix products, arithmetic and copies ran while one was open for 0% of the time, Pallas kernels for 0%

profile of v2, /device:TPU:0, one launch (start us, length us, event | category | flops | bytes accessed | tf_op | source)
XLA Modules:
  0.0 61.7 jit_solution(17954070235720795694)
XLA Ops:
  1.3 0.8 %copy.9.index_ref = s32[32,4]{1,0:T(8,128)S(1)} copy(s32[32,4]{0,1:T(4,128)} %bitcast.4) | data formatting | bytes 1024 | tf_op jit(solution)/shard_map/reshape | solution.py:255
  2.0 0.0 copy-start
  2.0 2.2 %copy-done = bf16[1,32,4,128,128]{4,3,2,1,0:T(8,128)(2,1)S(1)} copy-done((bf16[1,32,4,128,128]{4,3,2,1,0:T(8,128)(2,1)S(1)}, bf16[1,32,4,128,128]{4,3,2,1,0:T(8,128)(2,1)}, u32[]{:S(2)}) %copy-start) | copy-done | bytes 4194328
  4.2 0.0 copy-start.1
  4.2 0.9 %copy-done.1 = bf16[32,32,128]{2,1,0:T(8,128)(2,1)S(1)} copy-done((bf16[32,32,128]{2,1,0:T(8,128)(2,1)S(1)}, bf16[32,32,128]{2,1,0:T(8,128)(2,1)}, u32[]{:S(2)}) %copy-start.1) | copy-done | bytes 262168
  5.2 3.7 %rhs.1 = (bf16[32,4,128,128]{3,2,1,0:T(8,128)(2,1)S(1)}, f32[24,32,128]{2,1,0:T(8,128)S(1)}, f32[8,32,128]{2,1,0:T(8,128)S(1)}, f32[8,32,128]{2,1,0:T(8,128)S(1)}) custom-call(s32[1]{0:T(128)} %bitcast.place_ref, s32[1]{0:T(128)S(6)} %copy.10.live_ref, s32[32,4]{1,0:T(8,128)S(1)} %copy.9.index_ref, bf16[32,32,128]{2,1,0:T(8,128)(2,1)S(1)} %copy-done.1, ...), custom_call_target="tpu_custom_call" | custom-call | tf_op jit(solution)/shard_map/rhs/pallas_call | solution.py:272
  8.9 3.0 %collective-permute-start = (f32[8,32,128]{2,1,0:T(8,128)S(1)}, f32[8,32,128]{2,1,0:T(8,128)S(1)}, u32[]{:S(2)}, u32[]{:S(2)}) collective-permute-start(f32[8,32,128]{2,1,0:T(8,128)S(1)} %get-tuple-element.22), channel_id=1, source_target_pairs={{0,4},{4,0},{8,12},{12,8},{16,20},{20,16},{24,28},{28,24},{1,5},{5... | collective-permute-start | bytes 393224 | tf_op jit(solution)/shard_map/ppermute | solution.py:269
  11.9 0.7 %collective-permute-start.1 = (f32[8,32,128]{2,1,0:T(8,128)S(1)}, f32[8,32,128]{2,1,0:T(8,128)S(1)}, u32[]{:S(2)}, u32[]{:S(2)}) collective-permute-start(f32[8,32,128]{2,1,0:T(8,128)S(1)} %get-tuple-element.23), channel_id=1, source_target_pairs={{4,8},{8,4},{12,16},{16,12},{20,24},{24,20},{5,9},{9,5},{13,17},{1... | collective-permute-start | bytes 393224 | tf_op jit(solution)/shard_map/ppermute | solution.py:269
  12.6 2.8 %collective-permute-done.even_in_ref = f32[8,32,128]{2,1,0:T(8,128)S(1)} collective-permute-done((f32[8,32,128]{2,1,0:T(8,128)S(1)}, f32[8,32,128]{2,1,0:T(8,128)S(1)}, u32[]{:S(2)}, u32[]{:S(2)}) %collective-permute-start) | collective-permute-done | bytes 131104 | tf_op jit(solution)/shard_map/ppermute | solution.py:269
  15.4 0.0 collective-permute-done.1.odd_in_ref
  15.4 3.4 %step0.1 = (f32[24,32,128]{2,1,0:T(8,128)S(1)}, f32[24,32,128]{2,1,0:T(8,128)S(1)}, f32[8,32,128]{2,1,0:T(8,128)S(1)}, f32[8,32,128]{2,1,0:T(8,128)S(1)}, f32[8,128]{1,0:T(8,128)S(1)}) custom-call(s32[1]{0:T(128)} %bitcast.place_ref, s32[1]{0:T(128)S(6)} %copy.10.live_ref, s32[32,4]{1,0:T(8,128)S(1)} %copy.9.index_ref, ...), custom_call_target="tpu_custom_call" | custom-call | tf_op jit(solution)/shard_map/step0/pallas_call | solution.py:292
  18.9 4.7 %collective-permute-start.2 = (f32[8,32,128]{2,1,0:T(8,128)S(1)}, f32[8,32,128]{2,1,0:T(8,128)S(1)}, u32[]{:S(2)}, u32[]{:S(2)}) collective-permute-start(f32[8,32,128]{2,1,0:T(8,128)S(1)} %get-tuple-element.26), channel_id=1, source_target_pairs={{0,4},{4,0},{8,12},{12,8},{16,20},{20,16},{24,28},{28,24},{1,5},{5... | collective-permute-start | bytes 393224 | tf_op jit(solution)/shard_map/ppermute | solution.py:269
  23.6 0.7 %collective-permute-start.3 = (f32[8,32,128]{2,1,0:T(8,128)S(1)}, f32[8,32,128]{2,1,0:T(8,128)S(1)}, u32[]{:S(2)}, u32[]{:S(2)}) collective-permute-start(f32[8,32,128]{2,1,0:T(8,128)S(1)} %get-tuple-element.27), channel_id=1, source_target_pairs={{4,8},{8,4},{12,16},{16,12},{20,24},{24,20},{5,9},{9,5},{13,17},{1... | collective-permute-start | bytes 393224 | tf_op jit(solution)/shard_map/ppermute | solution.py:269
  24.3 3.3 %collective-permute-done.2.even_in_ref = f32[8,32,128]{2,1,0:T(8,128)S(1)} collective-permute-done((f32[8,32,128]{2,1,0:T(8,128)S(1)}, f32[8,32,128]{2,1,0:T(8,128)S(1)}, u32[]{:S(2)}, u32[]{:S(2)}) %collective-permute-start.2) | collective-permute-done | bytes 131104 | tf_op jit(solution)/shard_map/ppermute | solution.py:269
  27.5 0.0 collective-permute-done.3.odd_in_ref
  27.5 3.4 %step1.1 = (f32[24,32,128]{2,1,0:T(8,128)S(1)}, f32[24,32,128]{2,1,0:T(8,128)S(1)}, f32[8,32,128]{2,1,0:T(8,128)S(1)}, f32[8,32,128]{2,1,0:T(8,128)S(1)}, f32[8,128]{1,0:T(8,128)S(1)}) custom-call(s32[1]{0:T(128)} %bitcast.place_ref, s32[1]{0:T(128)S(6)} %copy.10.live_ref, s32[32,4]{1,0:T(8,128)S(1)} %copy.9.index_ref, ...), custom_call_target="tpu_custom_call" | custom-call | tf_op jit(solution)/shard_map/step1/pallas_call | solution.py:292
  31.0 4.2 %collective-permute-start.4 = (f32[8,32,128]{2,1,0:T(8,128)S(1)}, f32[8,32,128]{2,1,0:T(8,128)S(1)}, u32[]{:S(2)}, u32[]{:S(2)}) collective-permute-start(f32[8,32,128]{2,1,0:T(8,128)S(1)} %get-tuple-element.30), channel_id=1, source_target_pairs={{0,4},{4,0},{8,12},{12,8},{16,20},{20,16},{24,28},{28,24},{1,5},{5... | collective-permute-start | bytes 393224 | tf_op jit(solution)/shard_map/ppermute | solution.py:269
  35.2 0.7 %collective-permute-start.5 = (f32[8,32,128]{2,1,0:T(8,128)S(1)}, f32[8,32,128]{2,1,0:T(8,128)S(1)}, u32[]{:S(2)}, u32[]{:S(2)}) collective-permute-start(f32[8,32,128]{2,1,0:T(8,128)S(1)} %get-tuple-element.31), channel_id=1, source_target_pairs={{4,8},{8,4},{12,16},{16,12},{20,24},{24,20},{5,9},{9,5},{13,17},{1... | collective-permute-start | bytes 393224 | tf_op jit(solution)/shard_map/ppermute | solution.py:269
  35.8 3.2 %collective-permute-done.4.even_in_ref = f32[8,32,128]{2,1,0:T(8,128)S(1)} collective-permute-done((f32[8,32,128]{2,1,0:T(8,128)S(1)}, f32[8,32,128]{2,1,0:T(8,128)S(1)}, u32[]{:S(2)}, u32[]{:S(2)}) %collective-permute-start.4) | collective-permute-done | bytes 131104 | tf_op jit(solution)/shard_map/ppermute | solution.py:269
  39.0 0.0 collective-permute-done.5.odd_in_ref
  39.0 3.9 %step2.1 = (f32[24,32,128]{2,1,0:T(8,128)S(1)}, f32[24,32,128]{2,1,0:T(8,128)S(1)}, f32[4,32,128]{2,1,0:T(8,128)S(1)}, f32[4,32,128]{2,1,0:T(8,128)S(1)}, f32[32,8,128]{2,1,0:T(8,128)}) custom-call(s32[1]{0:T(128)} %bitcast.place_ref, s32[1]{0:T(128)S(6)} %copy.10.live_ref, s32[32,4]{1,0:T(8,128)S(1)} %copy.9.index_ref, ...), custom_call_target="tpu_custom_call" | custom-call | tf_op jit(solution)/shard_map/step2/pallas_call | solution.py:292
  43.0 9.2 %all-to-all-start = ((f32[32,8,128]{2,1,0:T(8,128)}), f32[32,8,128]{2,1,0:T(8,128)S(1)}, u32[]{:S(2)}, u32[]{:S(2)}) async-start(f32[32,8,128]{2,1,0:T(8,128)} %get-tuple-element.33), calls=%async_computation | async-start | bytes 262144 | tf_op jit(solution)/shard_map/all_to_all | solution.py:306
  52.1 1.8 %collective-permute-start.6 = (f32[4,32,128]{2,1,0:T(8,128)S(1)}, f32[4,32,128]{2,1,0:T(8,128)S(1)}, u32[]{:S(2)}, u32[]{:S(2)}) collective-permute-start(f32[4,32,128]{2,1,0:T(8,128)S(1)} %get-tuple-element.38), channel_id=1, source_target_pairs={{0,4},{4,0},{8,12},{12,8},{16,20},{20,16},{24,28},{28,24},{1,5},{5... | collective-permute-start | bytes 196616 | tf_op jit(solution)/shard_map/ppermute | solution.py:269
  54.0 0.7 %collective-permute-start.7 = (f32[4,32,128]{2,1,0:T(8,128)S(1)}, f32[4,32,128]{2,1,0:T(8,128)S(1)}, u32[]{:S(2)}, u32[]{:S(2)}) collective-permute-start(f32[4,32,128]{2,1,0:T(8,128)S(1)} %get-tuple-element.39), channel_id=1, source_target_pairs={{4,8},{8,4},{12,16},{16,12},{20,24},{24,20},{5,9},{9,5},{13,17},{1... | collective-permute-start | bytes 196616 | tf_op jit(solution)/shard_map/ppermute | solution.py:269
  54.6 2.6 %collective-permute-done.6.even_in_ref = f32[4,32,128]{2,1,0:T(8,128)S(1)} collective-permute-done((f32[4,32,128]{2,1,0:T(8,128)S(1)}, f32[4,32,128]{2,1,0:T(8,128)S(1)}, u32[]{:S(2)}, u32[]{:S(2)}) %collective-permute-start.6) | collective-permute-done | bytes 65568 | tf_op jit(solution)/shard_map/ppermute | solution.py:269
  57.2 0.0 collective-permute-done.7.odd_in_ref
  57.2 3.1 %all-to-all-done.moments_ref = f32[32,8,128]{2,1,0:T(8,128)S(1)} async-done(((f32[32,8,128]{2,1,0:T(8,128)}), f32[32,8,128]{2,1,0:T(8,128)S(1)}, u32[]{:S(2)}, u32[]{:S(2)}) %all-to-all-start) | async-done | bytes 131104 | tf_op jit(solution)/shard_map/all_to_all | solution.py:306
  60.3 1.4 %combine.1 = (f32[32,16,128]{2,1,0:T(8,128)}, f32[32,16,128]{2,1,0:T(8,128)}) custom-call(s32[1]{0:T(128)} %bitcast.place_ref, f32[32,8,128]{2,1,0:T(8,128)S(1)} %all-to-all-done.moments_ref, f32[24,32,128]{2,1,0:T(8,128)S(1)} %get-tuple-element.34.first_ref, f32[24,32,128]{2,1,0:T(8,128)S(1)} %get-tuple-element.35.second_ref, ...), custom_call_target="tpu_custom_call" | custom-call | tf_op jit(solution)/shard_map/combine/pallas_call | solution.py:308
  (1 shorter events, 0.0 us)
Async XLA Ops:
  2.0 2.2 %copy-start = (bf16[1,32,4,128,128]{4,3,2,1,0:T(8,128)(2,1)S(1)}, bf16[1,32,4,128,128]{4,3,2,1,0:T(8,128)(2,1)}, u32[]{:S(2)}) copy-start(bf16[1,32,4,128,128]{4,3,2,1,0:T(8,128)(2,1)} %param.5) | copy-start | bytes 12582916
  4.2 0.9 %copy-start.1 = (bf16[32,32,128]{2,1,0:T(8,128)(2,1)S(1)}, bf16[32,32,128]{2,1,0:T(8,128)(2,1)}, u32[]{:S(2)}) copy-start(bf16[32,32,128]{2,1,0:T(8,128)(2,1)} %data_ref.1) | copy-start | bytes 786436
  8.9 6.5 %collective-permute-start = (f32[8,32,128]{2,1,0:T(8,128)S(1)}, f32[8,32,128]{2,1,0:T(8,128)S(1)}, u32[]{:S(2)}, u32[]{:S(2)}) collective-permute-start(f32[8,32,128]{2,1,0:T(8,128)S(1)} %get-tuple-element.22), channel_id=1, source_target_pairs={{0,4},{4,0},{8,12},{12,8},{16,20},{20,16},{24,28},{28,24},{1,5},{5... | collective-permute-start | bytes 393224 | tf_op jit(solution)/shard_map/ppermute | solution.py:269
  11.9 3.5 %collective-permute-start.1 = (f32[8,32,128]{2,1,0:T(8,128)S(1)}, f32[8,32,128]{2,1,0:T(8,128)S(1)}, u32[]{:S(2)}, u32[]{:S(2)}) collective-permute-start(f32[8,32,128]{2,1,0:T(8,128)S(1)} %get-tuple-element.23), channel_id=1, source_target_pairs={{4,8},{8,4},{12,16},{16,12},{20,24},{24,20},{5,9},{9,5},{13,17},{1... | collective-permute-start | bytes 393224 | tf_op jit(solution)/shard_map/ppermute | solution.py:269
  18.9 8.6 %collective-permute-start.2 = (f32[8,32,128]{2,1,0:T(8,128)S(1)}, f32[8,32,128]{2,1,0:T(8,128)S(1)}, u32[]{:S(2)}, u32[]{:S(2)}) collective-permute-start(f32[8,32,128]{2,1,0:T(8,128)S(1)} %get-tuple-element.26), channel_id=1, source_target_pairs={{0,4},{4,0},{8,12},{12,8},{16,20},{20,16},{24,28},{28,24},{1,5},{5... | collective-permute-start | bytes 393224 | tf_op jit(solution)/shard_map/ppermute | solution.py:269
  23.6 3.9 %collective-permute-start.3 = (f32[8,32,128]{2,1,0:T(8,128)S(1)}, f32[8,32,128]{2,1,0:T(8,128)S(1)}, u32[]{:S(2)}, u32[]{:S(2)}) collective-permute-start(f32[8,32,128]{2,1,0:T(8,128)S(1)} %get-tuple-element.27), channel_id=1, source_target_pairs={{4,8},{8,4},{12,16},{16,12},{20,24},{24,20},{5,9},{9,5},{13,17},{1... | collective-permute-start | bytes 393224 | tf_op jit(solution)/shard_map/ppermute | solution.py:269
  31.0 8.1 %collective-permute-start.4 = (f32[8,32,128]{2,1,0:T(8,128)S(1)}, f32[8,32,128]{2,1,0:T(8,128)S(1)}, u32[]{:S(2)}, u32[]{:S(2)}) collective-permute-start(f32[8,32,128]{2,1,0:T(8,128)S(1)} %get-tuple-element.30), channel_id=1, source_target_pairs={{0,4},{4,0},{8,12},{12,8},{16,20},{20,16},{24,28},{28,24},{1,5},{5... | collective-permute-start | bytes 393224 | tf_op jit(solution)/shard_map/ppermute | solution.py:269
  35.2 3.9 %collective-permute-start.5 = (f32[8,32,128]{2,1,0:T(8,128)S(1)}, f32[8,32,128]{2,1,0:T(8,128)S(1)}, u32[]{:S(2)}, u32[]{:S(2)}) collective-permute-start(f32[8,32,128]{2,1,0:T(8,128)S(1)} %get-tuple-element.31), channel_id=1, source_target_pairs={{4,8},{8,4},{12,16},{16,12},{20,24},{24,20},{5,9},{9,5},{13,17},{1... | collective-permute-start | bytes 393224 | tf_op jit(solution)/shard_map/ppermute | solution.py:269
  43.0 17.4 %all-to-all-start = ((f32[32,8,128]{2,1,0:T(8,128)}), f32[32,8,128]{2,1,0:T(8,128)S(1)}, u32[]{:S(2)}, u32[]{:S(2)}) async-start(f32[32,8,128]{2,1,0:T(8,128)} %get-tuple-element.33), calls=%async_computation | async-start | bytes 262144 | tf_op jit(solution)/shard_map/all_to_all | solution.py:306
  52.1 5.1 %collective-permute-start.6 = (f32[4,32,128]{2,1,0:T(8,128)S(1)}, f32[4,32,128]{2,1,0:T(8,128)S(1)}, u32[]{:S(2)}, u32[]{:S(2)}) collective-permute-start(f32[4,32,128]{2,1,0:T(8,128)S(1)} %get-tuple-element.38), channel_id=1, source_target_pairs={{0,4},{4,0},{8,12},{12,8},{16,20},{20,16},{24,28},{28,24},{1,5},{5... | collective-permute-start | bytes 196616 | tf_op jit(solution)/shard_map/ppermute | solution.py:269
  54.0 3.2 %collective-permute-start.7 = (f32[4,32,128]{2,1,0:T(8,128)S(1)}, f32[4,32,128]{2,1,0:T(8,128)S(1)}, u32[]{:S(2)}, u32[]{:S(2)}) collective-permute-start(f32[4,32,128]{2,1,0:T(8,128)S(1)} %get-tuple-element.39), channel_id=1, source_target_pairs={{4,8},{8,4},{12,16},{16,12},{20,24},{24,20},{5,9},{9,5},{13,17},{1... | collective-permute-start | bytes 196616 | tf_op jit(solution)/shard_map/ppermute | solution.py:269

commit v3 on v2

--- a/solution.py
+++ b/solution.py
@@ -31,8 +31,8 @@
 def scatter(spread, place_ref, index_ref, group, partial_ref):
     lanes = partial_ref.shape[2]
     first = place_ref[0] * BLOCKS_DEV - HALO_BLOCKS
-    for slot in range(index_ref.shape[1]):
-        block = index_ref[group, slot] - first
+    for slot in range(index_ref.shape[0]):
+        block = index_ref[slot, group] - first
         partial_ref[block] += spread[:, slot * lanes : (slot + 1) * lanes]
 
 
@@ -128,7 +128,7 @@
     energy = jnp.zeros((waves, fibres), jnp.float32)
     for group in range(groups):
         picked = jnp.concatenate(
-            [operand_ref[index_ref[group, slot] - first_block] for slot in range(slots)], axis=1
+            [operand_ref[index_ref[slot, group] - first_block] for slot in range(slots)], axis=1
         )
         weights = kernels_ref[group].reshape(slots * spaxels, fibres)
         image = halves_sum(jnp.dot(picked, weights, preferred_element_type=jnp.float32))
@@ -252,7 +252,7 @@
     _, groups, slots, spaxels, fibres = kernels.shape
     waves = fibre_data.shape[0]
     place = lax.axis_index("tile").reshape(1)
-    index = block_index.reshape(groups, slots)
+    index = jnp.swapaxes(block_index, 1, 2).reshape(slots, groups)
     weights = kernels.reshape(groups, slots, spaxels, fibres)
     window = jax.ShapeDtypeStruct((EXTENT, waves, spaxels), jnp.float32)
     rim = jax.ShapeDtypeStruct((RIM, waves, spaxels), jnp.float32)
@@ -282,7 +282,13 @@
         ],
         compiler_params=params,
         name="rhs",
-    )(place, live_count, index, fibre_data, weights)
+    )(
+        place,
+        live_count,
+        index,
+        pltpu.with_memory_space_constraint(fibre_data, pltpu.HBM),
+        pltpu.with_memory_space_constraint(weights, pltpu.HBM),
+    )
     moments = jnp.zeros(moment.shape, jnp.float32)
     vectors = []
     for power in range(3):

time: 62 us -> 59.3 us (0.956)
  local copies, waits for them, and re-layouts: 3.9 us -> 0.68 us
    unnamed x4 -> x2, local copies, waits for them, and re-layouts: 3.14 us -> 0.67 us
    pallas_call x1, Pallas kernels: 3.7 us -> 5.13 us  [shards(): pl.pallas_call(rhs_kernel, out_shape=(jax.ShapeDtypeStruct(weights.shape,...]
    pallas_call x3, Pallas kernels: 10.8 us -> 9.94 us  [shards(): pl.pallas_call(functools.partial(step_kernel, power, final), out_shape=(w...]
    reshape x1 -> x0, local copies, waits for them, and re-layouts: 0.76 us -> none  [shards(): index = block_index.reshape(groups, slots)]
where the time goes in v3:
time: 59.3 us; the launch traced here: 59 us
  starting transfers between devices  25.5 us (43%)
  Pallas kernels  16.4 us (28%)
  waiting for transfers between devices  15 us (25%)
  between operations  1.36 us (2%)
  local copies, waits for them, and re-layouts  0.68 us (1%)
    ppermute x4, starting transfers between devices, swap(): lax.ppermute(even, 'tile', even_pairs)  13.7 us
    ppermute x4, waiting for transfers between devices, swap(): lax.ppermute(even, 'tile', even_pairs)  11.9 us
    pallas_call x3, Pallas kernels, shards(): pl.pallas_call(functools.partial(step_kernel, power, final), out_shape=(w...  9.94 us
    all_to_all x1, starting transfers between devices, shards(): moments = lax.all_to_all(moments, ('tile', 'wave'), 0, 0)  9.12 us
    pallas_call x1, Pallas kernels, shards(): pl.pallas_call(rhs_kernel, out_shape=(jax.ShapeDtypeStruct(weights.shape,...  5.13 us
    all_to_all x1, waiting for transfers between devices, shards(): moments = lax.all_to_all(moments, ('tile', 'wave'), 0, 0)  3.13 us
    ppermute x4, starting transfers between devices, swap(): lax.ppermute(odd, 'tile', odd_pairs)  2.62 us
    pallas_call x1, Pallas kernels, shards(): pl.pallas_call(final_kernel, out_shape=(out, out), in_specs=smem(1) + vme...  1.36 us
  transfers between devices with their start and end apart: 9, of which 5 were waited for; matrix products, arithmetic and copies ran while one was open for 0% of the time, Pallas kernels for 0%

profile of v3, /device:TPU:0, one launch (start us, length us, event | category | flops | bytes accessed | tf_op | source)
XLA Modules:
  0.0 59.0 jit_solution(17672121154040213303)
XLA Ops:
  1.3 0.0 copy-start
  1.3 0.7 %copy-done = s32[1,32,4]{1,2,0:T(4,128)S(1)} copy-done((s32[1,32,4]{1,2,0:T(4,128)S(1)}, s32[1,32,4]{1,2,0:T(4,128)}, u32[]{:S(2)}) %copy-start) | copy-done | bytes 536
  2.0 5.1 %rhs.1 = (bf16[32,4,128,128]{3,2,1,0:T(8,128)(2,1)S(1)}, f32[24,32,128]{2,1,0:T(8,128)S(1)}, f32[8,32,128]{2,1,0:T(8,128)S(1)}, f32[8,32,128]{2,1,0:T(8,128)S(1)}) custom-call(s32[1]{0:T(128)} %bitcast.place_ref, s32[1]{0:T(128)S(6)} %copy.6.live_ref, s32[4,32]{1,0:T(4,128)S(1)} %bitcast.5, bf16[32,32,128]{2,1,0:T(8,128)(2,1)} %data_ref.1, ...), custom_call_target="tpu_custom_call" | custom-call | tf_op jit(solution)/shard_map/rhs/pallas_call | solution.py:272
  7.1 3.0 %collective-permute-start = (f32[8,32,128]{2,1,0:T(8,128)S(1)}, f32[8,32,128]{2,1,0:T(8,128)S(1)}, u32[]{:S(2)}, u32[]{:S(2)}) collective-permute-start(f32[8,32,128]{2,1,0:T(8,128)S(1)} %get-tuple-element.22), channel_id=1, source_target_pairs={{0,4},{4,0},{8,12},{12,8},{16,20},{20,16},{24,28},{28,24},{1,5},{5... | collective-permute-start | bytes 393224 | tf_op jit(solution)/shard_map/ppermute | solution.py:269
  10.1 0.7 %collective-permute-start.1 = (f32[8,32,128]{2,1,0:T(8,128)S(1)}, f32[8,32,128]{2,1,0:T(8,128)S(1)}, u32[]{:S(2)}, u32[]{:S(2)}) collective-permute-start(f32[8,32,128]{2,1,0:T(8,128)S(1)} %get-tuple-element.23), channel_id=1, source_target_pairs={{4,8},{8,4},{12,16},{16,12},{20,24},{24,20},{5,9},{9,5},{13,17},{1... | collective-permute-start | bytes 393224 | tf_op jit(solution)/shard_map/ppermute | solution.py:269
  10.8 2.8 %collective-permute-done.even_in_ref = f32[8,32,128]{2,1,0:T(8,128)S(1)} collective-permute-done((f32[8,32,128]{2,1,0:T(8,128)S(1)}, f32[8,32,128]{2,1,0:T(8,128)S(1)}, u32[]{:S(2)}, u32[]{:S(2)}) %collective-permute-start) | collective-permute-done | bytes 131104 | tf_op jit(solution)/shard_map/ppermute | solution.py:269
  13.6 0.0 collective-permute-done.1.odd_in_ref
  13.6 3.2 %step0.1 = (f32[24,32,128]{2,1,0:T(8,128)S(1)}, f32[24,32,128]{2,1,0:T(8,128)S(1)}, f32[8,32,128]{2,1,0:T(8,128)S(1)}, f32[8,32,128]{2,1,0:T(8,128)S(1)}, f32[8,128]{1,0:T(8,128)S(1)}) custom-call(s32[1]{0:T(128)} %bitcast.place_ref, s32[1]{0:T(128)S(6)} %copy.6.live_ref, s32[4,32]{1,0:T(4,128)S(1)} %bitcast.6, ...), custom_call_target="tpu_custom_call" | custom-call | tf_op jit(solution)/shard_map/step0/pallas_call | solution.py:298
  16.8 4.7 %collective-permute-start.2 = (f32[8,32,128]{2,1,0:T(8,128)S(1)}, f32[8,32,128]{2,1,0:T(8,128)S(1)}, u32[]{:S(2)}, u32[]{:S(2)}) collective-permute-start(f32[8,32,128]{2,1,0:T(8,128)S(1)} %get-tuple-element.26), channel_id=1, source_target_pairs={{0,4},{4,0},{8,12},{12,8},{16,20},{20,16},{24,28},{28,24},{1,5},{5... | collective-permute-start | bytes 393224 | tf_op jit(solution)/shard_map/ppermute | solution.py:269
  21.5 0.7 %collective-permute-start.3 = (f32[8,32,128]{2,1,0:T(8,128)S(1)}, f32[8,32,128]{2,1,0:T(8,128)S(1)}, u32[]{:S(2)}, u32[]{:S(2)}) collective-permute-start(f32[8,32,128]{2,1,0:T(8,128)S(1)} %get-tuple-element.27), channel_id=1, source_target_pairs={{4,8},{8,4},{12,16},{16,12},{20,24},{24,20},{5,9},{9,5},{13,17},{1... | collective-permute-start | bytes 393224 | tf_op jit(solution)/shard_map/ppermute | solution.py:269
  22.2 3.3 %collective-permute-done.2.even_in_ref = f32[8,32,128]{2,1,0:T(8,128)S(1)} collective-permute-done((f32[8,32,128]{2,1,0:T(8,128)S(1)}, f32[8,32,128]{2,1,0:T(8,128)S(1)}, u32[]{:S(2)}, u32[]{:S(2)}) %collective-permute-start.2) | collective-permute-done | bytes 131104 | tf_op jit(solution)/shard_map/ppermute | solution.py:269
  25.4 0.0 collective-permute-done.3.odd_in_ref
  25.4 3.1 %step1.1 = (f32[24,32,128]{2,1,0:T(8,128)S(1)}, f32[24,32,128]{2,1,0:T(8,128)S(1)}, f32[8,32,128]{2,1,0:T(8,128)S(1)}, f32[8,32,128]{2,1,0:T(8,128)S(1)}, f32[8,128]{1,0:T(8,128)S(1)}) custom-call(s32[1]{0:T(128)} %bitcast.place_ref, s32[1]{0:T(128)S(6)} %copy.6.live_ref, s32[4,32]{1,0:T(4,128)S(1)} %bitcast.7, ...), custom_call_target="tpu_custom_call" | custom-call | tf_op jit(solution)/shard_map/step1/pallas_call | solution.py:298
  28.6 4.1 %collective-permute-start.4 = (f32[8,32,128]{2,1,0:T(8,128)S(1)}, f32[8,32,128]{2,1,0:T(8,128)S(1)}, u32[]{:S(2)}, u32[]{:S(2)}) collective-permute-start(f32[8,32,128]{2,1,0:T(8,128)S(1)} %get-tuple-element.30), channel_id=1, source_target_pairs={{0,4},{4,0},{8,12},{12,8},{16,20},{20,16},{24,28},{28,24},{1,5},{5... | collective-permute-start | bytes 393224 | tf_op jit(solution)/shard_map/ppermute | solution.py:269
  32.7 0.7 %collective-permute-start.5 = (f32[8,32,128]{2,1,0:T(8,128)S(1)}, f32[8,32,128]{2,1,0:T(8,128)S(1)}, u32[]{:S(2)}, u32[]{:S(2)}) collective-permute-start(f32[8,32,128]{2,1,0:T(8,128)S(1)} %get-tuple-element.31), channel_id=1, source_target_pairs={{4,8},{8,4},{12,16},{16,12},{20,24},{24,20},{5,9},{9,5},{13,17},{1... | collective-permute-start | bytes 393224 | tf_op jit(solution)/shard_map/ppermute | solution.py:269
  33.4 3.2 %collective-permute-done.4.even_in_ref = f32[8,32,128]{2,1,0:T(8,128)S(1)} collective-permute-done((f32[8,32,128]{2,1,0:T(8,128)S(1)}, f32[8,32,128]{2,1,0:T(8,128)S(1)}, u32[]{:S(2)}, u32[]{:S(2)}) %collective-permute-start.4) | collective-permute-done | bytes 131104 | tf_op jit(solution)/shard_map/ppermute | solution.py:269
  36.6 0.0 collective-permute-done.5.odd_in_ref
  36.6 3.6 %step2.1 = (f32[24,32,128]{2,1,0:T(8,128)S(1)}, f32[24,32,128]{2,1,0:T(8,128)S(1)}, f32[4,32,128]{2,1,0:T(8,128)S(1)}, f32[4,32,128]{2,1,0:T(8,128)S(1)}, f32[32,8,128]{2,1,0:T(8,128)}) custom-call(s32[1]{0:T(128)} %bitcast.place_ref, s32[1]{0:T(128)S(6)} %copy.6.live_ref, s32[4,32]{1,0:T(4,128)S(1)} %bitcast.8, ...), custom_call_target="tpu_custom_call" | custom-call | tf_op jit(solution)/shard_map/step2/pallas_call | solution.py:298
  40.3 9.1 %all-to-all-start = ((f32[32,8,128]{2,1,0:T(8,128)}), f32[32,8,128]{2,1,0:T(8,128)S(1)}, u32[]{:S(2)}, u32[]{:S(2)}) async-start(f32[32,8,128]{2,1,0:T(8,128)} %get-tuple-element.33), calls=%async_computation | async-start | bytes 262144 | tf_op jit(solution)/shard_map/all_to_all | solution.py:312
  49.4 1.8 %collective-permute-start.6 = (f32[4,32,128]{2,1,0:T(8,128)S(1)}, f32[4,32,128]{2,1,0:T(8,128)S(1)}, u32[]{:S(2)}, u32[]{:S(2)}) collective-permute-start(f32[4,32,128]{2,1,0:T(8,128)S(1)} %get-tuple-element.38), channel_id=1, source_target_pairs={{0,4},{4,0},{8,12},{12,8},{16,20},{20,16},{24,28},{28,24},{1,5},{5... | collective-permute-start | bytes 196616 | tf_op jit(solution)/shard_map/ppermute | solution.py:269
  51.2 0.7 %collective-permute-start.7 = (f32[4,32,128]{2,1,0:T(8,128)S(1)}, f32[4,32,128]{2,1,0:T(8,128)S(1)}, u32[]{:S(2)}, u32[]{:S(2)}) collective-permute-start(f32[4,32,128]{2,1,0:T(8,128)S(1)} %get-tuple-element.39), channel_id=1, source_target_pairs={{4,8},{8,4},{12,16},{16,12},{20,24},{24,20},{5,9},{9,5},{13,17},{1... | collective-permute-start | bytes 196616 | tf_op jit(solution)/shard_map/ppermute | solution.py:269
  51.9 2.6 %collective-permute-done.6.even_in_ref = f32[4,32,128]{2,1,0:T(8,128)S(1)} collective-permute-done((f32[4,32,128]{2,1,0:T(8,128)S(1)}, f32[4,32,128]{2,1,0:T(8,128)S(1)}, u32[]{:S(2)}, u32[]{:S(2)}) %collective-permute-start.6) | collective-permute-done | bytes 65568 | tf_op jit(solution)/shard_map/ppermute | solution.py:269
  54.5 0.0 collective-permute-done.7.odd_in_ref
  54.5 3.1 %all-to-all-done.moments_ref = f32[32,8,128]{2,1,0:T(8,128)S(1)} async-done(((f32[32,8,128]{2,1,0:T(8,128)}), f32[32,8,128]{2,1,0:T(8,128)S(1)}, u32[]{:S(2)}, u32[]{:S(2)}) %all-to-all-start) | async-done | bytes 131104 | tf_op jit(solution)/shard_map/all_to_all | solution.py:312
  57.6 1.4 %combine.1 = (f32[32,16,128]{2,1,0:T(8,128)}, f32[32,16,128]{2,1,0:T(8,128)}) custom-call(s32[1]{0:T(128)} %bitcast.place_ref, f32[32,8,128]{2,1,0:T(8,128)S(1)} %all-to-all-done.moments_ref, f32[24,32,128]{2,1,0:T(8,128)S(1)} %get-tuple-element.34.first_ref, f32[24,32,128]{2,1,0:T(8,128)S(1)} %get-tuple-element.35.second_ref, ...), custom_call_target="tpu_custom_call" | custom-call | tf_op jit(solution)/shard_map/combine/pallas_call | solution.py:314
  (1 shorter events, 0.0 us)
Async XLA Ops:
  1.3 0.7 %copy-start = (s32[1,32,4]{1,2,0:T(4,128)S(1)}, s32[1,32,4]{1,2,0:T(4,128)}, u32[]{:S(2)}) copy-start(s32[1,32,4]{1,2,0:T(4,128)} %param.6) | copy-start | bytes 1540
  7.1 6.5 %collective-permute-start = (f32[8,32,128]{2,1,0:T(8,128)S(1)}, f32[8,32,128]{2,1,0:T(8,128)S(1)}, u32[]{:S(2)}, u32[]{:S(2)}) collective-permute-start(f32[8,32,128]{2,1,0:T(8,128)S(1)} %get-tuple-element.22), channel_id=1, source_target_pairs={{0,4},{4,0},{8,12},{12,8},{16,20},{20,16},{24,28},{28,24},{1,5},{5... | collective-permute-start | bytes 393224 | tf_op jit(solution)/shard_map/ppermute | solution.py:269
  10.1 3.5 %collective-permute-start.1 = (f32[8,32,128]{2,1,0:T(8,128)S(1)}, f32[8,32,128]{2,1,0:T(8,128)S(1)}, u32[]{:S(2)}, u32[]{:S(2)}) collective-permute-start(f32[8,32,128]{2,1,0:T(8,128)S(1)} %get-tuple-element.23), channel_id=1, source_target_pairs={{4,8},{8,4},{12,16},{16,12},{20,24},{24,20},{5,9},{9,5},{13,17},{1... | collective-permute-start | bytes 393224 | tf_op jit(solution)/shard_map/ppermute | solution.py:269
  16.8 8.6 %collective-permute-start.2 = (f32[8,32,128]{2,1,0:T(8,128)S(1)}, f32[8,32,128]{2,1,0:T(8,128)S(1)}, u32[]{:S(2)}, u32[]{:S(2)}) collective-permute-start(f32[8,32,128]{2,1,0:T(8,128)S(1)} %get-tuple-element.26), channel_id=1, source_target_pairs={{0,4},{4,0},{8,12},{12,8},{16,20},{20,16},{24,28},{28,24},{1,5},{5... | collective-permute-start | bytes 393224 | tf_op jit(solution)/shard_map/ppermute | solution.py:269
  21.5 3.9 %collective-permute-start.3 = (f32[8,32,128]{2,1,0:T(8,128)S(1)}, f32[8,32,128]{2,1,0:T(8,128)S(1)}, u32[]{:S(2)}, u32[]{:S(2)}) collective-permute-start(f32[8,32,128]{2,1,0:T(8,128)S(1)} %get-tuple-element.27), channel_id=1, source_target_pairs={{4,8},{8,4},{12,16},{16,12},{20,24},{24,20},{5,9},{9,5},{13,17},{1... | collective-permute-start | bytes 393224 | tf_op jit(solution)/shard_map/ppermute | solution.py:269
  28.6 8.0 %collective-permute-start.4 = (f32[8,32,128]{2,1,0:T(8,128)S(1)}, f32[8,32,128]{2,1,0:T(8,128)S(1)}, u32[]{:S(2)}, u32[]{:S(2)}) collective-permute-start(f32[8,32,128]{2,1,0:T(8,128)S(1)} %get-tuple-element.30), channel_id=1, source_target_pairs={{0,4},{4,0},{8,12},{12,8},{16,20},{20,16},{24,28},{28,24},{1,5},{5... | collective-permute-start | bytes 393224 | tf_op jit(solution)/shard_map/ppermute | solution.py:269
  32.7 3.9 %collective-permute-start.5 = (f32[8,32,128]{2,1,0:T(8,128)S(1)}, f32[8,32,128]{2,1,0:T(8,128)S(1)}, u32[]{:S(2)}, u32[]{:S(2)}) collective-permute-start(f32[8,32,128]{2,1,0:T(8,128)S(1)} %get-tuple-element.31), channel_id=1, source_target_pairs={{4,8},{8,4},{12,16},{16,12},{20,24},{24,20},{5,9},{9,5},{13,17},{1... | collective-permute-start | bytes 393224 | tf_op jit(solution)/shard_map/ppermute | solution.py:269
  40.3 17.3 %all-to-all-start = ((f32[32,8,128]{2,1,0:T(8,128)}), f32[32,8,128]{2,1,0:T(8,128)S(1)}, u32[]{:S(2)}, u32[]{:S(2)}) async-start(f32[32,8,128]{2,1,0:T(8,128)} %get-tuple-element.33), calls=%async_computation | async-start | bytes 262144 | tf_op jit(solution)/shard_map/all_to_all | solution.py:312
  49.4 5.1 %collective-permute-start.6 = (f32[4,32,128]{2,1,0:T(8,128)S(1)}, f32[4,32,128]{2,1,0:T(8,128)S(1)}, u32[]{:S(2)}, u32[]{:S(2)}) collective-permute-start(f32[4,32,128]{2,1,0:T(8,128)S(1)} %get-tuple-element.38), channel_id=1, source_target_pairs={{0,4},{4,0},{8,12},{12,8},{16,20},{20,16},{24,28},{28,24},{1,5},{5... | collective-permute-start | bytes 196616 | tf_op jit(solution)/shard_map/ppermute | solution.py:269
  51.2 3.2 %collective-permute-start.7 = (f32[4,32,128]{2,1,0:T(8,128)S(1)}, f32[4,32,128]{2,1,0:T(8,128)S(1)}, u32[]{:S(2)}, u32[]{:S(2)}) collective-permute-start(f32[4,32,128]{2,1,0:T(8,128)S(1)} %get-tuple-element.39), channel_id=1, source_target_pairs={{4,8},{8,4},{12,16},{16,12},{20,24},{24,20},{5,9},{9,5},{13,17},{1... | collective-permute-start | bytes 196616 | tf_op jit(solution)/shard_map/ppermute | solution.py:269

commit v4 on v3

--- a/solution.py
+++ b/solution.py
@@ -12,7 +12,7 @@
 EXTENT = BLOCKS_DEV + 2 * HALO_BLOCKS
 RIM = 2 * HALO_BLOCKS
 TIKHONOV = 0.5
-CHUNKS = 8
+CHUNKS = 2
 MOMENT_ROWS = 8
 VMEM_LIMIT = 24 * 1024 * 1024
 
@@ -42,12 +42,23 @@
     )
 
 
-def emit_rims(place_ref, partial_ref, even_ref, odd_ref):
-    width = even_ref.shape[0]
-    top = EXTENT - width
-    is_even = lax.rem(place_ref[0], 2) == 0
-    even_ref[...] = partial_ref[pl.ds(jnp.where(is_even, top, 0), width)]
-    odd_ref[...] = partial_ref[pl.ds(jnp.where(is_even, 0, top), width)]
+def emit_rims(partial_ref, upper_ref, lower_ref):
+    width = upper_ref.shape[0]
+    upper_ref[...] = partial_ref[EXTENT - width :]
+    lower_ref[...] = partial_ref[:width]
+
+
+def add_rims(tiles, place_ref, target_ref, from_below_ref, from_above_ref):
+    width = from_below_ref.shape[0]
+    tile = place_ref[0]
+
+    @pl.when(tile > 0)
+    def _():
+        target_ref[:width] += from_below_ref[...]
+
+    @pl.when(tile < tiles - 1)
+    def _():
+        target_ref[target_ref.shape[0] - width :] += from_above_ref[...]
 
 
 def rhs_kernel(
@@ -58,8 +69,8 @@
     source_ref,
     kernels_ref,
     partial_ref,
-    even_ref,
-    odd_ref,
+    upper_ref,
+    lower_ref,
     narrow_ref,
     wide_ref,
     sems,
@@ -87,24 +98,25 @@
             data = jnp.where(group < live, wide_ref[:, group, :], 0.0).astype(jnp.bfloat16)
             spread = spread_of(data, kernels_ref[group].reshape(slots * spaxels, fibres))
             scatter(spread, place_ref, index_ref, group, partial_ref)
-    emit_rims(place_ref, partial_ref, even_ref, odd_ref)
+    emit_rims(partial_ref, upper_ref, lower_ref)
 
 
 def step_kernel(
+    tiles,
     power,
     final,
     place_ref,
     live_ref,
     index_ref,
     held_ref,
-    even_in_ref,
-    odd_in_ref,
+    from_below_ref,
+    from_above_ref,
     moments_in_ref,
     kernels_ref,
     vector_ref,
     partial_ref,
-    even_ref,
-    odd_ref,
+    upper_ref,
+    lower_ref,
     moments_ref,
     operand_ref,
     image_ref,
@@ -112,12 +124,9 @@
     groups, slots, spaxels, fibres = kernels_ref.shape
     waves = held_ref.shape[1]
     live = live_ref[0]
-    is_even = lax.rem(place_ref[0], 2) == 0
     first_block = place_ref[0] * BLOCKS_DEV - HALO_BLOCKS
-    top = EXTENT - RIM
     vector_ref[...] = held_ref[...]
-    vector_ref[pl.ds(jnp.where(is_even, top, 0), RIM)] += even_in_ref[...]
-    vector_ref[pl.ds(jnp.where(is_even, 0, top), RIM)] += odd_in_ref[...]
+    add_rims(tiles, place_ref, vector_ref, from_below_ref, from_above_ref)
     square = jnp.zeros(vector_ref.shape[1:], jnp.float32)
     for block in range(EXTENT):
         value = vector_ref[block]
@@ -139,7 +148,7 @@
         weights = kernels_ref[group].reshape(slots * spaxels, fibres)
         spread = halves_sum(spread_of(image_ref[group], weights))
         scatter(spread, place_ref, index_ref, group, partial_ref)
-    emit_rims(place_ref, partial_ref, even_ref, odd_ref)
+    emit_rims(partial_ref, upper_ref, lower_ref)
     for block in range(EXTENT):
         partial_ref[block] += TIKHONOV * vector_ref[block]
     square_row = jnp.sum(square, axis=0, keepdims=True)
@@ -187,14 +196,15 @@
 
 
 def final_kernel(
+    tiles,
     place_ref,
     moments_ref,
     first_ref,
     second_ref,
     third_ref,
     held_ref,
-    even_in_ref,
-    odd_in_ref,
+    from_below_ref,
+    from_above_ref,
     solution_ref,
     residual_ref,
     last_ref,
@@ -218,11 +228,8 @@
         power = power * unit
         if row < 3:
             answer_scaled.append(answer[row] * power)
-    is_even = lax.rem(place_ref[0], 2) == 0
     last_ref[...] = held_ref[pl.ds(HALO_BLOCKS, BLOCKS_DEV)]
-    low, high = 0, BLOCKS_DEV - HALO_BLOCKS
-    last_ref[pl.ds(jnp.where(is_even, high, low), HALO_BLOCKS)] += even_in_ref[...]
-    last_ref[pl.ds(jnp.where(is_even, low, high), HALO_BLOCKS)] += odd_in_ref[...]
+    add_rims(tiles, place_ref, last_ref, from_below_ref, from_above_ref)
     for block in range(BLOCKS_DEV):
         first = first_ref[HALO_BLOCKS + block]
         second = second_ref[HALO_BLOCKS + block]
@@ -260,16 +267,14 @@
     moment = jax.ShapeDtypeStruct((MOMENT_ROWS, spaxels), jnp.float32)
     moment_all = jax.ShapeDtypeStruct((devices, MOMENT_ROWS, spaxels), jnp.float32)
     params = pltpu.CompilerParams(vmem_limit_bytes=VMEM_LIMIT)
-    even_pairs = [(i, i ^ 1) for i in range(tiles) if (i ^ 1) < tiles]
-    odd_pairs = [
-        (i, j) for i in range(tiles) for j in [((i + 1) ^ 1) - 1] if 0 <= j < tiles
-    ]
-
-    def swap(even, odd):
-        return lax.ppermute(even, "tile", even_pairs), lax.ppermute(odd, "tile", odd_pairs)
+    upward = [(i, (i + 1) % tiles) for i in range(tiles)]
+    downward = [(j, i) for i, j in upward]
+
+    def swap(upper, lower):
+        return lax.ppermute(upper, "tile", upward), lax.ppermute(lower, "tile", downward)
 
     chunks = CHUNKS if groups % CHUNKS == 0 else 1
-    weights, held, even, odd = pl.pallas_call(
+    weights, held, upper, lower = pl.pallas_call(
         rhs_kernel,
         out_shape=(jax.ShapeDtypeStruct(weights.shape, weights.dtype), window, rim, rim),
         in_specs=smem(3) + [pl.BlockSpec(memory_space=pltpu.HBM)] * 2,
@@ -293,10 +298,10 @@
     vectors = []
     for power in range(3):
         final = power == 2
-        even, odd = swap(even, odd)
+        upper, lower = swap(upper, lower)
         out_rim = half_rim if final else rim
-        vector, held, even, odd, moments = pl.pallas_call(
-            functools.partial(step_kernel, power, final),
+        vector, held, upper, lower, moments = pl.pallas_call(
+            functools.partial(step_kernel, tiles, power, final),
             out_shape=(window, window, out_rim, out_rim, moment_all if final else moment),
             in_specs=smem(3) + vmem(5),
             out_specs=tuple(vmem(5)),
@@ -306,20 +311,20 @@
             ],
             compiler_params=params,
             name=f"step{power}",
-        )(place, live_count, index, held, even, odd, moments, weights)
+        )(place, live_count, index, held, upper, lower, moments, weights)
         vectors.append(vector)
-    even, odd = swap(even, odd)
+    upper, lower = swap(upper, lower)
     moments = lax.all_to_all(moments, ("tile", "wave"), 0, 0)
     out = jax.ShapeDtypeStruct((waves, BLOCKS_DEV, spaxels), jnp.float32)
     return pl.pallas_call(
-        final_kernel,
+        functools.partial(final_kernel, tiles),
         out_shape=(out, out),
         in_specs=smem(1) + vmem(7),
         out_specs=tuple(vmem(2)),
         scratch_shapes=[pltpu.VMEM((BLOCKS_DEV, waves, spaxels), jnp.float32)],
         compiler_params=params,
         name="combine",
-    )(place, moments, *vectors, held, even, odd)
+    )(place, moments, *vectors, held, upper, lower)
 
 
 def solution(mesh):

time: 59.3 us -> 60.2 us (1.015)
  waiting for transfers between devices: 15 us -> 17.6 us
  Pallas kernels: 16.4 us -> 15.4 us
    ppermute x8, waiting for transfers between devices: 11.9 us -> 17.6 us  [the longest x4 14.4 us: swap(): lax.ppermute(upper, 'tile', upward)]
    all_to_all x1, starting transfers between devices: 9.12 us -> 4.55 us  [shards(): moments = lax.all_to_all(moments, ('tile', 'wave'), 0, 0)]
    ppermute x8, starting transfers between devices: 16.3 us -> 20.4 us  [the longest x4 15.2 us: swap(): lax.ppermute(lower, 'tile', downward)]
    all_to_all x1, waiting for transfers between devices: 3.13 us -> 0.01 us  [shards(): moments = lax.all_to_all(moments, ('tile', 'wave'), 0, 0)]
    pallas_call x1, Pallas kernels: 5.13 us -> 3.93 us  [shards(): pl.pallas_call(rhs_kernel, out_shape=(jax.ShapeDtypeStruct(weights.shape,...]
  transfers between devices with their start and end apart: 9 -> 9, of which waited for: 5 -> 7; matrix products, arithmetic and copies ran while one was open for 0% -> 0% of each run, Pallas kernels for 0% -> 0%
where the time goes in v4:
time: 60.2 us; the launch traced here: 60 us
  starting transfers between devices  25 us (42%)
  waiting for transfers between devices  17.6 us (29%)
  Pallas kernels  15.4 us (26%)
  between operations  1.34 us (2%)
  local copies, waits for them, and re-layouts  0.68 us (1%)
    ppermute x4, starting transfers between devices, swap(): lax.ppermute(lower, 'tile', downward)  15.2 us
    ppermute x4, waiting for transfers between devices, swap(): lax.ppermute(upper, 'tile', upward)  14.4 us
    pallas_call x3, Pallas kernels, shards(): pl.pallas_call(functools.partial(step_kernel, tiles, power, final), out_s...  10.1 us
    ppermute x4, starting transfers between devices, swap(): lax.ppermute(upper, 'tile', upward)  5.22 us
    all_to_all x1, starting transfers between devices, shards(): moments = lax.all_to_all(moments, ('tile', 'wave'), 0, 0)  4.55 us
    pallas_call x1, Pallas kernels, shards(): pl.pallas_call(rhs_kernel, out_shape=(jax.ShapeDtypeStruct(weights.shape,...  3.93 us
    ppermute x4, waiting for transfers between devices, swap(): lax.ppermute(lower, 'tile', downward)  3.23 us
    pallas_call x1, Pallas kernels, shards(): pl.pallas_call(functools.partial(final_kernel, tiles), out_shape=(out, ou...  1.35 us
  transfers between devices with their start and end apart: 9, of which 7 were waited for; matrix products, arithmetic and copies ran while one was open for 0% of the time, Pallas kernels for 0%

profile of v4, /device:TPU:0, one launch (start us, length us, event | category | flops | bytes accessed | tf_op | source)
XLA Modules:
  0.0 60.0 jit_solution(5710830102850963897)
XLA Ops:
  1.3 0.0 copy-start
  1.3 0.7 %copy-done = s32[1,32,4]{1,2,0:T(4,128)S(1)} copy-done((s32[1,32,4]{1,2,0:T(4,128)S(1)}, s32[1,32,4]{1,2,0:T(4,128)}, u32[]{:S(2)}) %copy-start) | copy-done | bytes 536
  2.0 3.9 %rhs.1 = (bf16[32,4,128,128]{3,2,1,0:T(8,128)(2,1)S(1)}, f32[24,32,128]{2,1,0:T(8,128)S(1)}, f32[8,32,128]{2,1,0:T(8,128)S(1)}, f32[8,32,128]{2,1,0:T(8,128)S(1)}) custom-call(s32[1]{0:T(128)} %bitcast.place_ref, s32[1]{0:T(128)S(6)} %copy.6.live_ref, s32[4,32]{1,0:T(4,128)S(1)} %bitcast.5, bf16[32,32,128]{2,1,0:T(8,128)(2,1)} %data_ref.1, ...), custom_call_target="tpu_custom_call" | custom-call | tf_op jit(solution)/shard_map/rhs/pallas_call | solution.py:277
  5.9 3.0 %collective-permute-start = (f32[8,32,128]{2,1,0:T(8,128)S(1)}, f32[8,32,128]{2,1,0:T(8,128)S(1)}, u32[]{:S(2)}, u32[]{:S(2)}) collective-permute-start(f32[8,32,128]{2,1,0:T(8,128)S(1)} %get-tuple-element.22), channel_id=1, source_target_pairs={{0,4},{4,8},{8,12},{12,16},{16,20},{20,24},{24,28},{28,0},{1,5},{5... | collective-permute-start | bytes 393224 | tf_op jit(solution)/shard_map/ppermute | solution.py:274
  8.9 3.1 %collective-permute-start.1 = (f32[8,32,128]{2,1,0:T(8,128)S(1)}, f32[8,32,128]{2,1,0:T(8,128)S(1)}, u32[]{:S(2)}, u32[]{:S(2)}) collective-permute-start(f32[8,32,128]{2,1,0:T(8,128)S(1)} %get-tuple-element.23), channel_id=1, source_target_pairs={{4,0},{8,4},{12,8},{16,12},{20,16},{24,20},{28,24},{0,28},{5,1},{9... | collective-permute-start | bytes 393224 | tf_op jit(solution)/shard_map/ppermute | solution.py:274
  12.0 3.5 %collective-permute-done.from_below_ref = f32[8,32,128]{2,1,0:T(8,128)S(1)} collective-permute-done((f32[8,32,128]{2,1,0:T(8,128)S(1)}, f32[8,32,128]{2,1,0:T(8,128)S(1)}, u32[]{:S(2)}, u32[]{:S(2)}) %collective-permute-start) | collective-permute-done | bytes 131104 | tf_op jit(solution)/shard_map/ppermute | solution.py:274
  15.6 1.1 %collective-permute-done.1.from_above_ref = f32[8,32,128]{2,1,0:T(8,128)S(1)} collective-permute-done((f32[8,32,128]{2,1,0:T(8,128)S(1)}, f32[8,32,128]{2,1,0:T(8,128)S(1)}, u32[]{:S(2)}, u32[]{:S(2)}) %collective-permute-start.1) | collective-permute-done | bytes 131104 | tf_op jit(solution)/shard_map/ppermute | solution.py:274
  16.7 3.2 %step0.1 = (f32[24,32,128]{2,1,0:T(8,128)S(1)}, f32[24,32,128]{2,1,0:T(8,128)S(1)}, f32[8,32,128]{2,1,0:T(8,128)S(1)}, f32[8,32,128]{2,1,0:T(8,128)S(1)}, f32[8,128]{1,0:T(8,128)S(1)}) custom-call(s32[1]{0:T(128)} %bitcast.place_ref, s32[1]{0:T(128)S(6)} %copy.6.live_ref, s32[4,32]{1,0:T(4,128)S(1)} %bitcast.6, ...), custom_call_target="tpu_custom_call" | custom-call | tf_op jit(solution)/shard_map/step0/pallas_call | solution.py:303
  19.9 0.3 collective-permute-start.2
  20.2 4.4 %collective-permute-start.3 = (f32[8,32,128]{2,1,0:T(8,128)S(1)}, f32[8,32,128]{2,1,0:T(8,128)S(1)}, u32[]{:S(2)}, u32[]{:S(2)}) collective-permute-start(f32[8,32,128]{2,1,0:T(8,128)S(1)} %get-tuple-element.27), channel_id=1, source_target_pairs={{4,0},{8,4},{12,8},{16,12},{20,16},{24,20},{28,24},{0,28},{5,1},{9... | collective-permute-start | bytes 393224 | tf_op jit(solution)/shard_map/ppermute | solution.py:274
  24.7 3.0 %collective-permute-done.2.from_below_ref = f32[8,32,128]{2,1,0:T(8,128)S(1)} collective-permute-done((f32[8,32,128]{2,1,0:T(8,128)S(1)}, f32[8,32,128]{2,1,0:T(8,128)S(1)}, u32[]{:S(2)}, u32[]{:S(2)}) %collective-permute-start.2) | collective-permute-done | bytes 131104 | tf_op jit(solution)/shard_map/ppermute | solution.py:274
  27.7 1.2 %collective-permute-done.3.from_above_ref = f32[8,32,128]{2,1,0:T(8,128)S(1)} collective-permute-done((f32[8,32,128]{2,1,0:T(8,128)S(1)}, f32[8,32,128]{2,1,0:T(8,128)S(1)}, u32[]{:S(2)}, u32[]{:S(2)}) %collective-permute-start.3) | collective-permute-done | bytes 131104 | tf_op jit(solution)/shard_map/ppermute | solution.py:274
  28.9 3.2 %step1.1 = (f32[24,32,128]{2,1,0:T(8,128)S(1)}, f32[24,32,128]{2,1,0:T(8,128)S(1)}, f32[8,32,128]{2,1,0:T(8,128)S(1)}, f32[8,32,128]{2,1,0:T(8,128)S(1)}, f32[8,128]{1,0:T(8,128)S(1)}) custom-call(s32[1]{0:T(128)} %bitcast.place_ref, s32[1]{0:T(128)S(6)} %copy.6.live_ref, s32[4,32]{1,0:T(4,128)S(1)} %bitcast.7, ...), custom_call_target="tpu_custom_call" | custom-call | tf_op jit(solution)/shard_map/step1/pallas_call | solution.py:303
  32.1 0.1 collective-permute-start.4
  32.1 4.7 %collective-permute-start.5 = (f32[8,32,128]{2,1,0:T(8,128)S(1)}, f32[8,32,128]{2,1,0:T(8,128)S(1)}, u32[]{:S(2)}, u32[]{:S(2)}) collective-permute-start(f32[8,32,128]{2,1,0:T(8,128)S(1)} %get-tuple-element.31), channel_id=1, source_target_pairs={{4,0},{8,4},{12,8},{16,12},{20,16},{24,20},{28,24},{0,28},{5,1},{9... | collective-permute-start | bytes 393224 | tf_op jit(solution)/shard_map/ppermute | solution.py:274
  36.9 3.5 %collective-permute-done.4.from_below_ref = f32[8,32,128]{2,1,0:T(8,128)S(1)} collective-permute-done((f32[8,32,128]{2,1,0:T(8,128)S(1)}, f32[8,32,128]{2,1,0:T(8,128)S(1)}, u32[]{:S(2)}, u32[]{:S(2)}) %collective-permute-start.4) | collective-permute-done | bytes 131104 | tf_op jit(solution)/shard_map/ppermute | solution.py:274
  40.3 0.9 %collective-permute-done.5.from_above_ref = f32[8,32,128]{2,1,0:T(8,128)S(1)} collective-permute-done((f32[8,32,128]{2,1,0:T(8,128)S(1)}, f32[8,32,128]{2,1,0:T(8,128)S(1)}, u32[]{:S(2)}, u32[]{:S(2)}) %collective-permute-start.5) | collective-permute-done | bytes 131104 | tf_op jit(solution)/shard_map/ppermute | solution.py:274
  41.3 3.7 %step2.1 = (f32[24,32,128]{2,1,0:T(8,128)S(1)}, f32[24,32,128]{2,1,0:T(8,128)S(1)}, f32[4,32,128]{2,1,0:T(8,128)S(1)}, f32[4,32,128]{2,1,0:T(8,128)S(1)}, f32[32,8,128]{2,1,0:T(8,128)}) custom-call(s32[1]{0:T(128)} %bitcast.place_ref, s32[1]{0:T(128)S(6)} %copy.6.live_ref, s32[4,32]{1,0:T(4,128)S(1)} %bitcast.8, ...), custom_call_target="tpu_custom_call" | custom-call | tf_op jit(solution)/shard_map/step2/pallas_call | solution.py:303
  45.0 4.6 %all-to-all-start = ((f32[32,8,128]{2,1,0:T(8,128)}), f32[32,8,128]{2,1,0:T(8,128)S(1)}, u32[]{:S(2)}, u32[]{:S(2)}) async-start(f32[32,8,128]{2,1,0:T(8,128)} %get-tuple-element.33), calls=%async_computation | async-start | bytes 262144 | tf_op jit(solution)/shard_map/all_to_all | solution.py:317
  49.5 1.8 %collective-permute-start.6 = (f32[4,32,128]{2,1,0:T(8,128)S(1)}, f32[4,32,128]{2,1,0:T(8,128)S(1)}, u32[]{:S(2)}, u32[]{:S(2)}) collective-permute-start(f32[4,32,128]{2,1,0:T(8,128)S(1)} %get-tuple-element.38), channel_id=1, source_target_pairs={{0,4},{4,8},{8,12},{12,16},{16,20},{20,24},{24,28},{28,0},{1,5},{5... | collective-permute-start | bytes 196616 | tf_op jit(solution)/shard_map/ppermute | solution.py:274
  51.4 3.0 %collective-permute-start.7 = (f32[4,32,128]{2,1,0:T(8,128)S(1)}, f32[4,32,128]{2,1,0:T(8,128)S(1)}, u32[]{:S(2)}, u32[]{:S(2)}) collective-permute-start(f32[4,32,128]{2,1,0:T(8,128)S(1)} %get-tuple-element.39), channel_id=1, source_target_pairs={{4,0},{8,4},{12,8},{16,12},{20,16},{24,20},{28,24},{0,28},{5,1},{9... | collective-permute-start | bytes 196616 | tf_op jit(solution)/shard_map/ppermute | solution.py:274
  54.3 4.3 %collective-permute-done.6.from_below_ref = f32[4,32,128]{2,1,0:T(8,128)S(1)} collective-permute-done((f32[4,32,128]{2,1,0:T(8,128)S(1)}, f32[4,32,128]{2,1,0:T(8,128)S(1)}, u32[]{:S(2)}, u32[]{:S(2)}) %collective-permute-start.6) | collective-permute-done | bytes 65568 | tf_op jit(solution)/shard_map/ppermute | solution.py:274
  58.6 0.0 collective-permute-done.7.from_above_ref
  58.7 0.0 all-to-all-done.moments_ref
  58.7 1.4 %combine.1 = (f32[32,16,128]{2,1,0:T(8,128)}, f32[32,16,128]{2,1,0:T(8,128)}) custom-call(s32[1]{0:T(128)} %bitcast.place_ref, f32[32,8,128]{2,1,0:T(8,128)S(1)} %all-to-all-done.moments_ref, f32[24,32,128]{2,1,0:T(8,128)S(1)} %get-tuple-element.34.first_ref, f32[24,32,128]{2,1,0:T(8,128)S(1)} %get-tuple-element.35.second_ref, ...), custom_call_target="tpu_custom_call" | custom-call | tf_op jit(solution)/shard_map/combine/pallas_call | solution.py:319
  (1 shorter events, 0.0 us)
Async XLA Ops:
  1.3 0.7 %copy-start = (s32[1,32,4]{1,2,0:T(4,128)S(1)}, s32[1,32,4]{1,2,0:T(4,128)}, u32[]{:S(2)}) copy-start(s32[1,32,4]{1,2,0:T(4,128)} %param.6) | copy-start | bytes 1540
  5.9 9.7 %collective-permute-start = (f32[8,32,128]{2,1,0:T(8,128)S(1)}, f32[8,32,128]{2,1,0:T(8,128)S(1)}, u32[]{:S(2)}, u32[]{:S(2)}) collective-permute-start(f32[8,32,128]{2,1,0:T(8,128)S(1)} %get-tuple-element.22), channel_id=1, source_target_pairs={{0,4},{4,8},{8,12},{12,16},{16,20},{20,24},{24,28},{28,0},{1,5},{5... | collective-permute-start | bytes 393224 | tf_op jit(solution)/shard_map/ppermute | solution.py:274
  8.9 7.8 %collective-permute-start.1 = (f32[8,32,128]{2,1,0:T(8,128)S(1)}, f32[8,32,128]{2,1,0:T(8,128)S(1)}, u32[]{:S(2)}, u32[]{:S(2)}) collective-permute-start(f32[8,32,128]{2,1,0:T(8,128)S(1)} %get-tuple-element.23), channel_id=1, source_target_pairs={{4,0},{8,4},{12,8},{16,12},{20,16},{24,20},{28,24},{0,28},{5,1},{9... | collective-permute-start | bytes 393224 | tf_op jit(solution)/shard_map/ppermute | solution.py:274
  19.9 7.8 %collective-permute-start.2 = (f32[8,32,128]{2,1,0:T(8,128)S(1)}, f32[8,32,128]{2,1,0:T(8,128)S(1)}, u32[]{:S(2)}, u32[]{:S(2)}) collective-permute-start(f32[8,32,128]{2,1,0:T(8,128)S(1)} %get-tuple-element.26), channel_id=1, source_target_pairs={{0,4},{4,8},{8,12},{12,16},{16,20},{20,24},{24,28},{28,0},{1,5},{5... | collective-permute-start | bytes 393224 | tf_op jit(solution)/shard_map/ppermute | solution.py:274
  20.2 8.7 %collective-permute-start.3 = (f32[8,32,128]{2,1,0:T(8,128)S(1)}, f32[8,32,128]{2,1,0:T(8,128)S(1)}, u32[]{:S(2)}, u32[]{:S(2)}) collective-permute-start(f32[8,32,128]{2,1,0:T(8,128)S(1)} %get-tuple-element.27), channel_id=1, source_target_pairs={{4,0},{8,4},{12,8},{16,12},{20,16},{24,20},{28,24},{0,28},{5,1},{9... | collective-permute-start | bytes 393224 | tf_op jit(solution)/shard_map/ppermute | solution.py:274
  32.1 8.3 %collective-permute-start.4 = (f32[8,32,128]{2,1,0:T(8,128)S(1)}, f32[8,32,128]{2,1,0:T(8,128)S(1)}, u32[]{:S(2)}, u32[]{:S(2)}) collective-permute-start(f32[8,32,128]{2,1,0:T(8,128)S(1)} %get-tuple-element.30), channel_id=1, source_target_pairs={{0,4},{4,8},{8,12},{12,16},{16,20},{20,24},{24,28},{28,0},{1,5},{5... | collective-permute-start | bytes 393224 | tf_op jit(solution)/shard_map/ppermute | solution.py:274
  32.1 9.1 %collective-permute-start.5 = (f32[8,32,128]{2,1,0:T(8,128)S(1)}, f32[8,32,128]{2,1,0:T(8,128)S(1)}, u32[]{:S(2)}, u32[]{:S(2)}) collective-permute-start(f32[8,32,128]{2,1,0:T(8,128)S(1)} %get-tuple-element.31), channel_id=1, source_target_pairs={{4,0},{8,4},{12,8},{16,12},{20,16},{24,20},{28,24},{0,28},{5,1},{9... | collective-permute-start | bytes 393224 | tf_op jit(solution)/shard_map/ppermute | solution.py:274
  45.0 13.7 %all-to-all-start = ((f32[32,8,128]{2,1,0:T(8,128)}), f32[32,8,128]{2,1,0:T(8,128)S(1)}, u32[]{:S(2)}, u32[]{:S(2)}) async-start(f32[32,8,128]{2,1,0:T(8,128)} %get-tuple-element.33), calls=%async_computation | async-start | bytes 262144 | tf_op jit(solution)/shard_map/all_to_all | solution.py:317
  49.5 9.1 %collective-permute-start.6 = (f32[4,32,128]{2,1,0:T(8,128)S(1)}, f32[4,32,128]{2,1,0:T(8,128)S(1)}, u32[]{:S(2)}, u32[]{:S(2)}) collective-permute-start(f32[4,32,128]{2,1,0:T(8,128)S(1)} %get-tuple-element.38), channel_id=1, source_target_pairs={{0,4},{4,8},{8,12},{12,16},{16,20},{20,24},{24,28},{28,0},{1,5},{5... | collective-permute-start | bytes 196616 | tf_op jit(solution)/shard_map/ppermute | solution.py:274
  51.4 7.3 %collective-permute-start.7 = (f32[4,32,128]{2,1,0:T(8,128)S(1)}, f32[4,32,128]{2,1,0:T(8,128)S(1)}, u32[]{:S(2)}, u32[]{:S(2)}) collective-permute-start(f32[4,32,128]{2,1,0:T(8,128)S(1)} %get-tuple-element.39), channel_id=1, source_target_pairs={{4,0},{8,4},{12,8},{16,12},{20,16},{24,20},{28,24},{0,28},{5,1},{9... | collective-permute-start | bytes 196616 | tf_op jit(solution)/shard_map/ppermute | solution.py:274

commit v5 on v3

--- a/solution.py
+++ b/solution.py
@@ -12,7 +12,10 @@
 EXTENT = BLOCKS_DEV + 2 * HALO_BLOCKS
 RIM = 2 * HALO_BLOCKS
 TIKHONOV = 0.5
-CHUNKS = 8
+CHUNKS = 2
+SCALE_ROWS = 16
+CODE_PEAK = 32768.0
+CODE_FLOOR = 1e-33
 MOMENT_ROWS = 8
 VMEM_LIMIT = 24 * 1024 * 1024
 
@@ -42,12 +45,58 @@
     )
 
 
+def folded(value, rows, combine):
+    parts = [value[start : start + rows] for start in range(0, value.shape[0], rows)]
+    return functools.reduce(combine, parts)
+
+
+def repeated(value, rows):
+    return jnp.concatenate([value] * (rows // value.shape[0]), axis=0)
+
+
+def encode(partial_ref, start, rim_ref):
+    waves = partial_ref.shape[1]
+    width = (rim_ref.shape[0] - SCALE_ROWS) // waves
+    scales = rim_ref.at[width * waves :]
+    peak = None
+    for block in range(width):
+        size = folded(jnp.abs(partial_ref[start + block]), 8, jnp.maximum)
+        peak = size if peak is None else jnp.maximum(peak, size)
+    scales[...] = repeated(jnp.maximum(peak, CODE_FLOOR), SCALE_ROWS).astype(jnp.bfloat16)
+    gain = repeated(CODE_PEAK / scales[...].astype(jnp.float32), waves)
+    for block in range(width):
+        value = partial_ref[start + block] * gain
+        for _ in range(3):
+            value = value * jnp.abs(value)
+        rim_ref[block * waves : (block + 1) * waves] = value.astype(jnp.bfloat16)
+
+
+def decode_add(rim_ref, target_ref, start):
+    waves = target_ref.shape[1]
+    width = (rim_ref.shape[0] - SCALE_ROWS) // waves
+    scale = repeated(rim_ref[width * waves :].astype(jnp.float32) / CODE_PEAK, waves)
+    for block in range(width):
+        code = rim_ref[block * waves : (block + 1) * waves].astype(jnp.float32)
+        root = jnp.sqrt(jnp.sqrt(jnp.sqrt(jnp.abs(code))))
+        target_ref[start + block] += jnp.where(code < 0.0, -root, root) * scale
+
+
+def rim_starts(place_ref, extent, rim_ref, waves):
+    top = extent - (rim_ref.shape[0] - SCALE_ROWS) // waves
+    is_even = lax.rem(place_ref[0], 2) == 0
+    return jnp.where(is_even, top, 0), jnp.where(is_even, 0, top)
+
+
 def emit_rims(place_ref, partial_ref, even_ref, odd_ref):
-    width = even_ref.shape[0]
-    top = EXTENT - width
-    is_even = lax.rem(place_ref[0], 2) == 0
-    even_ref[...] = partial_ref[pl.ds(jnp.where(is_even, top, 0), width)]
-    odd_ref[...] = partial_ref[pl.ds(jnp.where(is_even, 0, top), width)]
+    even, odd = rim_starts(place_ref, partial_ref.shape[0], even_ref, partial_ref.shape[1])
+    encode(partial_ref, even, even_ref)
+    encode(partial_ref, odd, odd_ref)
+
+
+def add_rims(place_ref, target_ref, even_in_ref, odd_in_ref):
+    even, odd = rim_starts(place_ref, target_ref.shape[0], even_in_ref, target_ref.shape[1])
+    decode_add(even_in_ref, target_ref, even)
+    decode_add(odd_in_ref, target_ref, odd)
 
 
 def rhs_kernel(
@@ -112,12 +161,9 @@
     groups, slots, spaxels, fibres = kernels_ref.shape
     waves = held_ref.shape[1]
     live = live_ref[0]
-    is_even = lax.rem(place_ref[0], 2) == 0
     first_block = place_ref[0] * BLOCKS_DEV - HALO_BLOCKS
-    top = EXTENT - RIM
     vector_ref[...] = held_ref[...]
-    vector_ref[pl.ds(jnp.where(is_even, top, 0), RIM)] += even_in_ref[...]
-    vector_ref[pl.ds(jnp.where(is_even, 0, top), RIM)] += odd_in_ref[...]
+    add_rims(place_ref, vector_ref, even_in_ref, odd_in_ref)
     square = jnp.zeros(vector_ref.shape[1:], jnp.float32)
     for block in range(EXTENT):
         value = vector_ref[block]
@@ -218,11 +264,8 @@
         power = power * unit
         if row < 3:
             answer_scaled.append(answer[row] * power)
-    is_even = lax.rem(place_ref[0], 2) == 0
     last_ref[...] = held_ref[pl.ds(HALO_BLOCKS, BLOCKS_DEV)]
-    low, high = 0, BLOCKS_DEV - HALO_BLOCKS
-    last_ref[pl.ds(jnp.where(is_even, high, low), HALO_BLOCKS)] += even_in_ref[...]
-    last_ref[pl.ds(jnp.where(is_even, low, high), HALO_BLOCKS)] += odd_in_ref[...]
+    add_rims(place_ref, last_ref, even_in_ref, odd_in_ref)
     for block in range(BLOCKS_DEV):
         first = first_ref[HALO_BLOCKS + block]
         second = second_ref[HALO_BLOCKS + block]
@@ -255,8 +298,8 @@
     index = jnp.swapaxes(block_index, 1, 2).reshape(slots, groups)
     weights = kernels.reshape(groups, slots, spaxels, fibres)
     window = jax.ShapeDtypeStruct((EXTENT, waves, spaxels), jnp.float32)
-    rim = jax.ShapeDtypeStruct((RIM, waves, spaxels), jnp.float32)
-    half_rim = jax.ShapeDtypeStruct((HALO_BLOCKS, waves, spaxels), jnp.float32)
+    rim = jax.ShapeDtypeStruct((RIM * waves + SCALE_ROWS, spaxels), jnp.bfloat16)
+    half_rim = jax.ShapeDtypeStruct((HALO_BLOCKS * waves + SCALE_ROWS, spaxels), jnp.bfloat16)
     moment = jax.ShapeDtypeStruct((MOMENT_ROWS, spaxels), jnp.float32)
     moment_all = jax.ShapeDtypeStruct((devices, MOMENT_ROWS, spaxels), jnp.float32)
     params = pltpu.CompilerParams(vmem_limit_bytes=VMEM_LIMIT)

time: 59.3 us -> 57 us (0.961)
  waiting for transfers between devices: 15 us -> 10.9 us
  starting transfers between devices: 25.5 us -> 27.6 us
    ppermute x4, waiting for transfers between devices: 11.9 us -> 6.91 us  [swap(): lax.ppermute(even, 'tile', even_pairs)]
    ppermute x4, starting transfers between devices: 13.7 us -> 15.2 us  [swap(): lax.ppermute(even, 'tile', even_pairs)]
    pallas_call x1, Pallas kernels: 5.13 us -> 4.04 us  [shards(): pl.pallas_call(rhs_kernel, out_shape=(jax.ShapeDtypeStruct(weights.shape,...]
    all_to_all x1, waiting for transfers between devices: 3.13 us -> 4 us  [shards(): moments = lax.all_to_all(moments, ('tile', 'wave'), 0, 0)]
    pallas_call x3, Pallas kernels: 9.94 us -> 10.7 us  [shards(): pl.pallas_call(functools.partial(step_kernel, power, final), out_shape=(w...]
    all_to_all x1, starting transfers between devices: 9.12 us -> 9.76 us  [shards(): moments = lax.all_to_all(moments, ('tile', 'wave'), 0, 0)]
where the time goes in v5:
time: 57 us; the launch traced here: 56.7 us
  starting transfers between devices  27.6 us (48%)
  Pallas kernels  16.1 us (28%)
  waiting for transfers between devices  10.9 us (19%)
  between operations  1.38 us (2%)
  local copies, waits for them, and re-layouts  0.68 us (1%)
    ppermute x4, starting transfers between devices, swap(): lax.ppermute(even, 'tile', even_pairs)  15.2 us
    pallas_call x3, Pallas kernels, shards(): pl.pallas_call(functools.partial(step_kernel, power, final), out_shape=(w...  10.7 us
    all_to_all x1, starting transfers between devices, shards(): moments = lax.all_to_all(moments, ('tile', 'wave'), 0, 0)  9.76 us
    ppermute x4, waiting for transfers between devices, swap(): lax.ppermute(even, 'tile', even_pairs)  6.91 us
    pallas_call x1, Pallas kernels, shards(): pl.pallas_call(rhs_kernel, out_shape=(jax.ShapeDtypeStruct(weights.shape,...  4.04 us
    all_to_all x1, waiting for transfers between devices, shards(): moments = lax.all_to_all(moments, ('tile', 'wave'), 0, 0)  4 us
    ppermute x4, starting transfers between devices, swap(): lax.ppermute(odd, 'tile', odd_pairs)  2.61 us
    pallas_call x1, Pallas kernels, shards(): pl.pallas_call(final_kernel, out_shape=(out, out), in_specs=smem(1) + vme...  1.4 us
  transfers between devices with their start and end apart: 9, of which 5 were waited for; matrix products, arithmetic and copies ran while one was open for 0% of the time, Pallas kernels for 0%

profile of v5, /device:TPU:0, one launch (start us, length us, event | category | flops | bytes accessed | tf_op | source)
XLA Modules:
  0.0 56.7 jit_solution(6395603406209439819)
XLA Ops:
  0.6 0.0 copy-start.1
  1.3 0.0 copy-start
  1.3 0.7 %copy-done = s32[1,32,4]{1,2,0:T(4,128)S(1)} copy-done((s32[1,32,4]{1,2,0:T(4,128)S(1)}, s32[1,32,4]{1,2,0:T(4,128)}, u32[]{:S(2)}) %copy-start) | copy-done | bytes 536
  2.0 4.0 %rhs.1 = (bf16[32,4,128,128]{3,2,1,0:T(8,128)(2,1)S(1)}, f32[24,32,128]{2,1,0:T(8,128)S(1)}, bf16[272,128]{1,0:T(8,128)(2,1)S(1)}, bf16[272,128]{1,0:T(8,128)(2,1)S(1)}) custom-call(s32[1]{0:T(128)} %bitcast.place_ref, s32[1]{0:T(128)S(6)} %copy.6.live_ref, s32[4,32]{1,0:T(4,128)S(1)} %bitcast.5, bf16[32,32,128]{2,1,0:T(8,128)(2,1)} %data_ref.1, ...), custom_call_target="tpu_custom_call" | custom-call | tf_op jit(solution)/shard_map/rhs/pallas_call | solution.py:315
  6.0 3.0 %collective-permute-start = (bf16[272,128]{1,0:T(8,128)(2,1)S(1)}, bf16[272,128]{1,0:T(8,128)(2,1)S(1)}, u32[]{:S(2)}, u32[]{:S(2)}) collective-permute-start(bf16[272,128]{1,0:T(8,128)(2,1)S(1)} %get-tuple-element.22), channel_id=1, source_target_pairs={{0,4},{4,0},{8,12},{12,8},{16,20},{20,16},{24,28},{28,24},{1,5},{5... | collective-permute-start | bytes 208904 | tf_op jit(solution)/shard_map/ppermute | solution.py:312
  9.0 0.7 %collective-permute-start.1 = (bf16[272,128]{1,0:T(8,128)(2,1)S(1)}, bf16[272,128]{1,0:T(8,128)(2,1)S(1)}, u32[]{:S(2)}, u32[]{:S(2)}) collective-permute-start(bf16[272,128]{1,0:T(8,128)(2,1)S(1)} %get-tuple-element.23), channel_id=1, source_target_pairs={{4,8},{8,4},{12,16},{16,12},{20,24},{24,20},{5,9},{9,5},{13,17},{1... | collective-permute-start | bytes 208904 | tf_op jit(solution)/shard_map/ppermute | solution.py:312
  9.7 1.6 %collective-permute-done.even_in_ref = bf16[272,128]{1,0:T(8,128)(2,1)S(1)} collective-permute-done((bf16[272,128]{1,0:T(8,128)(2,1)S(1)}, bf16[272,128]{1,0:T(8,128)(2,1)S(1)}, u32[]{:S(2)}, u32[]{:S(2)}) %collective-permute-start) | collective-permute-done | bytes 69664 | tf_op jit(solution)/shard_map/ppermute | solution.py:312
  11.3 0.0 collective-permute-done.1.odd_in_ref
  11.3 0.0 copy-done.1
  11.3 3.4 %step0.1 = (f32[24,32,128]{2,1,0:T(8,128)S(1)}, f32[24,32,128]{2,1,0:T(8,128)S(1)}, bf16[272,128]{1,0:T(8,128)(2,1)S(1)}, bf16[272,128]{1,0:T(8,128)(2,1)S(1)}, f32[8,128]{1,0:T(8,128)S(1)}) custom-call(s32[1]{0:T(128)} %bitcast.place_ref, s32[1]{0:T(128)S(6)} %copy.6.live_ref, s32[4,32]{1,0:T(4,128)S(1)} %bitcast.6, ...), custom_call_target="tpu_custom_call" | custom-call | tf_op jit(solution)/shard_map/step0/pallas_call | solution.py:341
  14.8 5.0 %collective-permute-start.2 = (bf16[272,128]{1,0:T(8,128)(2,1)S(1)}, bf16[272,128]{1,0:T(8,128)(2,1)S(1)}, u32[]{:S(2)}, u32[]{:S(2)}) collective-permute-start(bf16[272,128]{1,0:T(8,128)(2,1)S(1)} %get-tuple-element.26), channel_id=1, source_target_pairs={{0,4},{4,0},{8,12},{12,8},{16,20},{20,16},{24,28},{28,24},{1,5},{5... | collective-permute-start | bytes 208904 | tf_op jit(solution)/shard_map/ppermute | solution.py:312
  19.8 0.7 %collective-permute-start.3 = (bf16[272,128]{1,0:T(8,128)(2,1)S(1)}, bf16[272,128]{1,0:T(8,128)(2,1)S(1)}, u32[]{:S(2)}, u32[]{:S(2)}) collective-permute-start(bf16[272,128]{1,0:T(8,128)(2,1)S(1)} %get-tuple-element.27), channel_id=1, source_target_pairs={{4,8},{8,4},{12,16},{16,12},{20,24},{24,20},{5,9},{9,5},{13,17},{1... | collective-permute-start | bytes 208904 | tf_op jit(solution)/shard_map/ppermute | solution.py:312
  20.4 1.6 %collective-permute-done.2.even_in_ref = bf16[272,128]{1,0:T(8,128)(2,1)S(1)} collective-permute-done((bf16[272,128]{1,0:T(8,128)(2,1)S(1)}, bf16[272,128]{1,0:T(8,128)(2,1)S(1)}, u32[]{:S(2)}, u32[]{:S(2)}) %collective-permute-start.2) | collective-permute-done | bytes 69664 | tf_op jit(solution)/shard_map/ppermute | solution.py:312
  22.1 0.0 collective-permute-done.3.odd_in_ref
  22.1 3.4 %step1.1 = (f32[24,32,128]{2,1,0:T(8,128)S(1)}, f32[24,32,128]{2,1,0:T(8,128)S(1)}, bf16[272,128]{1,0:T(8,128)(2,1)S(1)}, bf16[272,128]{1,0:T(8,128)(2,1)S(1)}, f32[8,128]{1,0:T(8,128)S(1)}) custom-call(s32[1]{0:T(128)} %bitcast.place_ref, s32[1]{0:T(128)S(6)} %copy.6.live_ref, s32[4,32]{1,0:T(4,128)S(1)} %bitcast.7, ...), custom_call_target="tpu_custom_call" | custom-call | tf_op jit(solution)/shard_map/step1/pallas_call | solution.py:341
  25.5 5.4 %collective-permute-start.4 = (bf16[272,128]{1,0:T(8,128)(2,1)S(1)}, bf16[272,128]{1,0:T(8,128)(2,1)S(1)}, u32[]{:S(2)}, u32[]{:S(2)}) collective-permute-start(bf16[272,128]{1,0:T(8,128)(2,1)S(1)} %get-tuple-element.30), channel_id=1, source_target_pairs={{0,4},{4,0},{8,12},{12,8},{16,20},{20,16},{24,28},{28,24},{1,5},{5... | collective-permute-start | bytes 208904 | tf_op jit(solution)/shard_map/ppermute | solution.py:312
  30.9 0.7 %collective-permute-start.5 = (bf16[272,128]{1,0:T(8,128)(2,1)S(1)}, bf16[272,128]{1,0:T(8,128)(2,1)S(1)}, u32[]{:S(2)}, u32[]{:S(2)}) collective-permute-start(bf16[272,128]{1,0:T(8,128)(2,1)S(1)} %get-tuple-element.31), channel_id=1, source_target_pairs={{4,8},{8,4},{12,16},{16,12},{20,24},{24,20},{5,9},{9,5},{13,17},{1... | collective-permute-start | bytes 208904 | tf_op jit(solution)/shard_map/ppermute | solution.py:312
  31.5 1.9 %collective-permute-done.4.even_in_ref = bf16[272,128]{1,0:T(8,128)(2,1)S(1)} collective-permute-done((bf16[272,128]{1,0:T(8,128)(2,1)S(1)}, bf16[272,128]{1,0:T(8,128)(2,1)S(1)}, u32[]{:S(2)}, u32[]{:S(2)}) %collective-permute-start.4) | collective-permute-done | bytes 69664 | tf_op jit(solution)/shard_map/ppermute | solution.py:312
  33.5 0.0 collective-permute-done.5.odd_in_ref
  33.5 3.8 %step2.1 = (f32[24,32,128]{2,1,0:T(8,128)S(1)}, f32[24,32,128]{2,1,0:T(8,128)S(1)}, bf16[144,128]{1,0:T(8,128)(2,1)S(1)}, bf16[144,128]{1,0:T(8,128)(2,1)S(1)}, f32[32,8,128]{2,1,0:T(8,128)}) custom-call(s32[1]{0:T(128)} %bitcast.place_ref, s32[1]{0:T(128)S(6)} %copy.6.live_ref, s32[4,32]{1,0:T(4,128)S(1)} %bitcast.8, ...), custom_call_target="tpu_custom_call" | custom-call | tf_op jit(solution)/shard_map/step2/pallas_call | solution.py:341
  37.3 9.8 %all-to-all-start = ((f32[32,8,128]{2,1,0:T(8,128)}), f32[32,8,128]{2,1,0:T(8,128)S(1)}, u32[]{:S(2)}, u32[]{:S(2)}) async-start(f32[32,8,128]{2,1,0:T(8,128)} %get-tuple-element.33), calls=%async_computation | async-start | bytes 262144 | tf_op jit(solution)/shard_map/all_to_all | solution.py:355
  47.1 1.8 %collective-permute-start.6 = (bf16[144,128]{1,0:T(8,128)(2,1)S(1)}, bf16[144,128]{1,0:T(8,128)(2,1)S(1)}, u32[]{:S(2)}, u32[]{:S(2)}) collective-permute-start(bf16[144,128]{1,0:T(8,128)(2,1)S(1)} %get-tuple-element.38), channel_id=1, source_target_pairs={{0,4},{4,0},{8,12},{12,8},{16,20},{20,16},{24,28},{28,24},{1,5},{5... | collective-permute-start | bytes 110600 | tf_op jit(solution)/shard_map/ppermute | solution.py:312
  48.9 0.7 %collective-permute-start.7 = (bf16[144,128]{1,0:T(8,128)(2,1)S(1)}, bf16[144,128]{1,0:T(8,128)(2,1)S(1)}, u32[]{:S(2)}, u32[]{:S(2)}) collective-permute-start(bf16[144,128]{1,0:T(8,128)(2,1)S(1)} %get-tuple-element.39), channel_id=1, source_target_pairs={{4,8},{8,4},{12,16},{16,12},{20,24},{24,20},{5,9},{9,5},{13,17},{1... | collective-permute-start | bytes 110600 | tf_op jit(solution)/shard_map/ppermute | solution.py:312
  49.6 1.7 %collective-permute-done.6.even_in_ref = bf16[144,128]{1,0:T(8,128)(2,1)S(1)} collective-permute-done((bf16[144,128]{1,0:T(8,128)(2,1)S(1)}, bf16[144,128]{1,0:T(8,128)(2,1)S(1)}, u32[]{:S(2)}, u32[]{:S(2)}) %collective-permute-start.6) | collective-permute-done | bytes 36896 | tf_op jit(solution)/shard_map/ppermute | solution.py:312
  51.3 0.0 collective-permute-done.7.odd_in_ref
  51.3 4.0 %all-to-all-done.moments_ref = f32[32,8,128]{2,1,0:T(8,128)S(1)} async-done(((f32[32,8,128]{2,1,0:T(8,128)}), f32[32,8,128]{2,1,0:T(8,128)S(1)}, u32[]{:S(2)}, u32[]{:S(2)}) %all-to-all-start) | async-done | bytes 131104 | tf_op jit(solution)/shard_map/all_to_all | solution.py:355
  55.3 1.4 %combine.1 = (f32[32,16,128]{2,1,0:T(8,128)}, f32[32,16,128]{2,1,0:T(8,128)}) custom-call(s32[1]{0:T(128)} %bitcast.place_ref, f32[32,8,128]{2,1,0:T(8,128)S(1)} %all-to-all-done.moments_ref, f32[24,32,128]{2,1,0:T(8,128)S(1)} %get-tuple-element.34.first_ref, f32[24,32,128]{2,1,0:T(8,128)S(1)} %get-tuple-element.35.second_ref, ...), custom_call_target="tpu_custom_call" | custom-call | tf_op jit(solution)/shard_map/combine/pallas_call | solution.py:357
  (1 shorter events, 0.0 us)
Async XLA Ops:
  0.6 10.7 %copy-start.1 = (s32[1,32,4]{1,2,0:T(4,128)S(1)}, s32[1,32,4]{1,2,0:T(4,128)}, u32[]{:S(2)}) copy-start(s32[1,32,4]{1,2,0:T(4,128)} %param.6) | copy-start | bytes 1540
  1.3 0.7 %copy-start = (s32[1,32,4]{1,2,0:T(4,128)S(1)}, s32[1,32,4]{1,2,0:T(4,128)}, u32[]{:S(2)}) copy-start(s32[1,32,4]{1,2,0:T(4,128)} %param.6) | copy-start | bytes 1540
  6.0 5.3 %collective-permute-start = (bf16[272,128]{1,0:T(8,128)(2,1)S(1)}, bf16[272,128]{1,0:T(8,128)(2,1)S(1)}, u32[]{:S(2)}, u32[]{:S(2)}) collective-permute-start(bf16[272,128]{1,0:T(8,128)(2,1)S(1)} %get-tuple-element.22), channel_id=1, source_target_pairs={{0,4},{4,0},{8,12},{12,8},{16,20},{20,16},{24,28},{28,24},{1,5},{5... | collective-permute-start | bytes 208904 | tf_op jit(solution)/shard_map/ppermute | solution.py:312
  9.0 2.3 %collective-permute-start.1 = (bf16[272,128]{1,0:T(8,128)(2,1)S(1)}, bf16[272,128]{1,0:T(8,128)(2,1)S(1)}, u32[]{:S(2)}, u32[]{:S(2)}) collective-permute-start(bf16[272,128]{1,0:T(8,128)(2,1)S(1)} %get-tuple-element.23), channel_id=1, source_target_pairs={{4,8},{8,4},{12,16},{16,12},{20,24},{24,20},{5,9},{9,5},{13,17},{1... | collective-permute-start | bytes 208904 | tf_op jit(solution)/shard_map/ppermute | solution.py:312
  14.8 7.3 %collective-permute-start.2 = (bf16[272,128]{1,0:T(8,128)(2,1)S(1)}, bf16[272,128]{1,0:T(8,128)(2,1)S(1)}, u32[]{:S(2)}, u32[]{:S(2)}) collective-permute-start(bf16[272,128]{1,0:T(8,128)(2,1)S(1)} %get-tuple-element.26), channel_id=1, source_target_pairs={{0,4},{4,0},{8,12},{12,8},{16,20},{20,16},{24,28},{28,24},{1,5},{5... | collective-permute-start | bytes 208904 | tf_op jit(solution)/shard_map/ppermute | solution.py:312
  19.8 2.3 %collective-permute-start.3 = (bf16[272,128]{1,0:T(8,128)(2,1)S(1)}, bf16[272,128]{1,0:T(8,128)(2,1)S(1)}, u32[]{:S(2)}, u32[]{:S(2)}) collective-permute-start(bf16[272,128]{1,0:T(8,128)(2,1)S(1)} %get-tuple-element.27), channel_id=1, source_target_pairs={{4,8},{8,4},{12,16},{16,12},{20,24},{24,20},{5,9},{9,5},{13,17},{1... | collective-permute-start | bytes 208904 | tf_op jit(solution)/shard_map/ppermute | solution.py:312
  25.5 8.0 %collective-permute-start.4 = (bf16[272,128]{1,0:T(8,128)(2,1)S(1)}, bf16[272,128]{1,0:T(8,128)(2,1)S(1)}, u32[]{:S(2)}, u32[]{:S(2)}) collective-permute-start(bf16[272,128]{1,0:T(8,128)(2,1)S(1)} %get-tuple-element.30), channel_id=1, source_target_pairs={{0,4},{4,0},{8,12},{12,8},{16,20},{20,16},{24,28},{28,24},{1,5},{5... | collective-permute-start | bytes 208904 | tf_op jit(solution)/shard_map/ppermute | solution.py:312
  30.9 2.6 %collective-permute-start.5 = (bf16[272,128]{1,0:T(8,128)(2,1)S(1)}, bf16[272,128]{1,0:T(8,128)(2,1)S(1)}, u32[]{:S(2)}, u32[]{:S(2)}) collective-permute-start(bf16[272,128]{1,0:T(8,128)(2,1)S(1)} %get-tuple-element.31), channel_id=1, source_target_pairs={{4,8},{8,4},{12,16},{16,12},{20,24},{24,20},{5,9},{9,5},{13,17},{1... | collective-permute-start | bytes 208904 | tf_op jit(solution)/shard_map/ppermute | solution.py:312
  37.3 18.0 %all-to-all-start = ((f32[32,8,128]{2,1,0:T(8,128)}), f32[32,8,128]{2,1,0:T(8,128)S(1)}, u32[]{:S(2)}, u32[]{:S(2)}) async-start(f32[32,8,128]{2,1,0:T(8,128)} %get-tuple-element.33), calls=%async_computation | async-start | bytes 262144 | tf_op jit(solution)/shard_map/all_to_all | solution.py:355
  47.1 4.2 %collective-permute-start.6 = (bf16[144,128]{1,0:T(8,128)(2,1)S(1)}, bf16[144,128]{1,0:T(8,128)(2,1)S(1)}, u32[]{:S(2)}, u32[]{:S(2)}) collective-permute-start(bf16[144,128]{1,0:T(8,128)(2,1)S(1)} %get-tuple-element.38), channel_id=1, source_target_pairs={{0,4},{4,0},{8,12},{12,8},{16,20},{20,16},{24,28},{28,24},{1,5},{5... | collective-permute-start | bytes 110600 | tf_op jit(solution)/shard_map/ppermute | solution.py:312
  48.9 2.4 %collective-permute-start.7 = (bf16[144,128]{1,0:T(8,128)(2,1)S(1)}, bf16[144,128]{1,0:T(8,128)(2,1)S(1)}, u32[]{:S(2)}, u32[]{:S(2)}) collective-permute-start(bf16[144,128]{1,0:T(8,128)(2,1)S(1)} %get-tuple-element.39), channel_id=1, source_target_pairs={{4,8},{8,4},{12,16},{16,12},{20,24},{24,20},{5,9},{9,5},{13,17},{1... | collective-permute-start | bytes 110600 | tf_op jit(solution)/shard_map/ppermute | solution.py:312

commit v6 on v5

--- a/solution.py
+++ b/solution.py
@@ -107,8 +107,8 @@
     source_ref,
     kernels_ref,
     partial_ref,
+    odd_ref,
     even_ref,
-    odd_ref,
     narrow_ref,
     wide_ref,
     sems,
@@ -146,14 +146,14 @@
     live_ref,
     index_ref,
     held_ref,
+    odd_in_ref,
     even_in_ref,
-    odd_in_ref,
     moments_in_ref,
     kernels_ref,
     vector_ref,
     partial_ref,
+    odd_ref,
     even_ref,
-    odd_ref,
     moments_ref,
     operand_ref,
     image_ref,
@@ -239,8 +239,8 @@
     second_ref,
     third_ref,
     held_ref,
+    odd_in_ref,
     even_in_ref,
-    odd_in_ref,
     solution_ref,
     residual_ref,
     last_ref,
@@ -308,11 +308,11 @@
         (i, j) for i in range(tiles) for j in [((i + 1) ^ 1) - 1] if 0 <= j < tiles
     ]
 
-    def swap(even, odd):
-        return lax.ppermute(even, "tile", even_pairs), lax.ppermute(odd, "tile", odd_pairs)
+    def swap(odd, even):
+        return lax.ppermute(odd, "tile", odd_pairs), lax.ppermute(even, "tile", even_pairs)
 
     chunks = CHUNKS if groups % CHUNKS == 0 else 1
-    weights, held, even, odd = pl.pallas_call(
+    weights, held, odd, even = pl.pallas_call(
         rhs_kernel,
         out_shape=(jax.ShapeDtypeStruct(weights.shape, weights.dtype), window, rim, rim),
         in_specs=smem(3) + [pl.BlockSpec(memory_space=pltpu.HBM)] * 2,
@@ -336,9 +336,9 @@
     vectors = []
     for power in range(3):
         final = power == 2
-        even, odd = swap(even, odd)
+        odd, even = swap(odd, even)
         out_rim = half_rim if final else rim
-        vector, held, even, odd, moments = pl.pallas_call(
+        vector, held, odd, even, moments = pl.pallas_call(
             functools.partial(step_kernel, power, final),
             out_shape=(window, window, out_rim, out_rim, moment_all if final else moment),
             in_specs=smem(3) + vmem(5),
@@ -349,9 +349,9 @@
             ],
             compiler_params=params,
             name=f"step{power}",
-        )(place, live_count, index, held, even, odd, moments, weights)
+        )(place, live_count, index, held, odd, even, moments, weights)
         vectors.append(vector)
-    even, odd = swap(even, odd)
+    odd, even = swap(odd, even)
     moments = lax.all_to_all(moments, ("tile", "wave"), 0, 0)
     out = jax.ShapeDtypeStruct((waves, BLOCKS_DEV, spaxels), jnp.float32)
     return pl.pallas_call(
@@ -362,7 +362,7 @@
         scratch_shapes=[pltpu.VMEM((BLOCKS_DEV, waves, spaxels), jnp.float32)],
         compiler_params=params,
         name="combine",
-    )(place, moments, *vectors, held, even, odd)
+    )(place, moments, *vectors, held, odd, even)
 
 
 def solution(mesh):

time: 57 us -> 57.2 us (level)
  starting transfers between devices: 27.6 us -> 28.9 us
  waiting for transfers between devices: 10.9 us -> 9.85 us
    ppermute x4, starting transfers between devices: 15.2 us -> 20.7 us  [swap(): lax.ppermute(even, 'tile', even_pairs)]
    all_to_all x1, starting transfers between devices: 9.76 us -> 5.5 us  [shards(): moments = lax.all_to_all(moments, ('tile', 'wave'), 0, 0)]
    all_to_all x1, waiting for transfers between devices: 4 us -> 0.92 us  [shards(): moments = lax.all_to_all(moments, ('tile', 'wave'), 0, 0)]
    ppermute x4, waiting for transfers between devices: 6.91 us -> 8.92 us  [swap(): lax.ppermute(even, 'tile', even_pairs)]
where the time goes in v6:
time: 57.2 us; the launch traced here: 56.9 us
  starting transfers between devices  28.9 us (51%)
  Pallas kernels  16.1 us (28%)
  waiting for transfers between devices  9.85 us (17%)
  between operations  1.38 us (2%)
  local copies, waits for them, and re-layouts  0.68 us (1%)
    ppermute x4, starting transfers between devices, swap(): lax.ppermute(even, 'tile', even_pairs)  20.7 us
    pallas_call x3, Pallas kernels, shards(): pl.pallas_call(functools.partial(step_kernel, power, final), out_shape=(w...  10.7 us
    ppermute x4, waiting for transfers between devices, swap(): lax.ppermute(even, 'tile', even_pairs)  8.92 us
    all_to_all x1, starting transfers between devices, shards(): moments = lax.all_to_all(moments, ('tile', 'wave'), 0, 0)  5.5 us
    pallas_call x1, Pallas kernels, shards(): pl.pallas_call(rhs_kernel, out_shape=(jax.ShapeDtypeStruct(weights.shape,...  4.03 us
    ppermute x4, starting transfers between devices, swap(): lax.ppermute(odd, 'tile', odd_pairs)  2.66 us
    pallas_call x1, Pallas kernels, shards(): pl.pallas_call(final_kernel, out_shape=(out, out), in_specs=smem(1) + vme...  1.4 us
  transfers between devices with their start and end apart: 9, of which 5 were waited for; matrix products, arithmetic and copies ran while one was open for 0% of the time, Pallas kernels for 0%

profile of v6, /device:TPU:0, one launch (start us, length us, event | category | flops | bytes accessed | tf_op | source)
XLA Modules:
  0.0 56.9 jit_solution(16164189690602103490)
XLA Ops:
  0.6 0.0 copy-start.1
  1.3 0.0 copy-start
  1.3 0.7 %copy-done = s32[1,32,4]{1,2,0:T(4,128)S(1)} copy-done((s32[1,32,4]{1,2,0:T(4,128)S(1)}, s32[1,32,4]{1,2,0:T(4,128)}, u32[]{:S(2)}) %copy-start) | copy-done | bytes 536
  2.0 4.0 %rhs.1 = (bf16[32,4,128,128]{3,2,1,0:T(8,128)(2,1)S(1)}, f32[24,32,128]{2,1,0:T(8,128)S(1)}, bf16[272,128]{1,0:T(8,128)(2,1)S(1)}, bf16[272,128]{1,0:T(8,128)(2,1)S(1)}) custom-call(s32[1]{0:T(128)} %bitcast.place_ref, s32[1]{0:T(128)S(6)} %copy.6.live_ref, s32[4,32]{1,0:T(4,128)S(1)} %bitcast.5, bf16[32,32,128]{2,1,0:T(8,128)(2,1)} %data_ref.1, ...), custom_call_target="tpu_custom_call" | custom-call | tf_op jit(solution)/shard_map/rhs/pallas_call | solution.py:315
  6.0 0.7 %collective-permute-start = (bf16[272,128]{1,0:T(8,128)(2,1)S(1)}, bf16[272,128]{1,0:T(8,128)(2,1)S(1)}, u32[]{:S(2)}, u32[]{:S(2)}) collective-permute-start(bf16[272,128]{1,0:T(8,128)(2,1)S(1)} %get-tuple-element.22), channel_id=1, source_target_pairs={{4,8},{8,4},{12,16},{16,12},{20,24},{24,20},{5,9},{9,5},{13,17},{1... | collective-permute-start | bytes 208904 | tf_op jit(solution)/shard_map/ppermute | solution.py:312
  6.7 5.8 %collective-permute-start.1 = (bf16[272,128]{1,0:T(8,128)(2,1)S(1)}, bf16[272,128]{1,0:T(8,128)(2,1)S(1)}, u32[]{:S(2)}, u32[]{:S(2)}) collective-permute-start(bf16[272,128]{1,0:T(8,128)(2,1)S(1)} %get-tuple-element.23), channel_id=1, source_target_pairs={{0,4},{4,0},{8,12},{12,8},{16,20},{20,16},{24,28},{28,24},{1,5},{5... | collective-permute-start | bytes 208904 | tf_op jit(solution)/shard_map/ppermute | solution.py:312
  12.5 0.0 collective-permute-done.odd_in_ref
  12.5 2.3 %collective-permute-done.1.even_in_ref = bf16[272,128]{1,0:T(8,128)(2,1)S(1)} collective-permute-done((bf16[272,128]{1,0:T(8,128)(2,1)S(1)}, bf16[272,128]{1,0:T(8,128)(2,1)S(1)}, u32[]{:S(2)}, u32[]{:S(2)}) %collective-permute-start.1) | collective-permute-done | bytes 69664 | tf_op jit(solution)/shard_map/ppermute | solution.py:312
  14.8 0.0 copy-done.1
  14.8 3.4 %step0.1 = (f32[24,32,128]{2,1,0:T(8,128)S(1)}, f32[24,32,128]{2,1,0:T(8,128)S(1)}, bf16[272,128]{1,0:T(8,128)(2,1)S(1)}, bf16[272,128]{1,0:T(8,128)(2,1)S(1)}, f32[8,128]{1,0:T(8,128)S(1)}) custom-call(s32[1]{0:T(128)} %bitcast.place_ref, s32[1]{0:T(128)S(6)} %copy.6.live_ref, s32[4,32]{1,0:T(4,128)S(1)} %bitcast.6, ...), custom_call_target="tpu_custom_call" | custom-call | tf_op jit(solution)/shard_map/step0/pallas_call | solution.py:341
  18.2 0.7 %collective-permute-start.2 = (bf16[272,128]{1,0:T(8,128)(2,1)S(1)}, bf16[272,128]{1,0:T(8,128)(2,1)S(1)}, u32[]{:S(2)}, u32[]{:S(2)}) collective-permute-start(bf16[272,128]{1,0:T(8,128)(2,1)S(1)} %get-tuple-element.26), channel_id=1, source_target_pairs={{4,8},{8,4},{12,16},{16,12},{20,24},{24,20},{5,9},{9,5},{13,17},{1... | collective-permute-start | bytes 208904 | tf_op jit(solution)/shard_map/ppermute | solution.py:312
  18.9 5.2 %collective-permute-start.3 = (bf16[272,128]{1,0:T(8,128)(2,1)S(1)}, bf16[272,128]{1,0:T(8,128)(2,1)S(1)}, u32[]{:S(2)}, u32[]{:S(2)}) collective-permute-start(bf16[272,128]{1,0:T(8,128)(2,1)S(1)} %get-tuple-element.27), channel_id=1, source_target_pairs={{0,4},{4,0},{8,12},{12,8},{16,20},{20,16},{24,28},{28,24},{1,5},{5... | collective-permute-start | bytes 208904 | tf_op jit(solution)/shard_map/ppermute | solution.py:312
  24.2 0.0 collective-permute-done.2.odd_in_ref
  24.2 2.3 %collective-permute-done.3.even_in_ref = bf16[272,128]{1,0:T(8,128)(2,1)S(1)} collective-permute-done((bf16[272,128]{1,0:T(8,128)(2,1)S(1)}, bf16[272,128]{1,0:T(8,128)(2,1)S(1)}, u32[]{:S(2)}, u32[]{:S(2)}) %collective-permute-start.3) | collective-permute-done | bytes 69664 | tf_op jit(solution)/shard_map/ppermute | solution.py:312
  26.4 3.4 %step1.1 = (f32[24,32,128]{2,1,0:T(8,128)S(1)}, f32[24,32,128]{2,1,0:T(8,128)S(1)}, bf16[272,128]{1,0:T(8,128)(2,1)S(1)}, bf16[272,128]{1,0:T(8,128)(2,1)S(1)}, f32[8,128]{1,0:T(8,128)S(1)}) custom-call(s32[1]{0:T(128)} %bitcast.place_ref, s32[1]{0:T(128)S(6)} %copy.6.live_ref, s32[4,32]{1,0:T(4,128)S(1)} %bitcast.7, ...), custom_call_target="tpu_custom_call" | custom-call | tf_op jit(solution)/shard_map/step1/pallas_call | solution.py:341
  29.9 0.7 %collective-permute-start.4 = (bf16[272,128]{1,0:T(8,128)(2,1)S(1)}, bf16[272,128]{1,0:T(8,128)(2,1)S(1)}, u32[]{:S(2)}, u32[]{:S(2)}) collective-permute-start(bf16[272,128]{1,0:T(8,128)(2,1)S(1)} %get-tuple-element.30), channel_id=1, source_target_pairs={{4,8},{8,4},{12,16},{16,12},{20,24},{24,20},{5,9},{9,5},{13,17},{1... | collective-permute-start | bytes 208904 | tf_op jit(solution)/shard_map/ppermute | solution.py:312
  30.6 5.1 %collective-permute-start.5 = (bf16[272,128]{1,0:T(8,128)(2,1)S(1)}, bf16[272,128]{1,0:T(8,128)(2,1)S(1)}, u32[]{:S(2)}, u32[]{:S(2)}) collective-permute-start(bf16[272,128]{1,0:T(8,128)(2,1)S(1)} %get-tuple-element.31), channel_id=1, source_target_pairs={{0,4},{4,0},{8,12},{12,8},{16,20},{20,16},{24,28},{28,24},{1,5},{5... | collective-permute-start | bytes 208904 | tf_op jit(solution)/shard_map/ppermute | solution.py:312
  35.7 0.0 collective-permute-done.4.odd_in_ref
  35.7 2.3 %collective-permute-done.5.even_in_ref = bf16[272,128]{1,0:T(8,128)(2,1)S(1)} collective-permute-done((bf16[272,128]{1,0:T(8,128)(2,1)S(1)}, bf16[272,128]{1,0:T(8,128)(2,1)S(1)}, u32[]{:S(2)}, u32[]{:S(2)}) %collective-permute-start.5) | collective-permute-done | bytes 69664 | tf_op jit(solution)/shard_map/ppermute | solution.py:312
  38.0 3.8 %step2.1 = (f32[24,32,128]{2,1,0:T(8,128)S(1)}, f32[24,32,128]{2,1,0:T(8,128)S(1)}, bf16[144,128]{1,0:T(8,128)(2,1)S(1)}, bf16[144,128]{1,0:T(8,128)(2,1)S(1)}, f32[32,8,128]{2,1,0:T(8,128)}) custom-call(s32[1]{0:T(128)} %bitcast.place_ref, s32[1]{0:T(128)S(6)} %copy.6.live_ref, s32[4,32]{1,0:T(4,128)S(1)} %bitcast.8, ...), custom_call_target="tpu_custom_call" | custom-call | tf_op jit(solution)/shard_map/step2/pallas_call | solution.py:341
  41.8 5.5 %all-to-all-start = ((f32[32,8,128]{2,1,0:T(8,128)}), f32[32,8,128]{2,1,0:T(8,128)S(1)}, u32[]{:S(2)}, u32[]{:S(2)}) async-start(f32[32,8,128]{2,1,0:T(8,128)} %get-tuple-element.33), calls=%async_computation | async-start | bytes 262144 | tf_op jit(solution)/shard_map/all_to_all | solution.py:355
  47.3 0.7 %collective-permute-start.6 = (bf16[144,128]{1,0:T(8,128)(2,1)S(1)}, bf16[144,128]{1,0:T(8,128)(2,1)S(1)}, u32[]{:S(2)}, u32[]{:S(2)}) collective-permute-start(bf16[144,128]{1,0:T(8,128)(2,1)S(1)} %get-tuple-element.38), channel_id=1, source_target_pairs={{4,8},{8,4},{12,16},{16,12},{20,24},{24,20},{5,9},{9,5},{13,17},{1... | collective-permute-start | bytes 110600 | tf_op jit(solution)/shard_map/ppermute | solution.py:312
  48.0 4.5 %collective-permute-start.7 = (bf16[144,128]{1,0:T(8,128)(2,1)S(1)}, bf16[144,128]{1,0:T(8,128)(2,1)S(1)}, u32[]{:S(2)}, u32[]{:S(2)}) collective-permute-start(bf16[144,128]{1,0:T(8,128)(2,1)S(1)} %get-tuple-element.39), channel_id=1, source_target_pairs={{0,4},{4,0},{8,12},{12,8},{16,20},{20,16},{24,28},{28,24},{1,5},{5... | collective-permute-start | bytes 110600 | tf_op jit(solution)/shard_map/ppermute | solution.py:312
  52.5 0.0 collective-permute-done.6.odd_in_ref
  52.5 2.1 %collective-permute-done.7.even_in_ref = bf16[144,128]{1,0:T(8,128)(2,1)S(1)} collective-permute-done((bf16[144,128]{1,0:T(8,128)(2,1)S(1)}, bf16[144,128]{1,0:T(8,128)(2,1)S(1)}, u32[]{:S(2)}, u32[]{:S(2)}) %collective-permute-start.7) | collective-permute-done | bytes 36896 | tf_op jit(solution)/shard_map/ppermute | solution.py:312
  54.6 0.9 %all-to-all-done.moments_ref = f32[32,8,128]{2,1,0:T(8,128)S(1)} async-done(((f32[32,8,128]{2,1,0:T(8,128)}), f32[32,8,128]{2,1,0:T(8,128)S(1)}, u32[]{:S(2)}, u32[]{:S(2)}) %all-to-all-start) | async-done | bytes 131104 | tf_op jit(solution)/shard_map/all_to_all | solution.py:355
  55.5 1.4 %combine.1 = (f32[32,16,128]{2,1,0:T(8,128)}, f32[32,16,128]{2,1,0:T(8,128)}) custom-call(s32[1]{0:T(128)} %bitcast.place_ref, f32[32,8,128]{2,1,0:T(8,128)S(1)} %all-to-all-done.moments_ref, f32[24,32,128]{2,1,0:T(8,128)S(1)} %get-tuple-element.34.first_ref, f32[24,32,128]{2,1,0:T(8,128)S(1)} %get-tuple-element.35.second_ref, ...), custom_call_target="tpu_custom_call" | custom-call | tf_op jit(solution)/shard_map/combine/pallas_call | solution.py:357
  (1 shorter events, 0.0 us)
Async XLA Ops:
  0.6 14.2 %copy-start.1 = (s32[1,32,4]{1,2,0:T(4,128)S(1)}, s32[1,32,4]{1,2,0:T(4,128)}, u32[]{:S(2)}) copy-start(s32[1,32,4]{1,2,0:T(4,128)} %param.6) | copy-start | bytes 1540
  1.3 0.7 %copy-start = (s32[1,32,4]{1,2,0:T(4,128)S(1)}, s32[1,32,4]{1,2,0:T(4,128)}, u32[]{:S(2)}) copy-start(s32[1,32,4]{1,2,0:T(4,128)} %param.6) | copy-start | bytes 1540
  6.0 6.5 %collective-permute-start = (bf16[272,128]{1,0:T(8,128)(2,1)S(1)}, bf16[272,128]{1,0:T(8,128)(2,1)S(1)}, u32[]{:S(2)}, u32[]{:S(2)}) collective-permute-start(bf16[272,128]{1,0:T(8,128)(2,1)S(1)} %get-tuple-element.22), channel_id=1, source_target_pairs={{4,8},{8,4},{12,16},{16,12},{20,24},{24,20},{5,9},{9,5},{13,17},{1... | collective-permute-start | bytes 208904 | tf_op jit(solution)/shard_map/ppermute | solution.py:312
  6.7 8.1 %collective-permute-start.1 = (bf16[272,128]{1,0:T(8,128)(2,1)S(1)}, bf16[272,128]{1,0:T(8,128)(2,1)S(1)}, u32[]{:S(2)}, u32[]{:S(2)}) collective-permute-start(bf16[272,128]{1,0:T(8,128)(2,1)S(1)} %get-tuple-element.23), channel_id=1, source_target_pairs={{0,4},{4,0},{8,12},{12,8},{16,20},{20,16},{24,28},{28,24},{1,5},{5... | collective-permute-start | bytes 208904 | tf_op jit(solution)/shard_map/ppermute | solution.py:312
  18.2 5.9 %collective-permute-start.2 = (bf16[272,128]{1,0:T(8,128)(2,1)S(1)}, bf16[272,128]{1,0:T(8,128)(2,1)S(1)}, u32[]{:S(2)}, u32[]{:S(2)}) collective-permute-start(bf16[272,128]{1,0:T(8,128)(2,1)S(1)} %get-tuple-element.26), channel_id=1, source_target_pairs={{4,8},{8,4},{12,16},{16,12},{20,24},{24,20},{5,9},{9,5},{13,17},{1... | collective-permute-start | bytes 208904 | tf_op jit(solution)/shard_map/ppermute | solution.py:312
  18.9 7.5 %collective-permute-start.3 = (bf16[272,128]{1,0:T(8,128)(2,1)S(1)}, bf16[272,128]{1,0:T(8,128)(2,1)S(1)}, u32[]{:S(2)}, u32[]{:S(2)}) collective-permute-start(bf16[272,128]{1,0:T(8,128)(2,1)S(1)} %get-tuple-element.27), channel_id=1, source_target_pairs={{0,4},{4,0},{8,12},{12,8},{16,20},{20,16},{24,28},{28,24},{1,5},{5... | collective-permute-start | bytes 208904 | tf_op jit(solution)/shard_map/ppermute | solution.py:312
  29.9 5.8 %collective-permute-start.4 = (bf16[272,128]{1,0:T(8,128)(2,1)S(1)}, bf16[272,128]{1,0:T(8,128)(2,1)S(1)}, u32[]{:S(2)}, u32[]{:S(2)}) collective-permute-start(bf16[272,128]{1,0:T(8,128)(2,1)S(1)} %get-tuple-element.30), channel_id=1, source_target_pairs={{4,8},{8,4},{12,16},{16,12},{20,24},{24,20},{5,9},{9,5},{13,17},{1... | collective-permute-start | bytes 208904 | tf_op jit(solution)/shard_map/ppermute | solution.py:312
  30.6 7.4 %collective-permute-start.5 = (bf16[272,128]{1,0:T(8,128)(2,1)S(1)}, bf16[272,128]{1,0:T(8,128)(2,1)S(1)}, u32[]{:S(2)}, u32[]{:S(2)}) collective-permute-start(bf16[272,128]{1,0:T(8,128)(2,1)S(1)} %get-tuple-element.31), channel_id=1, source_target_pairs={{0,4},{4,0},{8,12},{12,8},{16,20},{20,16},{24,28},{28,24},{1,5},{5... | collective-permute-start | bytes 208904 | tf_op jit(solution)/shard_map/ppermute | solution.py:312
  41.8 13.7 %all-to-all-start = ((f32[32,8,128]{2,1,0:T(8,128)}), f32[32,8,128]{2,1,0:T(8,128)S(1)}, u32[]{:S(2)}, u32[]{:S(2)}) async-start(f32[32,8,128]{2,1,0:T(8,128)} %get-tuple-element.33), calls=%async_computation | async-start | bytes 262144 | tf_op jit(solution)/shard_map/all_to_all | solution.py:355
  47.3 5.2 %collective-permute-start.6 = (bf16[144,128]{1,0:T(8,128)(2,1)S(1)}, bf16[144,128]{1,0:T(8,128)(2,1)S(1)}, u32[]{:S(2)}, u32[]{:S(2)}) collective-permute-start(bf16[144,128]{1,0:T(8,128)(2,1)S(1)} %get-tuple-element.38), channel_id=1, source_target_pairs={{4,8},{8,4},{12,16},{16,12},{20,24},{24,20},{5,9},{9,5},{13,17},{1... | collective-permute-start | bytes 110600 | tf_op jit(solution)/shard_map/ppermute | solution.py:312
  48.0 6.6 %collective-permute-start.7 = (bf16[144,128]{1,0:T(8,128)(2,1)S(1)}, bf16[144,128]{1,0:T(8,128)(2,1)S(1)}, u32[]{:S(2)}, u32[]{:S(2)}) collective-permute-start(bf16[144,128]{1,0:T(8,128)(2,1)S(1)} %get-tuple-element.39), channel_id=1, source_target_pairs={{0,4},{4,0},{8,12},{12,8},{16,20},{20,16},{24,28},{28,24},{1,5},{5... | collective-permute-start | bytes 110600 | tf_op jit(solution)/shard_map/ppermute | solution.py:312

commit v7 on v4

--- a/solution.py
+++ b/solution.py
@@ -13,6 +13,9 @@
 RIM = 2 * HALO_BLOCKS
 TIKHONOV = 0.5
 CHUNKS = 2
+SCALE_ROWS = 16
+CODE_PEAK = 32768.0
+CODE_FLOOR = 1e-33
 MOMENT_ROWS = 8
 VMEM_LIMIT = 24 * 1024 * 1024
 
@@ -42,23 +45,57 @@
     )
 
 
+def folded(value, rows, combine):
+    parts = [value[start : start + rows] for start in range(0, value.shape[0], rows)]
+    return functools.reduce(combine, parts)
+
+
+def repeated(value, rows):
+    return jnp.concatenate([value] * (rows // value.shape[0]), axis=0)
+
+
+def encode(partial_ref, start, rim_ref):
+    waves = partial_ref.shape[1]
+    width = (rim_ref.shape[0] - SCALE_ROWS) // waves
+    scales = rim_ref.at[width * waves :]
+    peak = None
+    for block in range(width):
+        size = folded(jnp.abs(partial_ref[start + block]), 8, jnp.maximum)
+        peak = size if peak is None else jnp.maximum(peak, size)
+    scales[...] = repeated(jnp.maximum(peak, CODE_FLOOR), SCALE_ROWS).astype(jnp.bfloat16)
+    gain = repeated(CODE_PEAK / scales[...].astype(jnp.float32), waves)
+    for block in range(width):
+        value = partial_ref[start + block] * gain
+        for _ in range(3):
+            value = value * jnp.abs(value)
+        rim_ref[block * waves : (block + 1) * waves] = value.astype(jnp.bfloat16)
+
+
+def decode_add(rim_ref, present, target_ref, start):
+    waves = target_ref.shape[1]
+    width = (rim_ref.shape[0] - SCALE_ROWS) // waves
+    scale = rim_ref[width * waves :].astype(jnp.float32) / CODE_PEAK
+    scale = repeated(jnp.where(present, scale, 0.0), waves)
+    for block in range(width):
+        code = rim_ref[block * waves : (block + 1) * waves].astype(jnp.float32)
+        root = jnp.sqrt(jnp.sqrt(jnp.sqrt(jnp.abs(code))))
+        target_ref[start + block] += jnp.where(code < 0.0, -root, root) * scale
+
+
+def rim_top(extent, rim_ref, waves):
+    return extent - (rim_ref.shape[0] - SCALE_ROWS) // waves
+
+
 def emit_rims(partial_ref, upper_ref, lower_ref):
-    width = upper_ref.shape[0]
-    upper_ref[...] = partial_ref[EXTENT - width :]
-    lower_ref[...] = partial_ref[:width]
+    encode(partial_ref, rim_top(partial_ref.shape[0], upper_ref, partial_ref.shape[1]), upper_ref)
+    encode(partial_ref, 0, lower_ref)
 
 
 def add_rims(tiles, place_ref, target_ref, from_below_ref, from_above_ref):
-    width = from_below_ref.shape[0]
     tile = place_ref[0]
-
-    @pl.when(tile > 0)
-    def _():
-        target_ref[:width] += from_below_ref[...]
-
-    @pl.when(tile < tiles - 1)
-    def _():
-        target_ref[target_ref.shape[0] - width :] += from_above_ref[...]
+    top = rim_top(target_ref.shape[0], from_above_ref, target_ref.shape[1])
+    decode_add(from_below_ref, tile > 0, target_ref, 0)
+    decode_add(from_above_ref, tile < tiles - 1, target_ref, top)
 
 
 def rhs_kernel(
@@ -262,8 +299,8 @@
     index = jnp.swapaxes(block_index, 1, 2).reshape(slots, groups)
     weights = kernels.reshape(groups, slots, spaxels, fibres)
     window = jax.ShapeDtypeStruct((EXTENT, waves, spaxels), jnp.float32)
-    rim = jax.ShapeDtypeStruct((RIM, waves, spaxels), jnp.float32)
-    half_rim = jax.ShapeDtypeStruct((HALO_BLOCKS, waves, spaxels), jnp.float32)
+    rim = jax.ShapeDtypeStruct((RIM * waves + SCALE_ROWS, spaxels), jnp.bfloat16)
+    half_rim = jax.ShapeDtypeStruct((HALO_BLOCKS * waves + SCALE_ROWS, spaxels), jnp.bfloat16)
     moment = jax.ShapeDtypeStruct((MOMENT_ROWS, spaxels), jnp.float32)
     moment_all = jax.ShapeDtypeStruct((devices, MOMENT_ROWS, spaxels), jnp.float32)
     params = pltpu.CompilerParams(vmem_limit_bytes=VMEM_LIMIT)

time: 60.2 us -> 55.7 us (0.925)
  waiting for transfers between devices: 17.6 us -> 10.9 us
  starting transfers between devices: 25 us -> 26.6 us
    ppermute x4, waiting for transfers between devices: 14.4 us -> 10.5 us  [swap(): lax.ppermute(upper, 'tile', upward)]
    ppermute x4, waiting for transfers between devices: 3.23 us -> 0.47 us  [swap(): lax.ppermute(lower, 'tile', downward)]
    all_to_all x1, starting transfers between devices: 4.55 us -> 6.09 us  [shards(): moments = lax.all_to_all(moments, ('tile', 'wave'), 0, 0)]
    ppermute x4, starting transfers between devices: 5.22 us -> 6.16 us  [swap(): lax.ppermute(upper, 'tile', upward)]
    ppermute x4, starting transfers between devices: 15.2 us -> 14.4 us  [swap(): lax.ppermute(lower, 'tile', downward)]
  transfers between devices with their start and end apart: 9 -> 9, of which waited for: 7 -> 5; matrix products, arithmetic and copies ran while one was open for 0% -> 0% of each run, Pallas kernels for 0% -> 0%
where the time goes in v7:
time: 55.7 us; the launch traced here: 55.5 us
  starting transfers between devices  26.6 us (48%)
  Pallas kernels  15.9 us (29%)
  waiting for transfers between devices  10.9 us (20%)
  between operations  1.35 us (2%)
  local copies, waits for them, and re-layouts  0.68 us (1%)
    ppermute x4, starting transfers between devices, swap(): lax.ppermute(lower, 'tile', downward)  14.4 us
    pallas_call x3, Pallas kernels, shards(): pl.pallas_call(functools.partial(step_kernel, tiles, power, final), out_s...  10.5 us
    ppermute x4, waiting for transfers between devices, swap(): lax.ppermute(upper, 'tile', upward)  10.5 us
    ppermute x4, starting transfers between devices, swap(): lax.ppermute(upper, 'tile', upward)  6.16 us
    all_to_all x1, starting transfers between devices, shards(): moments = lax.all_to_all(moments, ('tile', 'wave'), 0, 0)  6.09 us
    pallas_call x1, Pallas kernels, shards(): pl.pallas_call(rhs_kernel, out_shape=(jax.ShapeDtypeStruct(weights.shape,...  4.03 us
    pallas_call x1, Pallas kernels, shards(): pl.pallas_call(functools.partial(final_kernel, tiles), out_shape=(out, ou...  1.4 us
  transfers between devices with their start and end apart: 9, of which 5 were waited for; matrix products, arithmetic and copies ran while one was open for 0% of the time, Pallas kernels for 0%

profile of v7, /device:TPU:0, one launch (start us, length us, event | category | flops | bytes accessed | tf_op | source)
XLA Modules:
  0.0 55.5 jit_solution(9737621891182837659)
XLA Ops:
  0.6 0.0 copy-start.1
  1.3 0.0 copy-start
  1.3 0.7 %copy-done = s32[1,32,4]{1,2,0:T(4,128)S(1)} copy-done((s32[1,32,4]{1,2,0:T(4,128)S(1)}, s32[1,32,4]{1,2,0:T(4,128)}, u32[]{:S(2)}) %copy-start) | copy-done | bytes 536
  2.0 4.0 %rhs.1 = (bf16[32,4,128,128]{3,2,1,0:T(8,128)(2,1)S(1)}, f32[24,32,128]{2,1,0:T(8,128)S(1)}, bf16[272,128]{1,0:T(8,128)(2,1)S(1)}, bf16[272,128]{1,0:T(8,128)(2,1)S(1)}) custom-call(s32[1]{0:T(128)} %bitcast.place_ref, s32[1]{0:T(128)S(6)} %copy.6.live_ref, s32[4,32]{1,0:T(4,128)S(1)} %bitcast.5, bf16[32,32,128]{2,1,0:T(8,128)(2,1)} %data_ref.1, ...), custom_call_target="tpu_custom_call" | custom-call | tf_op jit(solution)/shard_map/rhs/pallas_call | solution.py:314
  6.0 3.0 %collective-permute-start = (bf16[272,128]{1,0:T(8,128)(2,1)S(1)}, bf16[272,128]{1,0:T(8,128)(2,1)S(1)}, u32[]{:S(2)}, u32[]{:S(2)}) collective-permute-start(bf16[272,128]{1,0:T(8,128)(2,1)S(1)} %get-tuple-element.22), channel_id=1, source_target_pairs={{0,4},{4,8},{8,12},{12,16},{16,20},{20,24},{24,28},{28,0},{1,5},{5... | collective-permute-start | bytes 208904 | tf_op jit(solution)/shard_map/ppermute | solution.py:311
  9.0 3.1 %collective-permute-start.1 = (bf16[272,128]{1,0:T(8,128)(2,1)S(1)}, bf16[272,128]{1,0:T(8,128)(2,1)S(1)}, u32[]{:S(2)}, u32[]{:S(2)}) collective-permute-start(bf16[272,128]{1,0:T(8,128)(2,1)S(1)} %get-tuple-element.23), channel_id=1, source_target_pairs={{4,0},{8,4},{12,8},{16,12},{20,16},{24,20},{28,24},{0,28},{5,1},{9... | collective-permute-start | bytes 208904 | tf_op jit(solution)/shard_map/ppermute | solution.py:311
  12.2 2.2 %collective-permute-done.from_below_ref = bf16[272,128]{1,0:T(8,128)(2,1)S(1)} collective-permute-done((bf16[272,128]{1,0:T(8,128)(2,1)S(1)}, bf16[272,128]{1,0:T(8,128)(2,1)S(1)}, u32[]{:S(2)}, u32[]{:S(2)}) %collective-permute-start) | collective-permute-done | bytes 69664 | tf_op jit(solution)/shard_map/ppermute | solution.py:311
  14.4 0.5 collective-permute-done.1.from_above_ref
  14.8 0.0 copy-done.1
  14.8 3.4 %step0.1 = (f32[24,32,128]{2,1,0:T(8,128)S(1)}, f32[24,32,128]{2,1,0:T(8,128)S(1)}, bf16[272,128]{1,0:T(8,128)(2,1)S(1)}, bf16[272,128]{1,0:T(8,128)(2,1)S(1)}, f32[8,128]{1,0:T(8,128)S(1)}) custom-call(s32[1]{0:T(128)} %bitcast.place_ref, s32[1]{0:T(128)S(6)} %copy.6.live_ref, s32[4,32]{1,0:T(4,128)S(1)} %bitcast.6, ...), custom_call_target="tpu_custom_call" | custom-call | tf_op jit(solution)/shard_map/step0/pallas_call | solution.py:340
  18.2 1.0 %collective-permute-start.2 = (bf16[272,128]{1,0:T(8,128)(2,1)S(1)}, bf16[272,128]{1,0:T(8,128)(2,1)S(1)}, u32[]{:S(2)}, u32[]{:S(2)}) collective-permute-start(bf16[272,128]{1,0:T(8,128)(2,1)S(1)} %get-tuple-element.26), channel_id=1, source_target_pairs={{0,4},{4,8},{8,12},{12,16},{16,20},{20,24},{24,28},{28,0},{1,5},{5... | collective-permute-start | bytes 208904 | tf_op jit(solution)/shard_map/ppermute | solution.py:311
  19.2 3.8 %collective-permute-start.3 = (bf16[272,128]{1,0:T(8,128)(2,1)S(1)}, bf16[272,128]{1,0:T(8,128)(2,1)S(1)}, u32[]{:S(2)}, u32[]{:S(2)}) collective-permute-start(bf16[272,128]{1,0:T(8,128)(2,1)S(1)} %get-tuple-element.27), channel_id=1, source_target_pairs={{4,0},{8,4},{12,8},{16,12},{20,16},{24,20},{28,24},{0,28},{5,1},{9... | collective-permute-start | bytes 208904 | tf_op jit(solution)/shard_map/ppermute | solution.py:311
  23.0 2.3 %collective-permute-done.2.from_below_ref = bf16[272,128]{1,0:T(8,128)(2,1)S(1)} collective-permute-done((bf16[272,128]{1,0:T(8,128)(2,1)S(1)}, bf16[272,128]{1,0:T(8,128)(2,1)S(1)}, u32[]{:S(2)}, u32[]{:S(2)}) %collective-permute-start.2) | collective-permute-done | bytes 69664 | tf_op jit(solution)/shard_map/ppermute | solution.py:311
  25.3 0.0 collective-permute-done.3.from_above_ref
  25.3 3.4 %step1.1 = (f32[24,32,128]{2,1,0:T(8,128)S(1)}, f32[24,32,128]{2,1,0:T(8,128)S(1)}, bf16[272,128]{1,0:T(8,128)(2,1)S(1)}, bf16[272,128]{1,0:T(8,128)(2,1)S(1)}, f32[8,128]{1,0:T(8,128)S(1)}) custom-call(s32[1]{0:T(128)} %bitcast.place_ref, s32[1]{0:T(128)S(6)} %copy.6.live_ref, s32[4,32]{1,0:T(4,128)S(1)} %bitcast.7, ...), custom_call_target="tpu_custom_call" | custom-call | tf_op jit(solution)/shard_map/step1/pallas_call | solution.py:340
  28.6 0.3 collective-permute-start.4
  28.9 4.5 %collective-permute-start.5 = (bf16[272,128]{1,0:T(8,128)(2,1)S(1)}, bf16[272,128]{1,0:T(8,128)(2,1)S(1)}, u32[]{:S(2)}, u32[]{:S(2)}) collective-permute-start(bf16[272,128]{1,0:T(8,128)(2,1)S(1)} %get-tuple-element.31), channel_id=1, source_target_pairs={{4,0},{8,4},{12,8},{16,12},{20,16},{24,20},{28,24},{0,28},{5,1},{9... | collective-permute-start | bytes 208904 | tf_op jit(solution)/shard_map/ppermute | solution.py:311
  33.5 2.2 %collective-permute-done.4.from_below_ref = bf16[272,128]{1,0:T(8,128)(2,1)S(1)} collective-permute-done((bf16[272,128]{1,0:T(8,128)(2,1)S(1)}, bf16[272,128]{1,0:T(8,128)(2,1)S(1)}, u32[]{:S(2)}, u32[]{:S(2)}) %collective-permute-start.4) | collective-permute-done | bytes 69664 | tf_op jit(solution)/shard_map/ppermute | solution.py:311
  35.7 0.0 collective-permute-done.5.from_above_ref
  35.7 3.8 %step2.1 = (f32[24,32,128]{2,1,0:T(8,128)S(1)}, f32[24,32,128]{2,1,0:T(8,128)S(1)}, bf16[144,128]{1,0:T(8,128)(2,1)S(1)}, bf16[144,128]{1,0:T(8,128)(2,1)S(1)}, f32[32,8,128]{2,1,0:T(8,128)}) custom-call(s32[1]{0:T(128)} %bitcast.place_ref, s32[1]{0:T(128)S(6)} %copy.6.live_ref, s32[4,32]{1,0:T(4,128)S(1)} %bitcast.8, ...), custom_call_target="tpu_custom_call" | custom-call | tf_op jit(solution)/shard_map/step2/pallas_call | solution.py:340
  39.5 6.1 %all-to-all-start = ((f32[32,8,128]{2,1,0:T(8,128)}), f32[32,8,128]{2,1,0:T(8,128)S(1)}, u32[]{:S(2)}, u32[]{:S(2)}) async-start(f32[32,8,128]{2,1,0:T(8,128)} %get-tuple-element.33), calls=%async_computation | async-start | bytes 262144 | tf_op jit(solution)/shard_map/all_to_all | solution.py:354
  45.6 1.8 %collective-permute-start.6 = (bf16[144,128]{1,0:T(8,128)(2,1)S(1)}, bf16[144,128]{1,0:T(8,128)(2,1)S(1)}, u32[]{:S(2)}, u32[]{:S(2)}) collective-permute-start(bf16[144,128]{1,0:T(8,128)(2,1)S(1)} %get-tuple-element.38), channel_id=1, source_target_pairs={{0,4},{4,8},{8,12},{12,16},{16,20},{20,24},{24,28},{28,0},{1,5},{5... | collective-permute-start | bytes 110600 | tf_op jit(solution)/shard_map/ppermute | solution.py:311
  47.4 3.0 %collective-permute-start.7 = (bf16[144,128]{1,0:T(8,128)(2,1)S(1)}, bf16[144,128]{1,0:T(8,128)(2,1)S(1)}, u32[]{:S(2)}, u32[]{:S(2)}) collective-permute-start(bf16[144,128]{1,0:T(8,128)(2,1)S(1)} %get-tuple-element.39), channel_id=1, source_target_pairs={{4,0},{8,4},{12,8},{16,12},{20,16},{24,20},{28,24},{0,28},{5,1},{9... | collective-permute-start | bytes 110600 | tf_op jit(solution)/shard_map/ppermute | solution.py:311
  50.3 3.7 %collective-permute-done.6.from_below_ref = bf16[144,128]{1,0:T(8,128)(2,1)S(1)} collective-permute-done((bf16[144,128]{1,0:T(8,128)(2,1)S(1)}, bf16[144,128]{1,0:T(8,128)(2,1)S(1)}, u32[]{:S(2)}, u32[]{:S(2)}) %collective-permute-start.6) | collective-permute-done | bytes 36896 | tf_op jit(solution)/shard_map/ppermute | solution.py:311
  54.1 0.0 collective-permute-done.7.from_above_ref
  54.1 0.0 all-to-all-done.moments_ref
  54.1 1.4 %combine.1 = (f32[32,16,128]{2,1,0:T(8,128)}, f32[32,16,128]{2,1,0:T(8,128)}) custom-call(s32[1]{0:T(128)} %bitcast.place_ref, f32[32,8,128]{2,1,0:T(8,128)S(1)} %all-to-all-done.moments_ref, f32[24,32,128]{2,1,0:T(8,128)S(1)} %get-tuple-element.34.first_ref, f32[24,32,128]{2,1,0:T(8,128)S(1)} %get-tuple-element.35.second_ref, ...), custom_call_target="tpu_custom_call" | custom-call | tf_op jit(solution)/shard_map/combine/pallas_call | solution.py:356
  (1 shorter events, 0.0 us)
Async XLA Ops:
  0.6 14.2 %copy-start.1 = (s32[1,32,4]{1,2,0:T(4,128)S(1)}, s32[1,32,4]{1,2,0:T(4,128)}, u32[]{:S(2)}) copy-start(s32[1,32,4]{1,2,0:T(4,128)} %param.6) | copy-start | bytes 1540
  1.3 0.7 %copy-start = (s32[1,32,4]{1,2,0:T(4,128)S(1)}, s32[1,32,4]{1,2,0:T(4,128)}, u32[]{:S(2)}) copy-start(s32[1,32,4]{1,2,0:T(4,128)} %param.6) | copy-start | bytes 1540
  6.0 8.4 %collective-permute-start = (bf16[272,128]{1,0:T(8,128)(2,1)S(1)}, bf16[272,128]{1,0:T(8,128)(2,1)S(1)}, u32[]{:S(2)}, u32[]{:S(2)}) collective-permute-start(bf16[272,128]{1,0:T(8,128)(2,1)S(1)} %get-tuple-element.22), channel_id=1, source_target_pairs={{0,4},{4,8},{8,12},{12,16},{16,20},{20,24},{24,28},{28,0},{1,5},{5... | collective-permute-start | bytes 208904 | tf_op jit(solution)/shard_map/ppermute | solution.py:311
  9.0 5.8 %collective-permute-start.1 = (bf16[272,128]{1,0:T(8,128)(2,1)S(1)}, bf16[272,128]{1,0:T(8,128)(2,1)S(1)}, u32[]{:S(2)}, u32[]{:S(2)}) collective-permute-start(bf16[272,128]{1,0:T(8,128)(2,1)S(1)} %get-tuple-element.23), channel_id=1, source_target_pairs={{4,0},{8,4},{12,8},{16,12},{20,16},{24,20},{28,24},{0,28},{5,1},{9... | collective-permute-start | bytes 208904 | tf_op jit(solution)/shard_map/ppermute | solution.py:311
  18.2 7.1 %collective-permute-start.2 = (bf16[272,128]{1,0:T(8,128)(2,1)S(1)}, bf16[272,128]{1,0:T(8,128)(2,1)S(1)}, u32[]{:S(2)}, u32[]{:S(2)}) collective-permute-start(bf16[272,128]{1,0:T(8,128)(2,1)S(1)} %get-tuple-element.26), channel_id=1, source_target_pairs={{0,4},{4,8},{8,12},{12,16},{16,20},{20,24},{24,28},{28,0},{1,5},{5... | collective-permute-start | bytes 208904 | tf_op jit(solution)/shard_map/ppermute | solution.py:311
  19.2 6.1 %collective-permute-start.3 = (bf16[272,128]{1,0:T(8,128)(2,1)S(1)}, bf16[272,128]{1,0:T(8,128)(2,1)S(1)}, u32[]{:S(2)}, u32[]{:S(2)}) collective-permute-start(bf16[272,128]{1,0:T(8,128)(2,1)S(1)} %get-tuple-element.27), channel_id=1, source_target_pairs={{4,0},{8,4},{12,8},{16,12},{20,16},{24,20},{28,24},{0,28},{5,1},{9... | collective-permute-start | bytes 208904 | tf_op jit(solution)/shard_map/ppermute | solution.py:311
  28.6 7.1 %collective-permute-start.4 = (bf16[272,128]{1,0:T(8,128)(2,1)S(1)}, bf16[272,128]{1,0:T(8,128)(2,1)S(1)}, u32[]{:S(2)}, u32[]{:S(2)}) collective-permute-start(bf16[272,128]{1,0:T(8,128)(2,1)S(1)} %get-tuple-element.30), channel_id=1, source_target_pairs={{0,4},{4,8},{8,12},{12,16},{16,20},{20,24},{24,28},{28,0},{1,5},{5... | collective-permute-start | bytes 208904 | tf_op jit(solution)/shard_map/ppermute | solution.py:311
  28.9 6.8 %collective-permute-start.5 = (bf16[272,128]{1,0:T(8,128)(2,1)S(1)}, bf16[272,128]{1,0:T(8,128)(2,1)S(1)}, u32[]{:S(2)}, u32[]{:S(2)}) collective-permute-start(bf16[272,128]{1,0:T(8,128)(2,1)S(1)} %get-tuple-element.31), channel_id=1, source_target_pairs={{4,0},{8,4},{12,8},{16,12},{20,16},{24,20},{28,24},{0,28},{5,1},{9... | collective-permute-start | bytes 208904 | tf_op jit(solution)/shard_map/ppermute | solution.py:311
  39.5 14.6 %all-to-all-start = ((f32[32,8,128]{2,1,0:T(8,128)}), f32[32,8,128]{2,1,0:T(8,128)S(1)}, u32[]{:S(2)}, u32[]{:S(2)}) async-start(f32[32,8,128]{2,1,0:T(8,128)} %get-tuple-element.33), calls=%async_computation | async-start | bytes 262144 | tf_op jit(solution)/shard_map/all_to_all | solution.py:354
  45.6 8.5 %collective-permute-start.6 = (bf16[144,128]{1,0:T(8,128)(2,1)S(1)}, bf16[144,128]{1,0:T(8,128)(2,1)S(1)}, u32[]{:S(2)}, u32[]{:S(2)}) collective-permute-start(bf16[144,128]{1,0:T(8,128)(2,1)S(1)} %get-tuple-element.38), channel_id=1, source_target_pairs={{0,4},{4,8},{8,12},{12,16},{16,20},{20,24},{24,28},{28,0},{1,5},{5... | collective-permute-start | bytes 110600 | tf_op jit(solution)/shard_map/ppermute | solution.py:311
  47.4 6.7 %collective-permute-start.7 = (bf16[144,128]{1,0:T(8,128)(2,1)S(1)}, bf16[144,128]{1,0:T(8,128)(2,1)S(1)}, u32[]{:S(2)}, u32[]{:S(2)}) collective-permute-start(bf16[144,128]{1,0:T(8,128)(2,1)S(1)} %get-tuple-element.39), channel_id=1, source_target_pairs={{4,0},{8,4},{12,8},{16,12},{20,16},{24,20},{28,24},{0,28},{5,1},{9... | collective-permute-start | bytes 110600 | tf_op jit(solution)/shard_map/ppermute | solution.py:311

commit v8 on v7

--- a/solution.py
+++ b/solution.py
@@ -86,16 +86,22 @@
     return extent - (rim_ref.shape[0] - SCALE_ROWS) // waves
 
 
-def emit_rims(partial_ref, upper_ref, lower_ref):
-    encode(partial_ref, rim_top(partial_ref.shape[0], upper_ref, partial_ref.shape[1]), upper_ref)
-    encode(partial_ref, 0, lower_ref)
-
-
-def add_rims(tiles, place_ref, target_ref, from_below_ref, from_above_ref):
-    tile = place_ref[0]
-    top = rim_top(target_ref.shape[0], from_above_ref, target_ref.shape[1])
-    decode_add(from_below_ref, tile > 0, target_ref, 0)
-    decode_add(from_above_ref, tile < tiles - 1, target_ref, top)
+def rim_start(place_ref, extent, rim_ref, waves, upper):
+    return jnp.where(upper == (place_ref[1] == 0), rim_top(extent, rim_ref, waves), 0)
+
+
+def emit_rims(place_ref, partial_ref, onward_ref, return_ref):
+    extent, waves = partial_ref.shape[:2]
+    for upper, rim_ref in ((True, onward_ref), (False, return_ref)):
+        encode(partial_ref, rim_start(place_ref, extent, rim_ref, waves, upper), rim_ref)
+
+
+def add_rims(tiles, place_ref, target_ref, onward_in_ref, return_in_ref):
+    extent, waves = target_ref.shape[:2]
+    for upper, rim_ref in ((False, onward_in_ref), (True, return_in_ref)):
+        start = rim_start(place_ref, extent, rim_ref, waves, upper)
+        end_tile = jnp.where(start > 0, tiles - 1, 0)
+        decode_add(rim_ref, place_ref[0] != end_tile, target_ref, start)
 
 
 def rhs_kernel(
@@ -106,8 +112,8 @@
     source_ref,
     kernels_ref,
     partial_ref,
-    upper_ref,
-    lower_ref,
+    onward_ref,
+    return_ref,
     narrow_ref,
     wide_ref,
     sems,
@@ -135,7 +141,7 @@
             data = jnp.where(group < live, wide_ref[:, group, :], 0.0).astype(jnp.bfloat16)
             spread = spread_of(data, kernels_ref[group].reshape(slots * spaxels, fibres))
             scatter(spread, place_ref, index_ref, group, partial_ref)
-    emit_rims(partial_ref, upper_ref, lower_ref)
+    emit_rims(place_ref, partial_ref, onward_ref, return_ref)
 
 
 def step_kernel(
@@ -146,14 +152,14 @@
     live_ref,
     index_ref,
     held_ref,
-    from_below_ref,
-    from_above_ref,
+    onward_in_ref,
+    return_in_ref,
     moments_in_ref,
     kernels_ref,
     vector_ref,
     partial_ref,
-    upper_ref,
-    lower_ref,
+    onward_ref,
+    return_ref,
     moments_ref,
     operand_ref,
     image_ref,
@@ -163,7 +169,7 @@
     live = live_ref[0]
     first_block = place_ref[0] * BLOCKS_DEV - HALO_BLOCKS
     vector_ref[...] = held_ref[...]
-    add_rims(tiles, place_ref, vector_ref, from_below_ref, from_above_ref)
+    add_rims(tiles, place_ref, vector_ref, onward_in_ref, return_in_ref)
     square = jnp.zeros(vector_ref.shape[1:], jnp.float32)
     for block in range(EXTENT):
         value = vector_ref[block]
@@ -185,7 +191,7 @@
         weights = kernels_ref[group].reshape(slots * spaxels, fibres)
         spread = halves_sum(spread_of(image_ref[group], weights))
         scatter(spread, place_ref, index_ref, group, partial_ref)
-    emit_rims(partial_ref, upper_ref, lower_ref)
+    emit_rims(place_ref, partial_ref, onward_ref, return_ref)
     for block in range(EXTENT):
         partial_ref[block] += TIKHONOV * vector_ref[block]
     square_row = jnp.sum(square, axis=0, keepdims=True)
@@ -240,8 +246,8 @@
     second_ref,
     third_ref,
     held_ref,
-    from_below_ref,
-    from_above_ref,
+    onward_in_ref,
+    return_in_ref,
     solution_ref,
     residual_ref,
     last_ref,
@@ -266,7 +272,7 @@
         if row < 3:
             answer_scaled.append(answer[row] * power)
     last_ref[...] = held_ref[pl.ds(HALO_BLOCKS, BLOCKS_DEV)]
-    add_rims(tiles, place_ref, last_ref, from_below_ref, from_above_ref)
+    add_rims(tiles, place_ref, last_ref, onward_in_ref, return_in_ref)
     for block in range(BLOCKS_DEV):
         first = first_ref[HALO_BLOCKS + block]
         second = second_ref[HALO_BLOCKS + block]
@@ -291,11 +297,21 @@
     return [pl.BlockSpec(memory_space=pltpu.SMEM)] * count
 
 
+def circuit_of(tiles, waves):
+    pairs = []
+    for wave in range(0, waves, 2):
+        path = [tile * waves + wave for tile in range(tiles)]
+        if wave + 1 < waves:
+            path += [tile * waves + wave + 1 for tile in reversed(range(tiles))]
+        pairs += [(node, path[(step + 1) % len(path)]) for step, node in enumerate(path)]
+    return pairs
+
+
 def shards(fibre_data, kernels, block_index, live_count):
     tiles, devices = lax.axis_size("tile"), lax.axis_size("tile") * lax.axis_size("wave")
     _, groups, slots, spaxels, fibres = kernels.shape
     waves = fibre_data.shape[0]
-    place = lax.axis_index("tile").reshape(1)
+    place = jnp.stack([lax.axis_index("tile"), lax.axis_index("wave") % 2])
     index = jnp.swapaxes(block_index, 1, 2).reshape(slots, groups)
     weights = kernels.reshape(groups, slots, spaxels, fibres)
     window = jax.ShapeDtypeStruct((EXTENT, waves, spaxels), jnp.float32)
@@ -304,14 +320,15 @@
     moment = jax.ShapeDtypeStruct((MOMENT_ROWS, spaxels), jnp.float32)
     moment_all = jax.ShapeDtypeStruct((devices, MOMENT_ROWS, spaxels), jnp.float32)
     params = pltpu.CompilerParams(vmem_limit_bytes=VMEM_LIMIT)
-    upward = [(i, (i + 1) % tiles) for i in range(tiles)]
-    downward = [(j, i) for i, j in upward]
-
-    def swap(upper, lower):
-        return lax.ppermute(upper, "tile", upward), lax.ppermute(lower, "tile", downward)
+    circuit = circuit_of(tiles, lax.axis_size("wave"))
+    reverse = [(j, i) for i, j in circuit]
+
+    def swap(onward, back):
+        axes = ("tile", "wave")
+        return lax.ppermute(onward, axes, circuit), lax.ppermute(back, axes, reverse)
 
     chunks = CHUNKS if groups % CHUNKS == 0 else 1
-    weights, held, upper, lower = pl.pallas_call(
+    weights, held, onward, back = pl.pallas_call(
         rhs_kernel,
         out_shape=(jax.ShapeDtypeStruct(weights.shape, weights.dtype), window, rim, rim),
         in_specs=smem(3) + [pl.BlockSpec(memory_space=pltpu.HBM)] * 2,
@@ -335,9 +352,9 @@
     vectors = []
     for power in range(3):
         final = power == 2
-        upper, lower = swap(upper, lower)
+        onward, back = swap(onward, back)
         out_rim = half_rim if final else rim
-        vector, held, upper, lower, moments = pl.pallas_call(
+        vector, held, onward, back, moments = pl.pallas_call(
             functools.partial(step_kernel, tiles, power, final),
             out_shape=(window, window, out_rim, out_rim, moment_all if final else moment),
             in_specs=smem(3) + vmem(5),
@@ -348,9 +365,9 @@
             ],
             compiler_params=params,
             name=f"step{power}",
-        )(place, live_count, index, held, upper, lower, moments, weights)
+        )(place, live_count, index, held, onward, back, moments, weights)
         vectors.append(vector)
-    upper, lower = swap(upper, lower)
+    onward, back = swap(onward, back)
     moments = lax.all_to_all(moments, ("tile", "wave"), 0, 0)
     out = jax.ShapeDtypeStruct((waves, BLOCKS_DEV, spaxels), jnp.float32)
     return pl.pallas_call(
@@ -361,7 +378,7 @@
         scratch_shapes=[pltpu.VMEM((BLOCKS_DEV, waves, spaxels), jnp.float32)],
         compiler_params=params,
         name="combine",
-    )(place, moments, *vectors, held, upper, lower)
+    )(place, moments, *vectors, held, onward, back)
 
 
 def solution(mesh):

time: 55.7 us -> 52.4 us (0.941)
  starting transfers between devices: 26.6 us -> 14.1 us
  waiting for transfers between devices: 10.9 us -> 19.3 us
  Pallas kernels: 15.9 us -> 16.7 us
    ppermute x8, starting transfers between devices: 20.5 us -> 9.78 us  [the longest x4 9.77 us: swap(): lax.ppermute(onward, axes, circuit)]
    ppermute x8, waiting for transfers between devices: 10.9 us -> 17 us  [the longest x4 8.86 us: swap(): lax.ppermute(back, axes, reverse)]
    all_to_all x1, waiting for transfers between devices: 0.01 us -> 2.29 us  [shards(): moments = lax.all_to_all(moments, ('tile', 'wave'), 0, 0)]
    all_to_all x1, starting transfers between devices: 6.09 us -> 4.31 us  [shards(): moments = lax.all_to_all(moments, ('tile', 'wave'), 0, 0)]
  transfers between devices with their start and end apart: 9 -> 9, of which waited for: 5 -> 9; matrix products, arithmetic and copies ran while one was open for 0% -> 0% of each run, Pallas kernels for 0% -> 0%
where the time goes in v8:
time: 52.4 us; the launch traced here: 52.2 us
  waiting for transfers between devices  19.3 us (37%)
  Pallas kernels  16.7 us (32%)
  starting transfers between devices  14.1 us (27%)
  between operations  1.34 us (3%)
  local copies, waits for them, and re-layouts  0.69 us (1%)
    pallas_call x3, Pallas kernels, shards(): pl.pallas_call(functools.partial(step_kernel, tiles, power, final), out_s...  10.7 us
    ppermute x4, starting transfers between devices, swap(): lax.ppermute(onward, axes, circuit)  9.77 us
    ppermute x4, waiting for transfers between devices, swap(): lax.ppermute(back, axes, reverse)  8.86 us
    ppermute x4, waiting for transfers between devices, swap(): lax.ppermute(onward, axes, circuit)  8.14 us
    all_to_all x1, starting transfers between devices, shards(): moments = lax.all_to_all(moments, ('tile', 'wave'), 0, 0)  4.31 us
    pallas_call x1, Pallas kernels, shards(): pl.pallas_call(rhs_kernel, out_shape=(jax.ShapeDtypeStruct(weights.shape,...  4.03 us
    all_to_all x1, waiting for transfers between devices, shards(): moments = lax.all_to_all(moments, ('tile', 'wave'), 0, 0)  2.29 us
    pallas_call x1, Pallas kernels, shards(): pl.pallas_call(functools.partial(final_kernel, tiles), out_shape=(out, ou...  1.94 us
  transfers between devices with their start and end apart: 9, of which 9 were waited for; matrix products, arithmetic and copies ran while one was open for 0% of the time, Pallas kernels for 0%

profile of v8, /device:TPU:0, one launch (start us, length us, event | category | flops | bytes accessed | tf_op | source)
XLA Modules:
  0.0 52.2 jit_solution(10490630735403197468)
XLA Ops:
  0.6 0.0 copy-start.1
  1.3 0.1 pad_add_fusion.place_ref
  1.4 0.0 copy-start
  1.4 0.7 %copy-done = s32[1,32,4]{1,2,0:T(4,128)S(1)} copy-done((s32[1,32,4]{1,2,0:T(4,128)S(1)}, s32[1,32,4]{1,2,0:T(4,128)}, u32[]{:S(2)}) %copy-start) | copy-done | bytes 536
  2.1 4.0 %rhs.1 = (bf16[32,4,128,128]{3,2,1,0:T(8,128)(2,1)S(1)}, f32[24,32,128]{2,1,0:T(8,128)S(1)}, bf16[272,128]{1,0:T(8,128)(2,1)S(1)}, bf16[272,128]{1,0:T(8,128)(2,1)S(1)}) custom-call(s32[2]{0:T(128)S(1)} %pad_add_fusion.place_ref, s32[1]{0:T(128)S(6)} %copy.6.live_ref, s32[4,32]{1,0:T(4,128)S(1)} %bitcast.6, bf16[32,32,128]{2,1,0:T(8,128)(2,1)} %data_ref.1, ...), custom_call_target="tpu_custom_call" | custom-call | tf_op jit(solution)/shard_map/rhs/pallas_call | solution.py:331
  6.1 3.0 %collective-permute-start = (bf16[272,128]{1,0:T(8,128)(2,1)S(1)}, bf16[272,128]{1,0:T(8,128)(2,1)S(1)}, u32[]{:S(2)}, u32[]{:S(2)}) collective-permute-start(bf16[272,128]{1,0:T(8,128)(2,1)S(1)} %get-tuple-element.22), channel_id=1, source_target_pairs={{0,4},{4,8},{8,12},{12,16},{16,20},{20,24},{24,28},{28,29},{29,25}... | collective-permute-start | bytes 208904 | tf_op jit(solution)/shard_map/ppermute | solution.py:328
  9.1 0.0 collective-permute-start.1
  9.1 2.3 %collective-permute-done.onward_in_ref = bf16[272,128]{1,0:T(8,128)(2,1)S(1)} collective-permute-done((bf16[272,128]{1,0:T(8,128)(2,1)S(1)}, bf16[272,128]{1,0:T(8,128)(2,1)S(1)}, u32[]{:S(2)}, u32[]{:S(2)}) %collective-permute-start) | collective-permute-done | bytes 69664 | tf_op jit(solution)/shard_map/ppermute | solution.py:328
  11.5 2.0 %collective-permute-done.1.return_in_ref = bf16[272,128]{1,0:T(8,128)(2,1)S(1)} collective-permute-done((bf16[272,128]{1,0:T(8,128)(2,1)S(1)}, bf16[272,128]{1,0:T(8,128)(2,1)S(1)}, u32[]{:S(2)}, u32[]{:S(2)}) %collective-permute-start.1) | collective-permute-done | bytes 69664 | tf_op jit(solution)/shard_map/ppermute | solution.py:328
  13.4 0.0 copy-done.1
  13.4 3.4 %step0.1 = (f32[24,32,128]{2,1,0:T(8,128)S(1)}, f32[24,32,128]{2,1,0:T(8,128)S(1)}, bf16[272,128]{1,0:T(8,128)(2,1)S(1)}, bf16[272,128]{1,0:T(8,128)(2,1)S(1)}, f32[8,128]{1,0:T(8,128)S(1)}) custom-call(s32[2]{0:T(128)S(1)} %pad_add_fusion.place_ref, s32[1]{0:T(128)S(6)} %copy.6.live_ref, s32[4,32]{1,0:T(4,128)S(1)} %bitcast.7, ...), custom_call_target="tpu_custom_call" | custom-call | tf_op jit(solution)/shard_map/step0/pallas_call | solution.py:357
  16.9 2.5 %collective-permute-start.2 = (bf16[272,128]{1,0:T(8,128)(2,1)S(1)}, bf16[272,128]{1,0:T(8,128)(2,1)S(1)}, u32[]{:S(2)}, u32[]{:S(2)}) collective-permute-start(bf16[272,128]{1,0:T(8,128)(2,1)S(1)} %get-tuple-element.26), channel_id=1, source_target_pairs={{0,4},{4,8},{8,12},{12,16},{16,20},{20,24},{24,28},{28,29},{29,25}... | collective-permute-start | bytes 208904 | tf_op jit(solution)/shard_map/ppermute | solution.py:328
  19.4 0.0 collective-permute-start.3
  19.4 1.9 %collective-permute-done.2.onward_in_ref = bf16[272,128]{1,0:T(8,128)(2,1)S(1)} collective-permute-done((bf16[272,128]{1,0:T(8,128)(2,1)S(1)}, bf16[272,128]{1,0:T(8,128)(2,1)S(1)}, u32[]{:S(2)}, u32[]{:S(2)}) %collective-permute-start.2) | collective-permute-done | bytes 69664 | tf_op jit(solution)/shard_map/ppermute | solution.py:328
  21.3 2.4 %collective-permute-done.3.return_in_ref = bf16[272,128]{1,0:T(8,128)(2,1)S(1)} collective-permute-done((bf16[272,128]{1,0:T(8,128)(2,1)S(1)}, bf16[272,128]{1,0:T(8,128)(2,1)S(1)}, u32[]{:S(2)}, u32[]{:S(2)}) %collective-permute-start.3) | collective-permute-done | bytes 69664 | tf_op jit(solution)/shard_map/ppermute | solution.py:328
  23.7 3.4 %step1.1 = (f32[24,32,128]{2,1,0:T(8,128)S(1)}, f32[24,32,128]{2,1,0:T(8,128)S(1)}, bf16[272,128]{1,0:T(8,128)(2,1)S(1)}, bf16[272,128]{1,0:T(8,128)(2,1)S(1)}, f32[8,128]{1,0:T(8,128)S(1)}) custom-call(s32[2]{0:T(128)S(1)} %pad_add_fusion.place_ref, s32[1]{0:T(128)S(6)} %copy.6.live_ref, s32[4,32]{1,0:T(4,128)S(1)} %bitcast.8, ...), custom_call_target="tpu_custom_call" | custom-call | tf_op jit(solution)/shard_map/step1/pallas_call | solution.py:357
  27.1 2.4 %collective-permute-start.4 = (bf16[272,128]{1,0:T(8,128)(2,1)S(1)}, bf16[272,128]{1,0:T(8,128)(2,1)S(1)}, u32[]{:S(2)}, u32[]{:S(2)}) collective-permute-start(bf16[272,128]{1,0:T(8,128)(2,1)S(1)} %get-tuple-element.30), channel_id=1, source_target_pairs={{0,4},{4,8},{8,12},{12,16},{16,20},{20,24},{24,28},{28,29},{29,25}... | collective-permute-start | bytes 208904 | tf_op jit(solution)/shard_map/ppermute | solution.py:328
  29.6 0.0 collective-permute-start.5
  29.6 1.9 %collective-permute-done.4.onward_in_ref = bf16[272,128]{1,0:T(8,128)(2,1)S(1)} collective-permute-done((bf16[272,128]{1,0:T(8,128)(2,1)S(1)}, bf16[272,128]{1,0:T(8,128)(2,1)S(1)}, u32[]{:S(2)}, u32[]{:S(2)}) %collective-permute-start.4) | collective-permute-done | bytes 69664 | tf_op jit(solution)/shard_map/ppermute | solution.py:328
  31.5 2.4 %collective-permute-done.5.return_in_ref = bf16[272,128]{1,0:T(8,128)(2,1)S(1)} collective-permute-done((bf16[272,128]{1,0:T(8,128)(2,1)S(1)}, bf16[272,128]{1,0:T(8,128)(2,1)S(1)}, u32[]{:S(2)}, u32[]{:S(2)}) %collective-permute-start.5) | collective-permute-done | bytes 69664 | tf_op jit(solution)/shard_map/ppermute | solution.py:328
  33.9 3.9 %step2.1 = (f32[24,32,128]{2,1,0:T(8,128)S(1)}, f32[24,32,128]{2,1,0:T(8,128)S(1)}, bf16[144,128]{1,0:T(8,128)(2,1)S(1)}, bf16[144,128]{1,0:T(8,128)(2,1)S(1)}, f32[32,8,128]{2,1,0:T(8,128)}) custom-call(s32[2]{0:T(128)S(1)} %pad_add_fusion.place_ref, s32[1]{0:T(128)S(6)} %copy.6.live_ref, s32[4,32]{1,0:T(4,128)S(1)} %bitcast.9, ...), custom_call_target="tpu_custom_call" | custom-call | tf_op jit(solution)/shard_map/step2/pallas_call | solution.py:357
  37.7 4.3 %all-to-all-start = ((f32[32,8,128]{2,1,0:T(8,128)}), f32[32,8,128]{2,1,0:T(8,128)S(1)}, u32[]{:S(2)}, u32[]{:S(2)}) async-start(f32[32,8,128]{2,1,0:T(8,128)} %get-tuple-element.33), calls=%async_computation | async-start | bytes 262144 | tf_op jit(solution)/shard_map/all_to_all | solution.py:371
  42.0 1.8 %collective-permute-start.6 = (bf16[144,128]{1,0:T(8,128)(2,1)S(1)}, bf16[144,128]{1,0:T(8,128)(2,1)S(1)}, u32[]{:S(2)}, u32[]{:S(2)}) collective-permute-start(bf16[144,128]{1,0:T(8,128)(2,1)S(1)} %get-tuple-element.38), channel_id=1, source_target_pairs={{0,4},{4,8},{8,12},{12,16},{16,20},{20,24},{24,28},{28,29},{29,25}... | collective-permute-start | bytes 110600 | tf_op jit(solution)/shard_map/ppermute | solution.py:328
  43.9 0.0 collective-permute-start.7
  43.9 1.9 %collective-permute-done.6.onward_in_ref = bf16[144,128]{1,0:T(8,128)(2,1)S(1)} collective-permute-done((bf16[144,128]{1,0:T(8,128)(2,1)S(1)}, bf16[144,128]{1,0:T(8,128)(2,1)S(1)}, u32[]{:S(2)}, u32[]{:S(2)}) %collective-permute-start.6) | collective-permute-done | bytes 36896 | tf_op jit(solution)/shard_map/ppermute | solution.py:328
  45.8 2.2 %collective-permute-done.7.return_in_ref = bf16[144,128]{1,0:T(8,128)(2,1)S(1)} collective-permute-done((bf16[144,128]{1,0:T(8,128)(2,1)S(1)}, bf16[144,128]{1,0:T(8,128)(2,1)S(1)}, u32[]{:S(2)}, u32[]{:S(2)}) %collective-permute-start.7) | collective-permute-done | bytes 36896 | tf_op jit(solution)/shard_map/ppermute | solution.py:328
  48.0 2.3 %all-to-all-done.moments_ref = f32[32,8,128]{2,1,0:T(8,128)S(1)} async-done(((f32[32,8,128]{2,1,0:T(8,128)}), f32[32,8,128]{2,1,0:T(8,128)S(1)}, u32[]{:S(2)}, u32[]{:S(2)}) %all-to-all-start) | async-done | bytes 131104 | tf_op jit(solution)/shard_map/all_to_all | solution.py:371
  50.3 1.9 %combine.1 = (f32[32,16,128]{2,1,0:T(8,128)}, f32[32,16,128]{2,1,0:T(8,128)}) custom-call(s32[2]{0:T(128)S(1)} %pad_add_fusion.place_ref, f32[32,8,128]{2,1,0:T(8,128)S(1)} %all-to-all-done.moments_ref, f32[24,32,128]{2,1,0:T(8,128)S(1)} %get-tuple-element.34.first_ref, f32[24,32,128]{2,1,0:T(8,128)S(1)} %get-tuple-element.35.second_ref, ...), custom_call_target="tpu_custom_call" | custom-call | tf_op jit(solution)/shard_map/combine/pallas_call | solution.py:373
  (1 shorter events, 0.0 us)
Async XLA Ops:
  0.6 12.8 %copy-start.1 = (s32[1,32,4]{1,2,0:T(4,128)S(1)}, s32[1,32,4]{1,2,0:T(4,128)}, u32[]{:S(2)}) copy-start(s32[1,32,4]{1,2,0:T(4,128)} %param.6) | copy-start | bytes 1540
  1.4 0.7 %copy-start = (s32[1,32,4]{1,2,0:T(4,128)S(1)}, s32[1,32,4]{1,2,0:T(4,128)}, u32[]{:S(2)}) copy-start(s32[1,32,4]{1,2,0:T(4,128)} %param.6) | copy-start | bytes 1540
  6.1 5.4 %collective-permute-start = (bf16[272,128]{1,0:T(8,128)(2,1)S(1)}, bf16[272,128]{1,0:T(8,128)(2,1)S(1)}, u32[]{:S(2)}, u32[]{:S(2)}) collective-permute-start(bf16[272,128]{1,0:T(8,128)(2,1)S(1)} %get-tuple-element.22), channel_id=1, source_target_pairs={{0,4},{4,8},{8,12},{12,16},{16,20},{20,24},{24,28},{28,29},{29,25}... | collective-permute-start | bytes 208904 | tf_op jit(solution)/shard_map/ppermute | solution.py:328
  9.1 4.3 %collective-permute-start.1 = (bf16[272,128]{1,0:T(8,128)(2,1)S(1)}, bf16[272,128]{1,0:T(8,128)(2,1)S(1)}, u32[]{:S(2)}, u32[]{:S(2)}) collective-permute-start(bf16[272,128]{1,0:T(8,128)(2,1)S(1)} %get-tuple-element.23), channel_id=1, source_target_pairs={{4,0},{8,4},{12,8},{16,12},{20,16},{24,20},{28,24},{29,28},{25,29}... | collective-permute-start | bytes 208904 | tf_op jit(solution)/shard_map/ppermute | solution.py:328
  16.9 4.4 %collective-permute-start.2 = (bf16[272,128]{1,0:T(8,128)(2,1)S(1)}, bf16[272,128]{1,0:T(8,128)(2,1)S(1)}, u32[]{:S(2)}, u32[]{:S(2)}) collective-permute-start(bf16[272,128]{1,0:T(8,128)(2,1)S(1)} %get-tuple-element.26), channel_id=1, source_target_pairs={{0,4},{4,8},{8,12},{12,16},{16,20},{20,24},{24,28},{28,29},{29,25}... | collective-permute-start | bytes 208904 | tf_op jit(solution)/shard_map/ppermute | solution.py:328
  19.4 4.3 %collective-permute-start.3 = (bf16[272,128]{1,0:T(8,128)(2,1)S(1)}, bf16[272,128]{1,0:T(8,128)(2,1)S(1)}, u32[]{:S(2)}, u32[]{:S(2)}) collective-permute-start(bf16[272,128]{1,0:T(8,128)(2,1)S(1)} %get-tuple-element.27), channel_id=1, source_target_pairs={{4,0},{8,4},{12,8},{16,12},{20,16},{24,20},{28,24},{29,28},{25,29}... | collective-permute-start | bytes 208904 | tf_op jit(solution)/shard_map/ppermute | solution.py:328
  27.1 4.4 %collective-permute-start.4 = (bf16[272,128]{1,0:T(8,128)(2,1)S(1)}, bf16[272,128]{1,0:T(8,128)(2,1)S(1)}, u32[]{:S(2)}, u32[]{:S(2)}) collective-permute-start(bf16[272,128]{1,0:T(8,128)(2,1)S(1)} %get-tuple-element.30), channel_id=1, source_target_pairs={{0,4},{4,8},{8,12},{12,16},{16,20},{20,24},{24,28},{28,29},{29,25}... | collective-permute-start | bytes 208904 | tf_op jit(solution)/shard_map/ppermute | solution.py:328
  29.6 4.3 %collective-permute-start.5 = (bf16[272,128]{1,0:T(8,128)(2,1)S(1)}, bf16[272,128]{1,0:T(8,128)(2,1)S(1)}, u32[]{:S(2)}, u32[]{:S(2)}) collective-permute-start(bf16[272,128]{1,0:T(8,128)(2,1)S(1)} %get-tuple-element.31), channel_id=1, source_target_pairs={{4,0},{8,4},{12,8},{16,12},{20,16},{24,20},{28,24},{29,28},{25,29}... | collective-permute-start | bytes 208904 | tf_op jit(solution)/shard_map/ppermute | solution.py:328
  37.7 12.5 %all-to-all-start = ((f32[32,8,128]{2,1,0:T(8,128)}), f32[32,8,128]{2,1,0:T(8,128)S(1)}, u32[]{:S(2)}, u32[]{:S(2)}) async-start(f32[32,8,128]{2,1,0:T(8,128)} %get-tuple-element.33), calls=%async_computation | async-start | bytes 262144 | tf_op jit(solution)/shard_map/all_to_all | solution.py:371
  42.0 3.8 %collective-permute-start.6 = (bf16[144,128]{1,0:T(8,128)(2,1)S(1)}, bf16[144,128]{1,0:T(8,128)(2,1)S(1)}, u32[]{:S(2)}, u32[]{:S(2)}) collective-permute-start(bf16[144,128]{1,0:T(8,128)(2,1)S(1)} %get-tuple-element.38), channel_id=1, source_target_pairs={{0,4},{4,8},{8,12},{12,16},{16,20},{20,24},{24,28},{28,29},{29,25}... | collective-permute-start | bytes 110600 | tf_op jit(solution)/shard_map/ppermute | solution.py:328
  43.9 4.1 %collective-permute-start.7 = (bf16[144,128]{1,0:T(8,128)(2,1)S(1)}, bf16[144,128]{1,0:T(8,128)(2,1)S(1)}, u32[]{:S(2)}, u32[]{:S(2)}) collective-permute-start(bf16[144,128]{1,0:T(8,128)(2,1)S(1)} %get-tuple-element.39), channel_id=1, source_target_pairs={{4,0},{8,4},{12,8},{16,12},{20,16},{24,20},{28,24},{29,28},{25,29}... | collective-permute-start | bytes 110600 | tf_op jit(solution)/shard_map/ppermute | solution.py:328

commit v9 on v8

--- a/solution.py
+++ b/solution.py
@@ -12,6 +12,8 @@
 EXTENT = BLOCKS_DEV + 2 * HALO_BLOCKS
 RIM = 2 * HALO_BLOCKS
 TIKHONOV = 0.5
+ITERATIONS = 3
+SPREAD_LIMIT = 40.0
 CHUNKS = 2
 SCALE_ROWS = 16
 CODE_PEAK = 32768.0
@@ -86,26 +88,27 @@
     return extent - (rim_ref.shape[0] - SCALE_ROWS) // waves
 
 
-def rim_start(place_ref, extent, rim_ref, waves, upper):
-    return jnp.where(upper == (place_ref[1] == 0), rim_top(extent, rim_ref, waves), 0)
-
-
-def emit_rims(place_ref, partial_ref, onward_ref, return_ref):
+def rim_start(lane_ref, extent, rim_ref, waves, upper):
+    return jnp.where(upper == (lane_ref[0] == 0), rim_top(extent, rim_ref, waves), 0)
+
+
+def emit_rims(lane_ref, partial_ref, onward_ref, return_ref):
     extent, waves = partial_ref.shape[:2]
     for upper, rim_ref in ((True, onward_ref), (False, return_ref)):
-        encode(partial_ref, rim_start(place_ref, extent, rim_ref, waves, upper), rim_ref)
-
-
-def add_rims(tiles, place_ref, target_ref, onward_in_ref, return_in_ref):
+        encode(partial_ref, rim_start(lane_ref, extent, rim_ref, waves, upper), rim_ref)
+
+
+def add_rims(tiles, place_ref, lane_ref, target_ref, onward_in_ref, return_in_ref):
     extent, waves = target_ref.shape[:2]
     for upper, rim_ref in ((False, onward_in_ref), (True, return_in_ref)):
-        start = rim_start(place_ref, extent, rim_ref, waves, upper)
+        start = rim_start(lane_ref, extent, rim_ref, waves, upper)
         end_tile = jnp.where(start > 0, tiles - 1, 0)
         decode_add(rim_ref, place_ref[0] != end_tile, target_ref, start)
 
 
 def rhs_kernel(
     place_ref,
+    lane_ref,
     live_ref,
     index_ref,
     data_ref,
@@ -141,7 +144,7 @@
             data = jnp.where(group < live, wide_ref[:, group, :], 0.0).astype(jnp.bfloat16)
             spread = spread_of(data, kernels_ref[group].reshape(slots * spaxels, fibres))
             scatter(spread, place_ref, index_ref, group, partial_ref)
-    emit_rims(place_ref, partial_ref, onward_ref, return_ref)
+    emit_rims(lane_ref, partial_ref, onward_ref, return_ref)
 
 
 def step_kernel(
@@ -149,6 +152,7 @@
     power,
     final,
     place_ref,
+    lane_ref,
     live_ref,
     index_ref,
     held_ref,
@@ -169,7 +173,7 @@
     live = live_ref[0]
     first_block = place_ref[0] * BLOCKS_DEV - HALO_BLOCKS
     vector_ref[...] = held_ref[...]
-    add_rims(tiles, place_ref, vector_ref, onward_in_ref, return_in_ref)
+    add_rims(tiles, place_ref, lane_ref, vector_ref, onward_in_ref, return_in_ref)
     square = jnp.zeros(vector_ref.shape[1:], jnp.float32)
     for block in range(EXTENT):
         value = vector_ref[block]
@@ -191,7 +195,7 @@
         weights = kernels_ref[group].reshape(slots * spaxels, fibres)
         spread = halves_sum(spread_of(image_ref[group], weights))
         scatter(spread, place_ref, index_ref, group, partial_ref)
-    emit_rims(place_ref, partial_ref, onward_ref, return_ref)
+    emit_rims(lane_ref, partial_ref, onward_ref, return_ref)
     for block in range(EXTENT):
         partial_ref[block] += TIKHONOV * vector_ref[block]
     square_row = jnp.sum(square, axis=0, keepdims=True)
@@ -241,6 +245,7 @@
 def final_kernel(
     tiles,
     place_ref,
+    lane_ref,
     moments_ref,
     first_ref,
     second_ref,
@@ -250,6 +255,7 @@
     return_in_ref,
     solution_ref,
     residual_ref,
+    flag_ref,
     last_ref,
 ):
     sums = moments_ref[0]
@@ -263,7 +269,11 @@
     for row in range(6):
         scaled.append(raw[row] * factor)
         factor = factor * unit
-    answer, residual = coefficients(scaled, 3)
+    answer, residual = coefficients(scaled, ITERATIONS)
+    sizes = [jnp.sqrt(scaled[2 * row]) for row in range(3)]
+    sizes.append(scaled[5] / sizes[2])
+    terms = sum(jnp.abs(c) * size for c, size in zip(residual, sizes))
+    flag_ref[0] = jnp.min(jnp.where(terms <= SPREAD_LIMIT, 1, 0))
     power = jnp.ones_like(unit)
     answer_scaled, residual_scaled = [], []
     for row in range(4):
@@ -272,7 +282,7 @@
         if row < 3:
             answer_scaled.append(answer[row] * power)
     last_ref[...] = held_ref[pl.ds(HALO_BLOCKS, BLOCKS_DEV)]
-    add_rims(tiles, place_ref, last_ref, onward_in_ref, return_in_ref)
+    add_rims(tiles, place_ref, lane_ref, last_ref, onward_in_ref, return_in_ref)
     for block in range(BLOCKS_DEV):
         first = first_ref[HALO_BLOCKS + block]
         second = second_ref[HALO_BLOCKS + block]
@@ -311,7 +321,8 @@
     tiles, devices = lax.axis_size("tile"), lax.axis_size("tile") * lax.axis_size("wave")
     _, groups, slots, spaxels, fibres = kernels.shape
     waves = fibre_data.shape[0]
-    place = jnp.stack([lax.axis_index("tile"), lax.axis_index("wave") % 2])
+    place = lax.axis_index("tile").reshape(1)
+    lane = (lax.axis_index("wave") % 2).reshape(1)
     index = jnp.swapaxes(block_index, 1, 2).reshape(slots, groups)
     weights = kernels.reshape(groups, slots, spaxels, fibres)
     window = jax.ShapeDtypeStruct((EXTENT, waves, spaxels), jnp.float32)
@@ -331,7 +342,7 @@
     weights, held, onward, back = pl.pallas_call(
         rhs_kernel,
         out_shape=(jax.ShapeDtypeStruct(weights.shape, weights.dtype), window, rim, rim),
-        in_specs=smem(3) + [pl.BlockSpec(memory_space=pltpu.HBM)] * 2,
+        in_specs=smem(4) + [pl.BlockSpec(memory_space=pltpu.HBM)] * 2,
         out_specs=tuple(vmem(4)),
         scratch_shapes=[
             pltpu.VMEM(fibre_data.shape, fibre_data.dtype),
@@ -343,11 +354,16 @@
         name="rhs",
     )(
         place,
+        lane,
         live_count,
         index,
         pltpu.with_memory_space_constraint(fibre_data, pltpu.HBM),
         pltpu.with_memory_space_constraint(weights, pltpu.HBM),
     )
+    scratch = [
+        pltpu.VMEM((EXTENT, 2 * waves, spaxels), jnp.bfloat16),
+        pltpu.VMEM((groups, 2 * waves, fibres), jnp.bfloat16),
+    ]
     moments = jnp.zeros(moment.shape, jnp.float32)
     vectors = []
     for power in range(3):
@@ -357,28 +373,86 @@
         vector, held, onward, back, moments = pl.pallas_call(
             functools.partial(step_kernel, tiles, power, final),
             out_shape=(window, window, out_rim, out_rim, moment_all if final else moment),
-            in_specs=smem(3) + vmem(5),
+            in_specs=smem(4) + vmem(5),
             out_specs=tuple(vmem(5)),
-            scratch_shapes=[
-                pltpu.VMEM((EXTENT, 2 * waves, spaxels), jnp.bfloat16),
-                pltpu.VMEM((groups, 2 * waves, fibres), jnp.bfloat16),
-            ],
+            scratch_shapes=scratch,
             compiler_params=params,
             name=f"step{power}",
-        )(place, live_count, index, held, onward, back, moments, weights)
+        )(place, lane, live_count, index, held, onward, back, moments, weights)
         vectors.append(vector)
     onward, back = swap(onward, back)
     moments = lax.all_to_all(moments, ("tile", "wave"), 0, 0)
     out = jax.ShapeDtypeStruct((waves, BLOCKS_DEV, spaxels), jnp.float32)
-    return pl.pallas_call(
+    answer, residual, steady = pl.pallas_call(
         functools.partial(final_kernel, tiles),
-        out_shape=(out, out),
-        in_specs=smem(1) + vmem(7),
-        out_specs=tuple(vmem(2)),
+        out_shape=(out, out, jax.ShapeDtypeStruct((1,), jnp.int32)),
+        in_specs=smem(2) + vmem(7),
+        out_specs=tuple(vmem(2) + smem(1)),
         scratch_shapes=[pltpu.VMEM((BLOCKS_DEV, waves, spaxels), jnp.float32)],
         compiler_params=params,
         name="combine",
-    )(place, moments, *vectors, held, onward, back)
+    )(place, lane, moments, *vectors, held, onward, back)
+
+    def settled(held, onward, back):
+        def decoded(code):
+            scale = code[RIM * waves :].astype(jnp.float32) / CODE_PEAK
+            code = code[: RIM * waves].astype(jnp.float32).reshape(-1, SCALE_ROWS, spaxels)
+            root = jnp.sqrt(jnp.sqrt(jnp.sqrt(jnp.abs(code))))
+            return (jnp.where(code < 0.0, -root, root) * scale).reshape(RIM, waves, spaxels)
+
+        first = lane[0] == 0
+        below = decoded(jnp.where(first, onward, back))
+        above = decoded(jnp.where(first, back, onward))
+        held = held.at[:RIM].add(jnp.where(place[0] > 0, below, 0.0))
+        return held.at[EXTENT - RIM :].add(jnp.where(place[0] < tiles - 1, above, 0.0))
+
+    def owned(vector):
+        return vector[HALO_BLOCKS : HALO_BLOCKS + BLOCKS_DEV]
+
+    def inner(first, second):
+        return lax.psum(jnp.sum(owned(first) * owned(second)), ("tile", "wave"))
+
+    def plain(operands):
+        start, _, _ = operands
+        none = jnp.zeros(rim.shape, rim.dtype)
+
+        def iterate(_, state):
+            total, left, direction, norm = state
+            _, held, onward, back, _ = pl.pallas_call(
+                functools.partial(step_kernel, tiles, 0, False),
+                out_shape=(window, window, rim, rim, moment),
+                in_specs=smem(4) + vmem(5),
+                out_specs=tuple(vmem(5)),
+                scratch_shapes=scratch,
+                compiler_params=params,
+                name="plain",
+            )(
+                place,
+                lane,
+                live_count,
+                index,
+                direction,
+                none,
+                none,
+                jnp.zeros(moment.shape, jnp.float32),
+                weights,
+            )
+            applied = settled(held, *swap(onward, back))
+            size = norm / inner(direction, applied)
+            total = total + size * direction
+            left = left - size * applied
+            following = inner(left, left)
+            direction = left + (following / norm) * direction
+            return total, left, direction, following
+
+        state = (jnp.zeros_like(start), start, start, inner(start, start))
+        total, left, _, _ = lax.fori_loop(0, ITERATIONS, iterate, state)
+        return jnp.swapaxes(owned(total), 0, 1), jnp.swapaxes(owned(left), 0, 1)
+
+    def kept(operands):
+        return operands[1], operands[2]
+
+    return lax.cond(steady[0] == 1, kept, plain, (vectors[0], answer, residual))
 
 
 def solution(mesh):

time: 52.4 us -> 53 us (1.011)
  Pallas kernels: 16.7 us -> 15.7 us
  local copies, waits for them, and re-layouts: 0.69 us -> 1.41 us
  between operations: 1.34 us -> 2.03 us
    pallas_call x1, Pallas kernels: 1.94 us -> 0.94 us  [shards(): pl.pallas_call(functools.partial(final_kernel, tiles), out_shape=(out, ou...]
    unnamed x4 -> x8, local copies, waits for them, and re-layouts: 0.69 us -> 1.41 us
where the time goes in v9:
time: 53 us; the launch traced here: 52.7 us
  waiting for transfers between devices  19.3 us (36%)
  Pallas kernels  15.7 us (30%)
  starting transfers between devices  14.1 us (27%)
  between operations  2.03 us (4%)
  local copies, waits for them, and re-layouts  1.41 us (3%)
    pallas_call x3, Pallas kernels, shards(): pl.pallas_call(functools.partial(step_kernel, tiles, power, final), out_s...  10.6 us
    ppermute x4, starting transfers between devices, swap(): lax.ppermute(onward, axes, circuit)  9.78 us
    ppermute x4, waiting for transfers between devices, swap(): lax.ppermute(back, axes, reverse)  8.85 us
    ppermute x4, waiting for transfers between devices, swap(): lax.ppermute(onward, axes, circuit)  8.15 us
    all_to_all x1, starting transfers between devices, shards(): moments = lax.all_to_all(moments, ('tile', 'wave'), 0, 0)  4.31 us
    pallas_call x1, Pallas kernels, shards(): pl.pallas_call(rhs_kernel, out_shape=(jax.ShapeDtypeStruct(weights.shape,...  4.15 us
    all_to_all x1, waiting for transfers between devices, shards(): moments = lax.all_to_all(moments, ('tile', 'wave'), 0, 0)  2.29 us
    unnamed x8, local copies, waits for them, and re-layouts  1.41 us
  transfers between devices with their start and end apart: 9, of which 9 were waited for; matrix products, arithmetic and copies ran while one was open for 0% of the time, Pallas kernels for 0%

profile of v9, /device:TPU:0, one launch (start us, length us, event | category | flops | bytes accessed | tf_op | source)
XLA Modules:
  0.0 52.7 jit_solution(4185048475732276416)
XLA Ops:
  0.6 0.0 copy-start.1
  1.3 4.1 %rhs.3 = (bf16[32,4,128,128]{3,2,1,0:T(8,128)(2,1)S(1)}, f32[24,32,128]{2,1,0:T(8,128)S(1)}, bf16[272,128]{1,0:T(8,128)(2,1)S(1)}, bf16[272,128]{1,0:T(8,128)(2,1)S(1)}) custom-call(s32[1]{0:T(128)} %bitcast.2.place_ref, s32[1]{0:T(128)} %bitcast.3.lane_ref, s32[1]{0:T(128)S(6)} %copy.39.live_ref, s32[4,32]{1,0:T(4,128)} %bitcast.40, ...), custom_call_target="tpu_custom_call" | custom-call | tf_op jit(solution)/shard_map/rhs/pallas_call | solution.py:342
  5.5 0.0 copy-start
  5.5 3.0 %collective-permute-start.2 = (bf16[272,128]{1,0:T(8,128)(2,1)S(1)}, bf16[272,128]{1,0:T(8,128)(2,1)S(1)}, u32[]{:S(2)}, u32[]{:S(2)}) collective-permute-start(bf16[272,128]{1,0:T(8,128)(2,1)S(1)} %get-tuple-element.237), channel_id=1, source_target_pairs={{0,4},{4,8},{8,12},{12,16},{16,20},{20,24},{24,28},{28,29},{29,25}... | collective-permute-start | bytes 208904 | tf_op jit(solution)/shard_map/ppermute | solution.py:339
  8.5 0.0 collective-permute-start.3
  8.5 2.3 %collective-permute-done.2.onward_in_ref = bf16[272,128]{1,0:T(8,128)(2,1)S(1)} collective-permute-done((bf16[272,128]{1,0:T(8,128)(2,1)S(1)}, bf16[272,128]{1,0:T(8,128)(2,1)S(1)}, u32[]{:S(2)}, u32[]{:S(2)}) %collective-permute-start.2) | collective-permute-done | bytes 69664 | tf_op jit(solution)/shard_map/ppermute | solution.py:339
  10.8 2.0 %collective-permute-done.3.return_in_ref = bf16[272,128]{1,0:T(8,128)(2,1)S(1)} collective-permute-done((bf16[272,128]{1,0:T(8,128)(2,1)S(1)}, bf16[272,128]{1,0:T(8,128)(2,1)S(1)}, u32[]{:S(2)}, u32[]{:S(2)}) %collective-permute-start.3) | collective-permute-done | bytes 69664 | tf_op jit(solution)/shard_map/ppermute | solution.py:339
  12.8 0.0 copy-done.1
  12.8 3.4 %step0.1 = (f32[24,32,128]{2,1,0:T(8,128)S(1)}, f32[24,32,128]{2,1,0:T(8,128)S(1)}, bf16[272,128]{1,0:T(8,128)(2,1)S(1)}, bf16[272,128]{1,0:T(8,128)(2,1)S(1)}, f32[8,128]{1,0:T(8,128)S(1)}) custom-call(s32[1]{0:T(128)} %bitcast.2.place_ref, s32[1]{0:T(128)} %bitcast.3.lane_ref, s32[1]{0:T(128)S(6)} %copy.39.live_ref, s32[4,32]{1,0:T(4,128)S(1)} %bitcast.41, ...), custom_call_target="tpu_custom_call" | custom-call | tf_op jit(solution)/shard_map/step0/pallas_call | solution.py:373
  16.2 2.5 %collective-permute-start.4 = (bf16[272,128]{1,0:T(8,128)(2,1)S(1)}, bf16[272,128]{1,0:T(8,128)(2,1)S(1)}, u32[]{:S(2)}, u32[]{:S(2)}) collective-permute-start(bf16[272,128]{1,0:T(8,128)(2,1)S(1)} %get-tuple-element.241), channel_id=1, source_target_pairs={{0,4},{4,8},{8,12},{12,16},{16,20},{20,24},{24,28},{28,29},{29,25}... | collective-permute-start | bytes 208904 | tf_op jit(solution)/shard_map/ppermute | solution.py:339
  18.7 0.0 collective-permute-start.5
  18.7 1.9 %collective-permute-done.4.onward_in_ref = bf16[272,128]{1,0:T(8,128)(2,1)S(1)} collective-permute-done((bf16[272,128]{1,0:T(8,128)(2,1)S(1)}, bf16[272,128]{1,0:T(8,128)(2,1)S(1)}, u32[]{:S(2)}, u32[]{:S(2)}) %collective-permute-start.4) | collective-permute-done | bytes 69664 | tf_op jit(solution)/shard_map/ppermute | solution.py:339
  20.6 2.4 %collective-permute-done.5.return_in_ref = bf16[272,128]{1,0:T(8,128)(2,1)S(1)} collective-permute-done((bf16[272,128]{1,0:T(8,128)(2,1)S(1)}, bf16[272,128]{1,0:T(8,128)(2,1)S(1)}, u32[]{:S(2)}, u32[]{:S(2)}) %collective-permute-start.5) | collective-permute-done | bytes 69664 | tf_op jit(solution)/shard_map/ppermute | solution.py:339
  23.0 3.4 %step1.1 = (f32[24,32,128]{2,1,0:T(8,128)S(1)}, f32[24,32,128]{2,1,0:T(8,128)S(1)}, bf16[272,128]{1,0:T(8,128)(2,1)S(1)}, bf16[272,128]{1,0:T(8,128)(2,1)S(1)}, f32[8,128]{1,0:T(8,128)S(1)}) custom-call(s32[1]{0:T(128)} %bitcast.2.place_ref, s32[1]{0:T(128)} %bitcast.3.lane_ref, s32[1]{0:T(128)S(6)} %copy.39.live_ref, s32[4,32]{1,0:T(4,128)S(1)} %bitcast.42, ...), custom_call_target="tpu_custom_call" | custom-call | tf_op jit(solution)/shard_map/step1/pallas_call | solution.py:373
  26.4 2.4 %collective-permute-start.6 = (bf16[272,128]{1,0:T(8,128)(2,1)S(1)}, bf16[272,128]{1,0:T(8,128)(2,1)S(1)}, u32[]{:S(2)}, u32[]{:S(2)}) collective-permute-start(bf16[272,128]{1,0:T(8,128)(2,1)S(1)} %get-tuple-element.245), channel_id=1, source_target_pairs={{0,4},{4,8},{8,12},{12,16},{16,20},{20,24},{24,28},{28,29},{29,25}... | collective-permute-start | bytes 208904 | tf_op jit(solution)/shard_map/ppermute | solution.py:339
  28.8 0.0 collective-permute-start.7
  28.8 1.9 %collective-permute-done.6.onward_in_ref = bf16[272,128]{1,0:T(8,128)(2,1)S(1)} collective-permute-done((bf16[272,128]{1,0:T(8,128)(2,1)S(1)}, bf16[272,128]{1,0:T(8,128)(2,1)S(1)}, u32[]{:S(2)}, u32[]{:S(2)}) %collective-permute-start.6) | collective-permute-done | bytes 69664 | tf_op jit(solution)/shard_map/ppermute | solution.py:339
  30.8 2.4 %collective-permute-done.7.return_in_ref = bf16[272,128]{1,0:T(8,128)(2,1)S(1)} collective-permute-done((bf16[272,128]{1,0:T(8,128)(2,1)S(1)}, bf16[272,128]{1,0:T(8,128)(2,1)S(1)}, u32[]{:S(2)}, u32[]{:S(2)}) %collective-permute-start.7) | collective-permute-done | bytes 69664 | tf_op jit(solution)/shard_map/ppermute | solution.py:339
  33.1 0.0 copy-done
  33.1 3.8 %step2.1 = (f32[24,32,128]{2,1,0:T(8,128)S(1)}, f32[24,32,128]{2,1,0:T(8,128)S(1)}, bf16[144,128]{1,0:T(8,128)(2,1)S(1)}, bf16[144,128]{1,0:T(8,128)(2,1)S(1)}, f32[32,8,128]{2,1,0:T(8,128)}) custom-call(s32[1]{0:T(128)} %bitcast.2.place_ref, s32[1]{0:T(128)} %bitcast.3.lane_ref, s32[1]{0:T(128)S(6)} %copy.39.live_ref, s32[4,32]{1,0:T(4,128)S(1)} %bitcast.43, ...), custom_call_target="tpu_custom_call" | custom-call | tf_op jit(solution)/shard_map/step2/pallas_call | solution.py:373
  37.0 4.3 %all-to-all-start = ((f32[32,8,128]{2,1,0:T(8,128)}), f32[32,8,128]{2,1,0:T(8,128)S(1)}, u32[]{:S(2)}, u32[]{:S(2)}) async-start(f32[32,8,128]{2,1,0:T(8,128)} %get-tuple-element.248), calls=%async_computation | async-start | bytes 262144 | tf_op jit(solution)/shard_map/all_to_all | solution.py:384
  41.3 1.8 %collective-permute-start.8 = (bf16[144,128]{1,0:T(8,128)(2,1)S(1)}, bf16[144,128]{1,0:T(8,128)(2,1)S(1)}, u32[]{:S(2)}, u32[]{:S(2)}) collective-permute-start(bf16[144,128]{1,0:T(8,128)(2,1)S(1)} %get-tuple-element.253), channel_id=1, source_target_pairs={{0,4},{4,8},{8,12},{12,16},{16,20},{20,24},{24,28},{28,29},{29,25}... | collective-permute-start | bytes 110600 | tf_op jit(solution)/shard_map/ppermute | solution.py:339
  43.1 0.0 collective-permute-start.9
  43.1 1.9 %collective-permute-done.8.onward_in_ref = bf16[144,128]{1,0:T(8,128)(2,1)S(1)} collective-permute-done((bf16[144,128]{1,0:T(8,128)(2,1)S(1)}, bf16[144,128]{1,0:T(8,128)(2,1)S(1)}, u32[]{:S(2)}, u32[]{:S(2)}) %collective-permute-start.8) | collective-permute-done | bytes 36896 | tf_op jit(solution)/shard_map/ppermute | solution.py:339
  45.0 2.2 %collective-permute-done.9.return_in_ref = bf16[144,128]{1,0:T(8,128)(2,1)S(1)} collective-permute-done((bf16[144,128]{1,0:T(8,128)(2,1)S(1)}, bf16[144,128]{1,0:T(8,128)(2,1)S(1)}, u32[]{:S(2)}, u32[]{:S(2)}) %collective-permute-start.9) | collective-permute-done | bytes 36896 | tf_op jit(solution)/shard_map/ppermute | solution.py:339
  47.2 2.3 %all-to-all-done.moments_ref = f32[32,8,128]{2,1,0:T(8,128)S(1)} async-done(((f32[32,8,128]{2,1,0:T(8,128)}), f32[32,8,128]{2,1,0:T(8,128)S(1)}, u32[]{:S(2)}, u32[]{:S(2)}) %all-to-all-start) | async-done | bytes 131104 | tf_op jit(solution)/shard_map/all_to_all | solution.py:384
  49.5 0.9 %combine.1 = (f32[32,16,128]{2,1,0:T(8,128)S(1)}, f32[32,16,128]{2,1,0:T(8,128)S(1)}, s32[1]{0:T(128)}) custom-call(s32[1]{0:T(128)} %bitcast.2.place_ref, s32[1]{0:T(128)} %bitcast.3.lane_ref, f32[32,8,128]{2,1,0:T(8,128)S(1)} %all-to-all-done.moments_ref, f32[24,32,128]{2,1,0:T(8,128)S(1)} %get-tuple-element.249.first_ref, ...), custom_call_target="tpu_custom_call" | custom-call | tf_op jit(solution)/shard_map/combine/pallas_call | solution.py:386
  51.1 0.2 conditional.1
  51.3 0.0 copy-start.2
  51.3 0.7 %copy-done.2 = f32[32,16,128]{2,1,0:T(8,128)} copy-done((f32[32,16,128]{2,1,0:T(8,128)}, f32[32,16,128]{2,1,0:T(8,128)S(1)}, u32[]{:S(2)}) %copy-start.2) | copy-done | bytes 262168
  52.0 0.0 copy-start.3
  52.0 0.7 %copy-done.3 = f32[32,16,128]{2,1,0:T(8,128)} copy-done((f32[32,16,128]{2,1,0:T(8,128)}, f32[32,16,128]{2,1,0:T(8,128)S(1)}, u32[]{:S(2)}) %copy-start.3) | copy-done | bytes 262168
  (1 shorter events, 0.0 us)
Async XLA Ops:
  0.6 12.2 %copy-start.1 = (s32[1,32,4]{1,2,0:T(4,128)S(1)}, s32[1,32,4]{1,2,0:T(4,128)}, u32[]{:S(2)}) copy-start(s32[1,32,4]{1,2,0:T(4,128)} %param.14) | copy-start | bytes 1540
  5.5 27.7 %copy-start = (bf16[32,4,128,128]{3,2,1,0:T(8,128)(2,1)}, bf16[32,4,128,128]{3,2,1,0:T(8,128)(2,1)S(1)}, u32[]{:S(2)}) copy-start(bf16[32,4,128,128]{3,2,1,0:T(8,128)(2,1)S(1)} %get-tuple-element.239.kernels_ref) | copy-start | bytes 12582916
  5.5 5.4 %collective-permute-start.2 = (bf16[272,128]{1,0:T(8,128)(2,1)S(1)}, bf16[272,128]{1,0:T(8,128)(2,1)S(1)}, u32[]{:S(2)}, u32[]{:S(2)}) collective-permute-start(bf16[272,128]{1,0:T(8,128)(2,1)S(1)} %get-tuple-element.237), channel_id=1, source_target_pairs={{0,4},{4,8},{8,12},{12,16},{16,20},{20,24},{24,28},{28,29},{29,25}... | collective-permute-start | bytes 208904 | tf_op jit(solution)/shard_map/ppermute | solution.py:339
  8.5 4.3 %collective-permute-start.3 = (bf16[272,128]{1,0:T(8,128)(2,1)S(1)}, bf16[272,128]{1,0:T(8,128)(2,1)S(1)}, u32[]{:S(2)}, u32[]{:S(2)}) collective-permute-start(bf16[272,128]{1,0:T(8,128)(2,1)S(1)} %get-tuple-element.238), channel_id=1, source_target_pairs={{4,0},{8,4},{12,8},{16,12},{20,16},{24,20},{28,24},{29,28},{25,29}... | collective-permute-start | bytes 208904 | tf_op jit(solution)/shard_map/ppermute | solution.py:339
  16.2 4.5 %collective-permute-start.4 = (bf16[272,128]{1,0:T(8,128)(2,1)S(1)}, bf16[272,128]{1,0:T(8,128)(2,1)S(1)}, u32[]{:S(2)}, u32[]{:S(2)}) collective-permute-start(bf16[272,128]{1,0:T(8,128)(2,1)S(1)} %get-tuple-element.241), channel_id=1, source_target_pairs={{0,4},{4,8},{8,12},{12,16},{16,20},{20,24},{24,28},{28,29},{29,25}... | collective-permute-start | bytes 208904 | tf_op jit(solution)/shard_map/ppermute | solution.py:339
  18.7 4.3 %collective-permute-start.5 = (bf16[272,128]{1,0:T(8,128)(2,1)S(1)}, bf16[272,128]{1,0:T(8,128)(2,1)S(1)}, u32[]{:S(2)}, u32[]{:S(2)}) collective-permute-start(bf16[272,128]{1,0:T(8,128)(2,1)S(1)} %get-tuple-element.242), channel_id=1, source_target_pairs={{4,0},{8,4},{12,8},{16,12},{20,16},{24,20},{28,24},{29,28},{25,29}... | collective-permute-start | bytes 208904 | tf_op jit(solution)/shard_map/ppermute | solution.py:339
  26.4 4.4 %collective-permute-start.6 = (bf16[272,128]{1,0:T(8,128)(2,1)S(1)}, bf16[272,128]{1,0:T(8,128)(2,1)S(1)}, u32[]{:S(2)}, u32[]{:S(2)}) collective-permute-start(bf16[272,128]{1,0:T(8,128)(2,1)S(1)} %get-tuple-element.245), channel_id=1, source_target_pairs={{0,4},{4,8},{8,12},{12,16},{16,20},{20,24},{24,28},{28,29},{29,25}... | collective-permute-start | bytes 208904 | tf_op jit(solution)/shard_map/ppermute | solution.py:339
  28.8 4.3 %collective-permute-start.7 = (bf16[272,128]{1,0:T(8,128)(2,1)S(1)}, bf16[272,128]{1,0:T(8,128)(2,1)S(1)}, u32[]{:S(2)}, u32[]{:S(2)}) collective-permute-start(bf16[272,128]{1,0:T(8,128)(2,1)S(1)} %get-tuple-element.246), channel_id=1, source_target_pairs={{4,0},{8,4},{12,8},{16,12},{20,16},{24,20},{28,24},{29,28},{25,29}... | collective-permute-start | bytes 208904 | tf_op jit(solution)/shard_map/ppermute | solution.py:339
  37.0 12.5 %all-to-all-start = ((f32[32,8,128]{2,1,0:T(8,128)}), f32[32,8,128]{2,1,0:T(8,128)S(1)}, u32[]{:S(2)}, u32[]{:S(2)}) async-start(f32[32,8,128]{2,1,0:T(8,128)} %get-tuple-element.248), calls=%async_computation | async-start | bytes 262144 | tf_op jit(solution)/shard_map/all_to_all | solution.py:384
  41.3 3.8 %collective-permute-start.8 = (bf16[144,128]{1,0:T(8,128)(2,1)S(1)}, bf16[144,128]{1,0:T(8,128)(2,1)S(1)}, u32[]{:S(2)}, u32[]{:S(2)}) collective-permute-start(bf16[144,128]{1,0:T(8,128)(2,1)S(1)} %get-tuple-element.253), channel_id=1, source_target_pairs={{0,4},{4,8},{8,12},{12,16},{16,20},{20,24},{24,28},{28,29},{29,25}... | collective-permute-start | bytes 110600 | tf_op jit(solution)/shard_map/ppermute | solution.py:339
  43.1 4.1 %collective-permute-start.9 = (bf16[144,128]{1,0:T(8,128)(2,1)S(1)}, bf16[144,128]{1,0:T(8,128)(2,1)S(1)}, u32[]{:S(2)}, u32[]{:S(2)}) collective-permute-start(bf16[144,128]{1,0:T(8,128)(2,1)S(1)} %get-tuple-element.254), channel_id=1, source_target_pairs={{4,0},{8,4},{12,8},{16,12},{20,16},{24,20},{28,24},{29,28},{25,29}... | collective-permute-start | bytes 110600 | tf_op jit(solution)/shard_map/ppermute | solution.py:339
  51.3 0.7 %copy-start.2 = (f32[32,16,128]{2,1,0:T(8,128)}, f32[32,16,128]{2,1,0:T(8,128)S(1)}, u32[]{:S(2)}) copy-start(f32[32,16,128]{2,1,0:T(8,128)S(1)} %get-tuple-element.535) | copy-start | bytes 786436
  52.0 0.7 %copy-start.3 = (f32[32,16,128]{2,1,0:T(8,128)}, f32[32,16,128]{2,1,0:T(8,128)S(1)}, u32[]{:S(2)}) copy-start(f32[32,16,128]{2,1,0:T(8,128)S(1)} %get-tuple-element.537) | copy-start | bytes 786436

commit v10 on v9

--- a/solution.py
+++ b/solution.py
@@ -257,6 +257,9 @@
     residual_ref,
     flag_ref,
     last_ref,
+    solution_buf,
+    residual_buf,
+    sems,
 ):
     sums = moments_ref[0]
     for source in range(1, moments_ref.shape[0]):
@@ -284,19 +287,26 @@
     last_ref[...] = held_ref[pl.ds(HALO_BLOCKS, BLOCKS_DEV)]
     add_rims(tiles, place_ref, lane_ref, last_ref, onward_in_ref, return_in_ref)
     for block in range(BLOCKS_DEV):
-        first = first_ref[HALO_BLOCKS + block]
-        second = second_ref[HALO_BLOCKS + block]
-        third = third_ref[HALO_BLOCKS + block]
-        last = last_ref[block]
-        solution_ref[:, block, :] = (
-            answer_scaled[0] * first + answer_scaled[1] * second + answer_scaled[2] * third
+        inside = HALO_BLOCKS + block
+        solution_buf[:, block, :] = (
+            answer_scaled[0] * first_ref[inside]
+            + answer_scaled[1] * second_ref[inside]
+            + answer_scaled[2] * third_ref[inside]
         )
-        residual_ref[:, block, :] = (
-            first
-            + residual_scaled[1] * second
-            + residual_scaled[2] * third
-            + residual_scaled[3] * last
+    solution_copy = pltpu.make_async_copy(solution_buf, solution_ref, sems.at[0])
+    solution_copy.start()
+    for block in range(BLOCKS_DEV):
+        inside = HALO_BLOCKS + block
+        residual_buf[:, block, :] = (
+            first_ref[inside]
+            + residual_scaled[1] * second_ref[inside]
+            + residual_scaled[2] * third_ref[inside]
+            + residual_scaled[3] * last_ref[block]
         )
+    residual_copy = pltpu.make_async_copy(residual_buf, residual_ref, sems.at[1])
+    residual_copy.start()
+    solution_copy.wait()
+    residual_copy.wait()
 
 
 def vmem(count):
@@ -356,7 +366,7 @@
         place,
         lane,
         live_count,
-        index,
+        pltpu.with_memory_space_constraint(index, pltpu.HBM),
         pltpu.with_memory_space_constraint(fibre_data, pltpu.HBM),
         pltpu.with_memory_space_constraint(weights, pltpu.HBM),
     )
@@ -382,13 +392,18 @@
         vectors.append(vector)
     onward, back = swap(onward, back)
     moments = lax.all_to_all(moments, ("tile", "wave"), 0, 0)
-    out = jax.ShapeDtypeStruct((waves, BLOCKS_DEV, spaxels), jnp.float32)
+    out = pltpu.HBM((waves, BLOCKS_DEV, spaxels), jnp.float32)
     answer, residual, steady = pl.pallas_call(
         functools.partial(final_kernel, tiles),
         out_shape=(out, out, jax.ShapeDtypeStruct((1,), jnp.int32)),
         in_specs=smem(2) + vmem(7),
-        out_specs=tuple(vmem(2) + smem(1)),
-        scratch_shapes=[pltpu.VMEM((BLOCKS_DEV, waves, spaxels), jnp.float32)],
+        out_specs=tuple([pl.BlockSpec(memory_space=pltpu.HBM)] * 2 + smem(1)),
+        scratch_shapes=[
+            pltpu.VMEM((BLOCKS_DEV, waves, spaxels), jnp.float32),
+            pltpu.VMEM((waves, BLOCKS_DEV, spaxels), jnp.float32),
+            pltpu.VMEM((waves, BLOCKS_DEV, spaxels), jnp.float32),
+            pltpu.SemaphoreType.DMA((2,)),
+        ],
         compiler_params=params,
         name="combine",
     )(place, lane, moments, *vectors, held, onward, back)

time: 53 us -> 52.6 us (level)
  local copies, waits for them, and re-layouts: 1.41 us -> 0.01 us
  Pallas kernels: 15.7 us -> 16.6 us
    unnamed x8 -> x4, local copies, waits for them, and re-layouts: 1.41 us -> 0.01 us
    pallas_call x1, Pallas kernels: 0.94 us -> 1.88 us  [shards(): pl.pallas_call(functools.partial(final_kernel, tiles), out_shape=(out, ou...]
where the time goes in v10:
time: 52.6 us; the launch traced here: 52.4 us
  waiting for transfers between devices  19.3 us (37%)
  Pallas kernels  16.6 us (32%)
  starting transfers between devices  14.1 us (27%)
  between operations  2.12 us (4%)
    pallas_call x3, Pallas kernels, shards(): pl.pallas_call(functools.partial(step_kernel, tiles, power, final), out_s...  10.6 us
    ppermute x4, starting transfers between devices, swap(): lax.ppermute(onward, axes, circuit)  9.77 us
    ppermute x4, waiting for transfers between devices, swap(): lax.ppermute(back, axes, reverse)  8.85 us
    ppermute x4, waiting for transfers between devices, swap(): lax.ppermute(onward, axes, circuit)  8.15 us
    all_to_all x1, starting transfers between devices, shards(): moments = lax.all_to_all(moments, ('tile', 'wave'), 0, 0)  4.31 us
    pallas_call x1, Pallas kernels, shards(): pl.pallas_call(rhs_kernel, out_shape=(jax.ShapeDtypeStruct(weights.shape,...  4.15 us
    all_to_all x1, waiting for transfers between devices, shards(): moments = lax.all_to_all(moments, ('tile', 'wave'), 0, 0)  2.29 us
    pallas_call x1, Pallas kernels, shards(): pl.pallas_call(functools.partial(final_kernel, tiles), out_shape=(out, ou...  1.88 us
  transfers between devices with their start and end apart: 9, of which 9 were waited for; matrix products, arithmetic and copies ran while one was open for 0% of the time, Pallas kernels for 0%

profile of v10, /device:TPU:0, one launch (start us, length us, event | category | flops | bytes accessed | tf_op | source)
XLA Modules:
  0.0 52.4 jit_solution(398337059293571570)
XLA Ops:
  0.6 0.0 copy-start.1
  1.3 4.2 %rhs.3 = (bf16[32,4,128,128]{3,2,1,0:T(8,128)(2,1)S(1)}, f32[24,32,128]{2,1,0:T(8,128)S(1)}, bf16[272,128]{1,0:T(8,128)(2,1)S(1)}, bf16[272,128]{1,0:T(8,128)(2,1)S(1)}) custom-call(s32[1]{0:T(128)} %bitcast.2.place_ref, s32[1]{0:T(128)} %bitcast.3.lane_ref, s32[1]{0:T(128)S(6)} %copy.39.live_ref, s32[4,32]{1,0:T(4,128)} %bitcast.40, ...), custom_call_target="tpu_custom_call" | custom-call | tf_op jit(solution)/shard_map/rhs/pallas_call | solution.py:352
  5.5 0.0 copy-start
  5.5 3.0 %collective-permute-start.2 = (bf16[272,128]{1,0:T(8,128)(2,1)S(1)}, bf16[272,128]{1,0:T(8,128)(2,1)S(1)}, u32[]{:S(2)}, u32[]{:S(2)}) collective-permute-start(bf16[272,128]{1,0:T(8,128)(2,1)S(1)} %get-tuple-element.237), channel_id=1, source_target_pairs={{0,4},{4,8},{8,12},{12,16},{16,20},{20,24},{24,28},{28,29},{29,25}... | collective-permute-start | bytes 208904 | tf_op jit(solution)/shard_map/ppermute | solution.py:349
  8.5 0.0 collective-permute-start.3
  8.5 2.3 %collective-permute-done.2.onward_in_ref = bf16[272,128]{1,0:T(8,128)(2,1)S(1)} collective-permute-done((bf16[272,128]{1,0:T(8,128)(2,1)S(1)}, bf16[272,128]{1,0:T(8,128)(2,1)S(1)}, u32[]{:S(2)}, u32[]{:S(2)}) %collective-permute-start.2) | collective-permute-done | bytes 69664 | tf_op jit(solution)/shard_map/ppermute | solution.py:349
  10.8 2.0 %collective-permute-done.3.return_in_ref = bf16[272,128]{1,0:T(8,128)(2,1)S(1)} collective-permute-done((bf16[272,128]{1,0:T(8,128)(2,1)S(1)}, bf16[272,128]{1,0:T(8,128)(2,1)S(1)}, u32[]{:S(2)}, u32[]{:S(2)}) %collective-permute-start.3) | collective-permute-done | bytes 69664 | tf_op jit(solution)/shard_map/ppermute | solution.py:349
  12.8 0.0 copy-done.1
  12.8 3.4 %step0.1 = (f32[24,32,128]{2,1,0:T(8,128)S(1)}, f32[24,32,128]{2,1,0:T(8,128)S(1)}, bf16[272,128]{1,0:T(8,128)(2,1)S(1)}, bf16[272,128]{1,0:T(8,128)(2,1)S(1)}, f32[8,128]{1,0:T(8,128)S(1)}) custom-call(s32[1]{0:T(128)} %bitcast.2.place_ref, s32[1]{0:T(128)} %bitcast.3.lane_ref, s32[1]{0:T(128)S(6)} %copy.39.live_ref, s32[4,32]{1,0:T(4,128)S(1)} %bitcast.41, ...), custom_call_target="tpu_custom_call" | custom-call | tf_op jit(solution)/shard_map/step0/pallas_call | solution.py:383
  16.2 2.5 %collective-permute-start.4 = (bf16[272,128]{1,0:T(8,128)(2,1)S(1)}, bf16[272,128]{1,0:T(8,128)(2,1)S(1)}, u32[]{:S(2)}, u32[]{:S(2)}) collective-permute-start(bf16[272,128]{1,0:T(8,128)(2,1)S(1)} %get-tuple-element.241), channel_id=1, source_target_pairs={{0,4},{4,8},{8,12},{12,16},{16,20},{20,24},{24,28},{28,29},{29,25}... | collective-permute-start | bytes 208904 | tf_op jit(solution)/shard_map/ppermute | solution.py:349
  18.7 0.0 collective-permute-start.5
  18.7 1.9 %collective-permute-done.4.onward_in_ref = bf16[272,128]{1,0:T(8,128)(2,1)S(1)} collective-permute-done((bf16[272,128]{1,0:T(8,128)(2,1)S(1)}, bf16[272,128]{1,0:T(8,128)(2,1)S(1)}, u32[]{:S(2)}, u32[]{:S(2)}) %collective-permute-start.4) | collective-permute-done | bytes 69664 | tf_op jit(solution)/shard_map/ppermute | solution.py:349
  20.6 2.4 %collective-permute-done.5.return_in_ref = bf16[272,128]{1,0:T(8,128)(2,1)S(1)} collective-permute-done((bf16[272,128]{1,0:T(8,128)(2,1)S(1)}, bf16[272,128]{1,0:T(8,128)(2,1)S(1)}, u32[]{:S(2)}, u32[]{:S(2)}) %collective-permute-start.5) | collective-permute-done | bytes 69664 | tf_op jit(solution)/shard_map/ppermute | solution.py:349
  23.0 3.4 %step1.1 = (f32[24,32,128]{2,1,0:T(8,128)S(1)}, f32[24,32,128]{2,1,0:T(8,128)S(1)}, bf16[272,128]{1,0:T(8,128)(2,1)S(1)}, bf16[272,128]{1,0:T(8,128)(2,1)S(1)}, f32[8,128]{1,0:T(8,128)S(1)}) custom-call(s32[1]{0:T(128)} %bitcast.2.place_ref, s32[1]{0:T(128)} %bitcast.3.lane_ref, s32[1]{0:T(128)S(6)} %copy.39.live_ref, s32[4,32]{1,0:T(4,128)S(1)} %bitcast.42, ...), custom_call_target="tpu_custom_call" | custom-call | tf_op jit(solution)/shard_map/step1/pallas_call | solution.py:383
  26.4 2.4 %collective-permute-start.6 = (bf16[272,128]{1,0:T(8,128)(2,1)S(1)}, bf16[272,128]{1,0:T(8,128)(2,1)S(1)}, u32[]{:S(2)}, u32[]{:S(2)}) collective-permute-start(bf16[272,128]{1,0:T(8,128)(2,1)S(1)} %get-tuple-element.245), channel_id=1, source_target_pairs={{0,4},{4,8},{8,12},{12,16},{16,20},{20,24},{24,28},{28,29},{29,25}... | collective-permute-start | bytes 208904 | tf_op jit(solution)/shard_map/ppermute | solution.py:349
  28.8 0.0 collective-permute-start.7
  28.8 1.9 %collective-permute-done.6.onward_in_ref = bf16[272,128]{1,0:T(8,128)(2,1)S(1)} collective-permute-done((bf16[272,128]{1,0:T(8,128)(2,1)S(1)}, bf16[272,128]{1,0:T(8,128)(2,1)S(1)}, u32[]{:S(2)}, u32[]{:S(2)}) %collective-permute-start.6) | collective-permute-done | bytes 69664 | tf_op jit(solution)/shard_map/ppermute | solution.py:349
  30.8 2.4 %collective-permute-done.7.return_in_ref = bf16[272,128]{1,0:T(8,128)(2,1)S(1)} collective-permute-done((bf16[272,128]{1,0:T(8,128)(2,1)S(1)}, bf16[272,128]{1,0:T(8,128)(2,1)S(1)}, u32[]{:S(2)}, u32[]{:S(2)}) %collective-permute-start.7) | collective-permute-done | bytes 69664 | tf_op jit(solution)/shard_map/ppermute | solution.py:349
  33.1 0.0 copy-done
  33.1 3.8 %step2.1 = (f32[24,32,128]{2,1,0:T(8,128)S(1)}, f32[24,32,128]{2,1,0:T(8,128)S(1)}, bf16[144,128]{1,0:T(8,128)(2,1)S(1)}, bf16[144,128]{1,0:T(8,128)(2,1)S(1)}, f32[32,8,128]{2,1,0:T(8,128)}) custom-call(s32[1]{0:T(128)} %bitcast.2.place_ref, s32[1]{0:T(128)} %bitcast.3.lane_ref, s32[1]{0:T(128)S(6)} %copy.39.live_ref, s32[4,32]{1,0:T(4,128)S(1)} %bitcast.43, ...), custom_call_target="tpu_custom_call" | custom-call | tf_op jit(solution)/shard_map/step2/pallas_call | solution.py:383
  37.0 4.3 %all-to-all-start = ((f32[32,8,128]{2,1,0:T(8,128)}), f32[32,8,128]{2,1,0:T(8,128)S(1)}, u32[]{:S(2)}, u32[]{:S(2)}) async-start(f32[32,8,128]{2,1,0:T(8,128)} %get-tuple-element.248), calls=%async_computation | async-start | bytes 262144 | tf_op jit(solution)/shard_map/all_to_all | solution.py:394
  41.3 1.8 %collective-permute-start.8 = (bf16[144,128]{1,0:T(8,128)(2,1)S(1)}, bf16[144,128]{1,0:T(8,128)(2,1)S(1)}, u32[]{:S(2)}, u32[]{:S(2)}) collective-permute-start(bf16[144,128]{1,0:T(8,128)(2,1)S(1)} %get-tuple-element.253), channel_id=1, source_target_pairs={{0,4},{4,8},{8,12},{12,16},{16,20},{20,24},{24,28},{28,29},{29,25}... | collective-permute-start | bytes 110600 | tf_op jit(solution)/shard_map/ppermute | solution.py:349
  43.1 0.0 collective-permute-start.9
  43.1 1.9 %collective-permute-done.8.onward_in_ref = bf16[144,128]{1,0:T(8,128)(2,1)S(1)} collective-permute-done((bf16[144,128]{1,0:T(8,128)(2,1)S(1)}, bf16[144,128]{1,0:T(8,128)(2,1)S(1)}, u32[]{:S(2)}, u32[]{:S(2)}) %collective-permute-start.8) | collective-permute-done | bytes 36896 | tf_op jit(solution)/shard_map/ppermute | solution.py:349
  45.0 2.2 %collective-permute-done.9.return_in_ref = bf16[144,128]{1,0:T(8,128)(2,1)S(1)} collective-permute-done((bf16[144,128]{1,0:T(8,128)(2,1)S(1)}, bf16[144,128]{1,0:T(8,128)(2,1)S(1)}, u32[]{:S(2)}, u32[]{:S(2)}) %collective-permute-start.9) | collective-permute-done | bytes 36896 | tf_op jit(solution)/shard_map/ppermute | solution.py:349
  47.2 2.3 %all-to-all-done.moments_ref = f32[32,8,128]{2,1,0:T(8,128)S(1)} async-done(((f32[32,8,128]{2,1,0:T(8,128)}), f32[32,8,128]{2,1,0:T(8,128)S(1)}, u32[]{:S(2)}, u32[]{:S(2)}) %all-to-all-start) | async-done | bytes 131104 | tf_op jit(solution)/shard_map/all_to_all | solution.py:394
  49.5 1.9 %combine.1 = (f32[32,16,128]{2,1,0:T(8,128)}, f32[32,16,128]{2,1,0:T(8,128)}, s32[1]{0:T(128)}) custom-call(s32[1]{0:T(128)} %bitcast.2.place_ref, s32[1]{0:T(128)} %bitcast.3.lane_ref, f32[32,8,128]{2,1,0:T(8,128)S(1)} %all-to-all-done.moments_ref, f32[24,32,128]{2,1,0:T(8,128)S(1)} %get-tuple-element.249.first_ref, ...), custom_call_target="tpu_custom_call" | custom-call | tf_op jit(solution)/shard_map/combine/pallas_call | solution.py:396
  52.0 0.2 conditional.1
  (1 shorter events, 0.0 us)
Async XLA Ops:
  0.6 12.2 %copy-start.1 = (s32[1,32,4]{1,2,0:T(4,128)S(1)}, s32[1,32,4]{1,2,0:T(4,128)}, u32[]{:S(2)}) copy-start(s32[1,32,4]{1,2,0:T(4,128)} %param.14) | copy-start | bytes 1540
  5.5 27.7 %copy-start = (bf16[32,4,128,128]{3,2,1,0:T(8,128)(2,1)}, bf16[32,4,128,128]{3,2,1,0:T(8,128)(2,1)S(1)}, u32[]{:S(2)}) copy-start(bf16[32,4,128,128]{3,2,1,0:T(8,128)(2,1)S(1)} %get-tuple-element.239.kernels_ref) | copy-start | bytes 12582916
  5.5 5.4 %collective-permute-start.2 = (bf16[272,128]{1,0:T(8,128)(2,1)S(1)}, bf16[272,128]{1,0:T(8,128)(2,1)S(1)}, u32[]{:S(2)}, u32[]{:S(2)}) collective-permute-start(bf16[272,128]{1,0:T(8,128)(2,1)S(1)} %get-tuple-element.237), channel_id=1, source_target_pairs={{0,4},{4,8},{8,12},{12,16},{16,20},{20,24},{24,28},{28,29},{29,25}... | collective-permute-start | bytes 208904 | tf_op jit(solution)/shard_map/ppermute | solution.py:349
  8.5 4.3 %collective-permute-start.3 = (bf16[272,128]{1,0:T(8,128)(2,1)S(1)}, bf16[272,128]{1,0:T(8,128)(2,1)S(1)}, u32[]{:S(2)}, u32[]{:S(2)}) collective-permute-start(bf16[272,128]{1,0:T(8,128)(2,1)S(1)} %get-tuple-element.238), channel_id=1, source_target_pairs={{4,0},{8,4},{12,8},{16,12},{20,16},{24,20},{28,24},{29,28},{25,29}... | collective-permute-start | bytes 208904 | tf_op jit(solution)/shard_map/ppermute | solution.py:349
  16.2 4.4 %collective-permute-start.4 = (bf16[272,128]{1,0:T(8,128)(2,1)S(1)}, bf16[272,128]{1,0:T(8,128)(2,1)S(1)}, u32[]{:S(2)}, u32[]{:S(2)}) collective-permute-start(bf16[272,128]{1,0:T(8,128)(2,1)S(1)} %get-tuple-element.241), channel_id=1, source_target_pairs={{0,4},{4,8},{8,12},{12,16},{16,20},{20,24},{24,28},{28,29},{29,25}... | collective-permute-start | bytes 208904 | tf_op jit(solution)/shard_map/ppermute | solution.py:349
  18.7 4.3 %collective-permute-start.5 = (bf16[272,128]{1,0:T(8,128)(2,1)S(1)}, bf16[272,128]{1,0:T(8,128)(2,1)S(1)}, u32[]{:S(2)}, u32[]{:S(2)}) collective-permute-start(bf16[272,128]{1,0:T(8,128)(2,1)S(1)} %get-tuple-element.242), channel_id=1, source_target_pairs={{4,0},{8,4},{12,8},{16,12},{20,16},{24,20},{28,24},{29,28},{25,29}... | collective-permute-start | bytes 208904 | tf_op jit(solution)/shard_map/ppermute | solution.py:349
  26.4 4.4 %collective-permute-start.6 = (bf16[272,128]{1,0:T(8,128)(2,1)S(1)}, bf16[272,128]{1,0:T(8,128)(2,1)S(1)}, u32[]{:S(2)}, u32[]{:S(2)}) collective-permute-start(bf16[272,128]{1,0:T(8,128)(2,1)S(1)} %get-tuple-element.245), channel_id=1, source_target_pairs={{0,4},{4,8},{8,12},{12,16},{16,20},{20,24},{24,28},{28,29},{29,25}... | collective-permute-start | bytes 208904 | tf_op jit(solution)/shard_map/ppermute | solution.py:349
  28.8 4.3 %collective-permute-start.7 = (bf16[272,128]{1,0:T(8,128)(2,1)S(1)}, bf16[272,128]{1,0:T(8,128)(2,1)S(1)}, u32[]{:S(2)}, u32[]{:S(2)}) collective-permute-start(bf16[272,128]{1,0:T(8,128)(2,1)S(1)} %get-tuple-element.246), channel_id=1, source_target_pairs={{4,0},{8,4},{12,8},{16,12},{20,16},{24,20},{28,24},{29,28},{25,29}... | collective-permute-start | bytes 208904 | tf_op jit(solution)/shard_map/ppermute | solution.py:349
  37.0 12.5 %all-to-all-start = ((f32[32,8,128]{2,1,0:T(8,128)}), f32[32,8,128]{2,1,0:T(8,128)S(1)}, u32[]{:S(2)}, u32[]{:S(2)}) async-start(f32[32,8,128]{2,1,0:T(8,128)} %get-tuple-element.248), calls=%async_computation | async-start | bytes 262144 | tf_op jit(solution)/shard_map/all_to_all | solution.py:394
  41.3 3.8 %collective-permute-start.8 = (bf16[144,128]{1,0:T(8,128)(2,1)S(1)}, bf16[144,128]{1,0:T(8,128)(2,1)S(1)}, u32[]{:S(2)}, u32[]{:S(2)}) collective-permute-start(bf16[144,128]{1,0:T(8,128)(2,1)S(1)} %get-tuple-element.253), channel_id=1, source_target_pairs={{0,4},{4,8},{8,12},{12,16},{16,20},{20,24},{24,28},{28,29},{29,25}... | collective-permute-start | bytes 110600 | tf_op jit(solution)/shard_map/ppermute | solution.py:349
  43.1 4.1 %collective-permute-start.9 = (bf16[144,128]{1,0:T(8,128)(2,1)S(1)}, bf16[144,128]{1,0:T(8,128)(2,1)S(1)}, u32[]{:S(2)}, u32[]{:S(2)}) collective-permute-start(bf16[144,128]{1,0:T(8,128)(2,1)S(1)} %get-tuple-element.254), channel_id=1, source_target_pairs={{4,0},{8,4},{12,8},{16,12},{20,16},{24,20},{28,24},{29,28},{25,29}... | collective-permute-start | bytes 110600 | tf_op jit(solution)/shard_map/ppermute | solution.py:349

commit v11 on v10

--- a/solution.py
+++ b/solution.py
@@ -39,12 +39,6 @@
     for slot in range(index_ref.shape[0]):
         block = index_ref[slot, group] - first
         partial_ref[block] += spread[:, slot * lanes : (slot + 1) * lanes]
-
-
-def spread_of(image, weights):
-    return lax.dot_general(
-        image, weights, (((1,), (1,)), ((), ())), preferred_element_type=jnp.float32
-    )
 
 
 def folded(value, rows, combine):
@@ -114,6 +108,7 @@
     data_ref,
     source_ref,
     kernels_ref,
+    turned_ref,
     partial_ref,
     onward_ref,
     return_ref,
@@ -142,7 +137,8 @@
         copy(chunk).wait()
         for group in range(chunk * size, (chunk + 1) * size):
             data = jnp.where(group < live, wide_ref[:, group, :], 0.0).astype(jnp.bfloat16)
-            spread = spread_of(data, kernels_ref[group].reshape(slots * spaxels, fibres))
+            turned_ref[group] = kernels_ref[group].reshape(slots * spaxels, fibres).T
+            spread = jnp.dot(data, turned_ref[group], preferred_element_type=jnp.float32)
             scatter(spread, place_ref, index_ref, group, partial_ref)
     emit_rims(lane_ref, partial_ref, onward_ref, return_ref)
 
@@ -160,6 +156,7 @@
     return_in_ref,
     moments_in_ref,
     kernels_ref,
+    turned_ref,
     vector_ref,
     partial_ref,
     onward_ref,
@@ -192,8 +189,9 @@
         energy = energy + image * image
         image_ref[group, :waves], image_ref[group, waves:] = split(image)
     for group in range(groups):
-        weights = kernels_ref[group].reshape(slots * spaxels, fibres)
-        spread = halves_sum(spread_of(image_ref[group], weights))
+        spread = halves_sum(
+            jnp.dot(image_ref[group], turned_ref[group], preferred_element_type=jnp.float32)
+        )
         scatter(spread, place_ref, index_ref, group, partial_ref)
     emit_rims(lane_ref, partial_ref, onward_ref, return_ref)
     for block in range(EXTENT):
@@ -334,7 +332,8 @@
     place = lax.axis_index("tile").reshape(1)
     lane = (lax.axis_index("wave") % 2).reshape(1)
     index = jnp.swapaxes(block_index, 1, 2).reshape(slots, groups)
-    weights = kernels.reshape(groups, slots, spaxels, fibres)
+    source = kernels.reshape(groups, slots, spaxels, fibres)
+    turned = jax.ShapeDtypeStruct((groups, fibres, slots * spaxels), kernels.dtype)
     window = jax.ShapeDtypeStruct((EXTENT, waves, spaxels), jnp.float32)
     rim = jax.ShapeDtypeStruct((RIM * waves + SCALE_ROWS, spaxels), jnp.bfloat16)
     half_rim = jax.ShapeDtypeStruct((HALO_BLOCKS * waves + SCALE_ROWS, spaxels), jnp.bfloat16)
@@ -349,11 +348,11 @@
         return lax.ppermute(onward, axes, circuit), lax.ppermute(back, axes, reverse)
 
     chunks = CHUNKS if groups % CHUNKS == 0 else 1
-    weights, held, onward, back = pl.pallas_call(
+    weights, turned, held, onward, back = pl.pallas_call(
         rhs_kernel,
-        out_shape=(jax.ShapeDtypeStruct(weights.shape, weights.dtype), window, rim, rim),
+        out_shape=(jax.ShapeDtypeStruct(source.shape, source.dtype), turned, window, rim, rim),
         in_specs=smem(4) + [pl.BlockSpec(memory_space=pltpu.HBM)] * 2,
-        out_specs=tuple(vmem(4)),
+        out_specs=tuple(vmem(5)),
         scratch_shapes=[
             pltpu.VMEM(fibre_data.shape, fibre_data.dtype),
             pltpu.VMEM(fibre_data.shape, jnp.float32),
@@ -368,7 +367,7 @@
         live_count,
         pltpu.with_memory_space_constraint(index, pltpu.HBM),
         pltpu.with_memory_space_constraint(fibre_data, pltpu.HBM),
-        pltpu.with_memory_space_constraint(weights, pltpu.HBM),
+        pltpu.with_memory_space_constraint(source, pltpu.HBM),
     )
     scratch = [
         pltpu.VMEM((EXTENT, 2 * waves, spaxels), jnp.bfloat16),
@@ -383,12 +382,12 @@
         vector, held, onward, back, moments = pl.pallas_call(
             functools.partial(step_kernel, tiles, power, final),
             out_shape=(window, window, out_rim, out_rim, moment_all if final else moment),
-            in_specs=smem(4) + vmem(5),
+            in_specs=smem(4) + vmem(6),
             out_specs=tuple(vmem(5)),
             scratch_shapes=scratch,
             compiler_params=params,
             name=f"step{power}",
-        )(place, lane, live_count, index, held, onward, back, moments, weights)
+        )(place, lane, live_count, index, held, onward, back, moments, weights, turned)
         vectors.append(vector)
     onward, back = swap(onward, back)
     moments = lax.all_to_all(moments, ("tile", "wave"), 0, 0)
@@ -436,7 +435,7 @@
             _, held, onward, back, _ = pl.pallas_call(
                 functools.partial(step_kernel, tiles, 0, False),
                 out_shape=(window, window, rim, rim, moment),
-                in_specs=smem(4) + vmem(5),
+                in_specs=smem(4) + vmem(6),
                 out_specs=tuple(vmem(5)),
                 scratch_shapes=scratch,
                 compiler_params=params,
@@ -450,7 +449,8 @@
                 none,
                 none,
                 jnp.zeros(moment.shape, jnp.float32),
-                weights,
+                source,
+                jnp.swapaxes(source.reshape(groups, slots * spaxels, fibres), 1, 2),
             )
             applied = settled(held, *swap(onward, back))
             size = norm / inner(direction, applied)

time: 52.6 us -> 50 us (0.951)
  Pallas kernels: 16.6 us -> 14 us
    pallas_call x3, Pallas kernels: 10.6 us -> 8.23 us  [shards(): pl.pallas_call(functools.partial(step_kernel, tiles, power, final), out_s...]
where the time goes in v11:
time: 50 us; the launch traced here: 49.8 us
  waiting for transfers between devices  19.3 us (39%)
  starting transfers between devices  14.1 us (28%)
  Pallas kernels  14 us (28%)
  between operations  2.16 us (4%)
    ppermute x4, starting transfers between devices, swap(): lax.ppermute(onward, axes, circuit)  9.77 us
    ppermute x4, waiting for transfers between devices, swap(): lax.ppermute(back, axes, reverse)  8.86 us
    pallas_call x3, Pallas kernels, shards(): pl.pallas_call(functools.partial(step_kernel, tiles, power, final), out_s...  8.23 us
    ppermute x4, waiting for transfers between devices, swap(): lax.ppermute(onward, axes, circuit)  8.14 us
    all_to_all x1, starting transfers between devices, shards(): moments = lax.all_to_all(moments, ('tile', 'wave'), 0, 0)  4.32 us
    pallas_call x1, Pallas kernels, shards(): pl.pallas_call(rhs_kernel, out_shape=(jax.ShapeDtypeStruct(source.shape,...  3.88 us
    all_to_all x1, waiting for transfers between devices, shards(): moments = lax.all_to_all(moments, ('tile', 'wave'), 0, 0)  2.29 us
    pallas_call x1, Pallas kernels, shards(): pl.pallas_call(functools.partial(final_kernel, tiles), out_shape=(out, ou...  1.88 us
  transfers between devices with their start and end apart: 9, of which 9 were waited for; matrix products, arithmetic and copies ran while one was open for 0% of the time, Pallas kernels for 0%

profile of v11, /device:TPU:0, one launch (start us, length us, event | category | flops | bytes accessed | tf_op | source)
XLA Modules:
  0.0 49.8 jit_solution(915874522805146069)
XLA Ops:
  0.6 0.0 copy-start
  1.3 3.9 %rhs.3 = (bf16[32,4,128,128]{3,2,1,0:T(8,128)(2,1)S(1)}, bf16[32,128,512]{2,1,0:T(8,128)(2,1)S(1)}, f32[24,32,128]{2,1,0:T(8,128)S(1)}, bf16[272,128]{1,0:T(8,128)(2,1)S(1)}, bf16[272,128]{1,0:T(8,128)(2,1)S(1)}) custom-call(s32[1]{0:T(128)} %bitcast.2.place_ref, s32[1]{0:T(128)} %bitcast.3.lane_ref, s32[1]{0:T(128)S(6)} %copy.40.live_ref, ...), custom_call_target="tpu_custom_call" | custom-call | tf_op jit(solution)/shard_map/rhs/pallas_call | solution.py:351
  5.2 3.0 %collective-permute-start.2 = (bf16[272,128]{1,0:T(8,128)(2,1)S(1)}, bf16[272,128]{1,0:T(8,128)(2,1)S(1)}, u32[]{:S(2)}, u32[]{:S(2)}) collective-permute-start(bf16[272,128]{1,0:T(8,128)(2,1)S(1)} %get-tuple-element.253), channel_id=1, source_target_pairs={{0,4},{4,8},{8,12},{12,16},{16,20},{20,24},{24,28},{28,29},{29,25}... | collective-permute-start | bytes 208904 | tf_op jit(solution)/shard_map/ppermute | solution.py:348
  8.2 0.0 collective-permute-start.3
  8.2 2.3 %collective-permute-done.2.onward_in_ref = bf16[272,128]{1,0:T(8,128)(2,1)S(1)} collective-permute-done((bf16[272,128]{1,0:T(8,128)(2,1)S(1)}, bf16[272,128]{1,0:T(8,128)(2,1)S(1)}, u32[]{:S(2)}, u32[]{:S(2)}) %collective-permute-start.2) | collective-permute-done | bytes 69664 | tf_op jit(solution)/shard_map/ppermute | solution.py:348
  10.6 2.0 %collective-permute-done.3.return_in_ref = bf16[272,128]{1,0:T(8,128)(2,1)S(1)} collective-permute-done((bf16[272,128]{1,0:T(8,128)(2,1)S(1)}, bf16[272,128]{1,0:T(8,128)(2,1)S(1)}, u32[]{:S(2)}, u32[]{:S(2)}) %collective-permute-start.3) | collective-permute-done | bytes 69664 | tf_op jit(solution)/shard_map/ppermute | solution.py:348
  12.5 0.0 copy-done
  12.5 2.6 %step0.1 = (f32[24,32,128]{2,1,0:T(8,128)S(1)}, f32[24,32,128]{2,1,0:T(8,128)S(1)}, bf16[272,128]{1,0:T(8,128)(2,1)S(1)}, bf16[272,128]{1,0:T(8,128)(2,1)S(1)}, f32[8,128]{1,0:T(8,128)S(1)}) custom-call(s32[1]{0:T(128)} %bitcast.2.place_ref, s32[1]{0:T(128)} %bitcast.3.lane_ref, s32[1]{0:T(128)S(6)} %copy.40.live_ref, s32[4,32]{1,0:T(4,128)S(1)} %bitcast.56, ...), custom_call_target="tpu_custom_call" | custom-call | tf_op jit(solution)/shard_map/step0/pallas_call | solution.py:382
  15.1 2.5 %collective-permute-start.4 = (bf16[272,128]{1,0:T(8,128)(2,1)S(1)}, bf16[272,128]{1,0:T(8,128)(2,1)S(1)}, u32[]{:S(2)}, u32[]{:S(2)}) collective-permute-start(bf16[272,128]{1,0:T(8,128)(2,1)S(1)} %get-tuple-element.258), channel_id=1, source_target_pairs={{0,4},{4,8},{8,12},{12,16},{16,20},{20,24},{24,28},{28,29},{29,25}... | collective-permute-start | bytes 208904 | tf_op jit(solution)/shard_map/ppermute | solution.py:348
  17.6 0.0 collective-permute-start.5
  17.6 1.9 %collective-permute-done.4.onward_in_ref = bf16[272,128]{1,0:T(8,128)(2,1)S(1)} collective-permute-done((bf16[272,128]{1,0:T(8,128)(2,1)S(1)}, bf16[272,128]{1,0:T(8,128)(2,1)S(1)}, u32[]{:S(2)}, u32[]{:S(2)}) %collective-permute-start.4) | collective-permute-done | bytes 69664 | tf_op jit(solution)/shard_map/ppermute | solution.py:348
  19.6 2.4 %collective-permute-done.5.return_in_ref = bf16[272,128]{1,0:T(8,128)(2,1)S(1)} collective-permute-done((bf16[272,128]{1,0:T(8,128)(2,1)S(1)}, bf16[272,128]{1,0:T(8,128)(2,1)S(1)}, u32[]{:S(2)}, u32[]{:S(2)}) %collective-permute-start.5) | collective-permute-done | bytes 69664 | tf_op jit(solution)/shard_map/ppermute | solution.py:348
  21.9 2.6 %step1.1 = (f32[24,32,128]{2,1,0:T(8,128)S(1)}, f32[24,32,128]{2,1,0:T(8,128)S(1)}, bf16[272,128]{1,0:T(8,128)(2,1)S(1)}, bf16[272,128]{1,0:T(8,128)(2,1)S(1)}, f32[8,128]{1,0:T(8,128)S(1)}) custom-call(s32[1]{0:T(128)} %bitcast.2.place_ref, s32[1]{0:T(128)} %bitcast.3.lane_ref, s32[1]{0:T(128)S(6)} %copy.40.live_ref, s32[4,32]{1,0:T(4,128)S(1)} %bitcast.57, ...), custom_call_target="tpu_custom_call" | custom-call | tf_op jit(solution)/shard_map/step1/pallas_call | solution.py:382
  24.5 2.4 %collective-permute-start.6 = (bf16[272,128]{1,0:T(8,128)(2,1)S(1)}, bf16[272,128]{1,0:T(8,128)(2,1)S(1)}, u32[]{:S(2)}, u32[]{:S(2)}) collective-permute-start(bf16[272,128]{1,0:T(8,128)(2,1)S(1)} %get-tuple-element.262), channel_id=1, source_target_pairs={{0,4},{4,8},{8,12},{12,16},{16,20},{20,24},{24,28},{28,29},{29,25}... | collective-permute-start | bytes 208904 | tf_op jit(solution)/shard_map/ppermute | solution.py:348
  26.9 0.0 collective-permute-start.7
  26.9 1.9 %collective-permute-done.6.onward_in_ref = bf16[272,128]{1,0:T(8,128)(2,1)S(1)} collective-permute-done((bf16[272,128]{1,0:T(8,128)(2,1)S(1)}, bf16[272,128]{1,0:T(8,128)(2,1)S(1)}, u32[]{:S(2)}, u32[]{:S(2)}) %collective-permute-start.6) | collective-permute-done | bytes 69664 | tf_op jit(solution)/shard_map/ppermute | solution.py:348
  28.9 2.4 %collective-permute-done.7.return_in_ref = bf16[272,128]{1,0:T(8,128)(2,1)S(1)} collective-permute-done((bf16[272,128]{1,0:T(8,128)(2,1)S(1)}, bf16[272,128]{1,0:T(8,128)(2,1)S(1)}, u32[]{:S(2)}, u32[]{:S(2)}) %collective-permute-start.7) | collective-permute-done | bytes 69664 | tf_op jit(solution)/shard_map/ppermute | solution.py:348
  31.2 3.1 %step2.1 = (f32[24,32,128]{2,1,0:T(8,128)S(1)}, f32[24,32,128]{2,1,0:T(8,128)S(1)}, bf16[144,128]{1,0:T(8,128)(2,1)S(1)}, bf16[144,128]{1,0:T(8,128)(2,1)S(1)}, f32[32,8,128]{2,1,0:T(8,128)}) custom-call(s32[1]{0:T(128)} %bitcast.2.place_ref, s32[1]{0:T(128)} %bitcast.3.lane_ref, s32[1]{0:T(128)S(6)} %copy.40.live_ref, s32[4,32]{1,0:T(4,128)S(1)} %bitcast.58, ...), custom_call_target="tpu_custom_call" | custom-call | tf_op jit(solution)/shard_map/step2/pallas_call | solution.py:382
  34.3 4.3 %all-to-all-start = ((f32[32,8,128]{2,1,0:T(8,128)}), f32[32,8,128]{2,1,0:T(8,128)S(1)}, u32[]{:S(2)}, u32[]{:S(2)}) async-start(f32[32,8,128]{2,1,0:T(8,128)} %get-tuple-element.265), calls=%async_computation | async-start | bytes 262144 | tf_op jit(solution)/shard_map/all_to_all | solution.py:393
  38.6 1.8 %collective-permute-start.8 = (bf16[144,128]{1,0:T(8,128)(2,1)S(1)}, bf16[144,128]{1,0:T(8,128)(2,1)S(1)}, u32[]{:S(2)}, u32[]{:S(2)}) collective-permute-start(bf16[144,128]{1,0:T(8,128)(2,1)S(1)} %get-tuple-element.270), channel_id=1, source_target_pairs={{0,4},{4,8},{8,12},{12,16},{16,20},{20,24},{24,28},{28,29},{29,25}... | collective-permute-start | bytes 110600 | tf_op jit(solution)/shard_map/ppermute | solution.py:348
  40.5 0.0 collective-permute-start.9
  40.5 1.9 %collective-permute-done.8.onward_in_ref = bf16[144,128]{1,0:T(8,128)(2,1)S(1)} collective-permute-done((bf16[144,128]{1,0:T(8,128)(2,1)S(1)}, bf16[144,128]{1,0:T(8,128)(2,1)S(1)}, u32[]{:S(2)}, u32[]{:S(2)}) %collective-permute-start.8) | collective-permute-done | bytes 36896 | tf_op jit(solution)/shard_map/ppermute | solution.py:348
  42.4 2.2 %collective-permute-done.9.return_in_ref = bf16[144,128]{1,0:T(8,128)(2,1)S(1)} collective-permute-done((bf16[144,128]{1,0:T(8,128)(2,1)S(1)}, bf16[144,128]{1,0:T(8,128)(2,1)S(1)}, u32[]{:S(2)}, u32[]{:S(2)}) %collective-permute-start.9) | collective-permute-done | bytes 36896 | tf_op jit(solution)/shard_map/ppermute | solution.py:348
  44.6 2.3 %all-to-all-done.moments_ref = f32[32,8,128]{2,1,0:T(8,128)S(1)} async-done(((f32[32,8,128]{2,1,0:T(8,128)}), f32[32,8,128]{2,1,0:T(8,128)S(1)}, u32[]{:S(2)}, u32[]{:S(2)}) %all-to-all-start) | async-done | bytes 131104 | tf_op jit(solution)/shard_map/all_to_all | solution.py:393
  46.8 1.9 %combine.1 = (f32[32,16,128]{2,1,0:T(8,128)}, f32[32,16,128]{2,1,0:T(8,128)}, s32[1]{0:T(128)}) custom-call(s32[1]{0:T(128)} %bitcast.2.place_ref, s32[1]{0:T(128)} %bitcast.3.lane_ref, f32[32,8,128]{2,1,0:T(8,128)S(1)} %all-to-all-done.moments_ref, f32[24,32,128]{2,1,0:T(8,128)S(1)} %get-tuple-element.266.first_ref, ...), custom_call_target="tpu_custom_call" | custom-call | tf_op jit(solution)/shard_map/combine/pallas_call | solution.py:395
  49.4 0.2 conditional.1
  (1 shorter events, 0.0 us)
Async XLA Ops:
  0.6 11.9 %copy-start = (s32[1,32,4]{1,2,0:T(4,128)S(1)}, s32[1,32,4]{1,2,0:T(4,128)}, u32[]{:S(2)}) copy-start(s32[1,32,4]{1,2,0:T(4,128)} %param.14) | copy-start | bytes 1540
  5.2 5.4 %collective-permute-start.2 = (bf16[272,128]{1,0:T(8,128)(2,1)S(1)}, bf16[272,128]{1,0:T(8,128)(2,1)S(1)}, u32[]{:S(2)}, u32[]{:S(2)}) collective-permute-start(bf16[272,128]{1,0:T(8,128)(2,1)S(1)} %get-tuple-element.253), channel_id=1, source_target_pairs={{0,4},{4,8},{8,12},{12,16},{16,20},{20,24},{24,28},{28,29},{29,25}... | collective-permute-start | bytes 208904 | tf_op jit(solution)/shard_map/ppermute | solution.py:348
  8.2 4.3 %collective-permute-start.3 = (bf16[272,128]{1,0:T(8,128)(2,1)S(1)}, bf16[272,128]{1,0:T(8,128)(2,1)S(1)}, u32[]{:S(2)}, u32[]{:S(2)}) collective-permute-start(bf16[272,128]{1,0:T(8,128)(2,1)S(1)} %get-tuple-element.254), channel_id=1, source_target_pairs={{4,0},{8,4},{12,8},{16,12},{20,16},{24,20},{28,24},{29,28},{25,29}... | collective-permute-start | bytes 208904 | tf_op jit(solution)/shard_map/ppermute | solution.py:348
  15.1 4.5 %collective-permute-start.4 = (bf16[272,128]{1,0:T(8,128)(2,1)S(1)}, bf16[272,128]{1,0:T(8,128)(2,1)S(1)}, u32[]{:S(2)}, u32[]{:S(2)}) collective-permute-start(bf16[272,128]{1,0:T(8,128)(2,1)S(1)} %get-tuple-element.258), channel_id=1, source_target_pairs={{0,4},{4,8},{8,12},{12,16},{16,20},{20,24},{24,28},{28,29},{29,25}... | collective-permute-start | bytes 208904 | tf_op jit(solution)/shard_map/ppermute | solution.py:348
  17.6 4.3 %collective-permute-start.5 = (bf16[272,128]{1,0:T(8,128)(2,1)S(1)}, bf16[272,128]{1,0:T(8,128)(2,1)S(1)}, u32[]{:S(2)}, u32[]{:S(2)}) collective-permute-start(bf16[272,128]{1,0:T(8,128)(2,1)S(1)} %get-tuple-element.259), channel_id=1, source_target_pairs={{4,0},{8,4},{12,8},{16,12},{20,16},{24,20},{28,24},{29,28},{25,29}... | collective-permute-start | bytes 208904 | tf_op jit(solution)/shard_map/ppermute | solution.py:348
  24.5 4.3 %collective-permute-start.6 = (bf16[272,128]{1,0:T(8,128)(2,1)S(1)}, bf16[272,128]{1,0:T(8,128)(2,1)S(1)}, u32[]{:S(2)}, u32[]{:S(2)}) collective-permute-start(bf16[272,128]{1,0:T(8,128)(2,1)S(1)} %get-tuple-element.262), channel_id=1, source_target_pairs={{0,4},{4,8},{8,12},{12,16},{16,20},{20,24},{24,28},{28,29},{29,25}... | collective-permute-start | bytes 208904 | tf_op jit(solution)/shard_map/ppermute | solution.py:348
  26.9 4.3 %collective-permute-start.7 = (bf16[272,128]{1,0:T(8,128)(2,1)S(1)}, bf16[272,128]{1,0:T(8,128)(2,1)S(1)}, u32[]{:S(2)}, u32[]{:S(2)}) collective-permute-start(bf16[272,128]{1,0:T(8,128)(2,1)S(1)} %get-tuple-element.263), channel_id=1, source_target_pairs={{4,0},{8,4},{12,8},{16,12},{20,16},{24,20},{28,24},{29,28},{25,29}... | collective-permute-start | bytes 208904 | tf_op jit(solution)/shard_map/ppermute | solution.py:348
  34.3 12.5 %all-to-all-start = ((f32[32,8,128]{2,1,0:T(8,128)}), f32[32,8,128]{2,1,0:T(8,128)S(1)}, u32[]{:S(2)}, u32[]{:S(2)}) async-start(f32[32,8,128]{2,1,0:T(8,128)} %get-tuple-element.265), calls=%async_computation | async-start | bytes 262144 | tf_op jit(solution)/shard_map/all_to_all | solution.py:393
  38.6 3.8 %collective-permute-start.8 = (bf16[144,128]{1,0:T(8,128)(2,1)S(1)}, bf16[144,128]{1,0:T(8,128)(2,1)S(1)}, u32[]{:S(2)}, u32[]{:S(2)}) collective-permute-start(bf16[144,128]{1,0:T(8,128)(2,1)S(1)} %get-tuple-element.270), channel_id=1, source_target_pairs={{0,4},{4,8},{8,12},{12,16},{16,20},{20,24},{24,28},{28,29},{29,25}... | collective-permute-start | bytes 110600 | tf_op jit(solution)/shard_map/ppermute | solution.py:348
  40.5 4.1 %collective-permute-start.9 = (bf16[144,128]{1,0:T(8,128)(2,1)S(1)}, bf16[144,128]{1,0:T(8,128)(2,1)S(1)}, u32[]{:S(2)}, u32[]{:S(2)}) collective-permute-start(bf16[144,128]{1,0:T(8,128)(2,1)S(1)} %get-tuple-element.271), channel_id=1, source_target_pairs={{4,0},{8,4},{12,8},{16,12},{20,16},{24,20},{28,24},{29,28},{25,29}... | collective-permute-start | bytes 110600 | tf_op jit(solution)/shard_map/ppermute | solution.py:348

commit v12 on v11

--- a/solution.py
+++ b/solution.py
@@ -204,7 +204,13 @@
         square_row,
         jnp.where(rows == 2 * power + 1, energy_row, moments_in_ref[...]),
     )
-    moments_ref[...] = jnp.broadcast_to(moments, moments_ref.shape) if final else moments
+    if not final:
+        moments_ref[...] = moments
+        return
+    lanes = lax.broadcasted_iota(jnp.int32, moments.shape, 1)
+    totals = jnp.sum(moments, axis=1, keepdims=True)
+    packed = jnp.sum(jnp.where(lanes == rows, totals, 0.0), axis=0, keepdims=True)
+    moments_ref[...] = jnp.broadcast_to(packed[None], moments_ref.shape)
 
 
 def coefficients(moments, steps):
@@ -259,12 +265,14 @@
     residual_buf,
     sems,
 ):
-    sums = moments_ref[0]
-    for source in range(1, moments_ref.shape[0]):
-        sums = sums + moments_ref[source]
-    sums = jnp.sum(sums, axis=1, keepdims=True)
-    lanes = first_ref.shape[2]
-    raw = [jnp.broadcast_to(sums[row : row + 1], (1, lanes)) for row in range(6)]
+    sums = jnp.sum(moments_ref[:, 0, :], axis=0, keepdims=True)
+    lanes = lax.broadcasted_iota(jnp.int32, sums.shape, 1)
+    raw = [
+        jnp.broadcast_to(
+            jnp.sum(jnp.where(lanes == row, sums, 0.0), axis=1, keepdims=True), sums.shape
+        )
+        for row in range(6)
+    ]
     unit = raw[0] / raw[1]
     scaled, factor = [], 1.0 / raw[0]
     for row in range(6):
@@ -338,7 +346,7 @@
     rim = jax.ShapeDtypeStruct((RIM * waves + SCALE_ROWS, spaxels), jnp.bfloat16)
     half_rim = jax.ShapeDtypeStruct((HALO_BLOCKS * waves + SCALE_ROWS, spaxels), jnp.bfloat16)
     moment = jax.ShapeDtypeStruct((MOMENT_ROWS, spaxels), jnp.float32)
-    moment_all = jax.ShapeDtypeStruct((devices, MOMENT_ROWS, spaxels), jnp.float32)
+    moment_all = jax.ShapeDtypeStruct((devices, 1, spaxels), jnp.float32)
     params = pltpu.CompilerParams(vmem_limit_bytes=VMEM_LIMIT)
     circuit = circuit_of(tiles, lax.axis_size("wave"))
     reverse = [(j, i) for i, j in circuit]

time: 50 us -> 51.3 us (1.026)
  starting transfers between devices: 14.1 us -> 14.8 us
  waiting for transfers between devices: 19.3 us -> 20 us
    all_to_all x1, waiting for transfers between devices: 2.29 us -> 7.1 us  [shards(): moments = lax.all_to_all(moments, ('tile', 'wave'), 0, 0)]
    ppermute x4, waiting for transfers between devices: 8.86 us -> 6.71 us  [swap(): lax.ppermute(back, axes, reverse)]
    ppermute x4, waiting for transfers between devices: 8.14 us -> 6.22 us  [swap(): lax.ppermute(onward, axes, circuit)]
    all_to_all x1, starting transfers between devices: 4.32 us -> 5.12 us  [shards(): moments = lax.all_to_all(moments, ('tile', 'wave'), 0, 0)]
  transfers between devices with their start and end apart: 9 -> 9, of which waited for: 9 -> 7; matrix products, arithmetic and copies ran while one was open for 0% -> 0% of each run, Pallas kernels for 0% -> 0%
where the time goes in v12:
time: 51.3 us; the launch traced here: 51.1 us
  waiting for transfers between devices  20 us (39%)
  starting transfers between devices  14.8 us (29%)
  Pallas kernels  13.9 us (27%)
  between operations  2.16 us (4%)
    ppermute x4, starting transfers between devices, swap(): lax.ppermute(onward, axes, circuit)  9.66 us
    pallas_call x3, Pallas kernels, shards(): pl.pallas_call(functools.partial(step_kernel, tiles, power, final), out_s...  8.14 us
    all_to_all x1, waiting for transfers between devices, shards(): moments = lax.all_to_all(moments, ('tile', 'wave'), 0, 0)  7.1 us
    ppermute x4, waiting for transfers between devices, swap(): lax.ppermute(back, axes, reverse)  6.71 us
    ppermute x4, waiting for transfers between devices, swap(): lax.ppermute(onward, axes, circuit)  6.22 us
    all_to_all x1, starting transfers between devices, shards(): moments = lax.all_to_all(moments, ('tile', 'wave'), 0, 0)  5.12 us
    pallas_call x1, Pallas kernels, shards(): pl.pallas_call(rhs_kernel, out_shape=(jax.ShapeDtypeStruct(source.shape,...  3.88 us
    pallas_call x1, Pallas kernels, shards(): pl.pallas_call(functools.partial(final_kernel, tiles), out_shape=(out, ou...  1.85 us
  transfers between devices with their start and end apart: 9, of which 7 were waited for; matrix products, arithmetic and copies ran while one was open for 0% of the time, Pallas kernels for 0%

profile of v12, /device:TPU:0, one launch (start us, length us, event | category | flops | bytes accessed | tf_op | source)
XLA Modules:
  0.0 51.1 jit_solution(11917616093059933087)
XLA Ops:
  0.6 0.0 copy-start
  1.3 3.9 %rhs.3 = (bf16[32,4,128,128]{3,2,1,0:T(8,128)(2,1)S(1)}, bf16[32,128,512]{2,1,0:T(8,128)(2,1)S(1)}, f32[24,32,128]{2,1,0:T(8,128)S(1)}, bf16[272,128]{1,0:T(8,128)(2,1)S(1)}, bf16[272,128]{1,0:T(8,128)(2,1)S(1)}) custom-call(s32[1]{0:T(128)} %bitcast.2.place_ref, s32[1]{0:T(128)} %bitcast.3.lane_ref, s32[1]{0:T(128)S(6)} %copy.40.live_ref, ...), custom_call_target="tpu_custom_call" | custom-call | tf_op jit(solution)/shard_map/rhs/pallas_call | solution.py:359
  5.2 3.0 %collective-permute-start.2 = (bf16[272,128]{1,0:T(8,128)(2,1)S(1)}, bf16[272,128]{1,0:T(8,128)(2,1)S(1)}, u32[]{:S(2)}, u32[]{:S(2)}) collective-permute-start(bf16[272,128]{1,0:T(8,128)(2,1)S(1)} %get-tuple-element.253), channel_id=1, source_target_pairs={{0,4},{4,8},{8,12},{12,16},{16,20},{20,24},{24,28},{28,29},{29,25}... | collective-permute-start | bytes 208904 | tf_op jit(solution)/shard_map/ppermute | solution.py:356
  8.2 0.0 collective-permute-start.3
  8.2 2.3 %collective-permute-done.2.onward_in_ref = bf16[272,128]{1,0:T(8,128)(2,1)S(1)} collective-permute-done((bf16[272,128]{1,0:T(8,128)(2,1)S(1)}, bf16[272,128]{1,0:T(8,128)(2,1)S(1)}, u32[]{:S(2)}, u32[]{:S(2)}) %collective-permute-start.2) | collective-permute-done | bytes 69664 | tf_op jit(solution)/shard_map/ppermute | solution.py:356
  10.5 2.0 %collective-permute-done.3.return_in_ref = bf16[272,128]{1,0:T(8,128)(2,1)S(1)} collective-permute-done((bf16[272,128]{1,0:T(8,128)(2,1)S(1)}, bf16[272,128]{1,0:T(8,128)(2,1)S(1)}, u32[]{:S(2)}, u32[]{:S(2)}) %collective-permute-start.3) | collective-permute-done | bytes 69664 | tf_op jit(solution)/shard_map/ppermute | solution.py:356
  12.5 0.0 copy-done
  12.5 2.6 %step0.1 = (f32[24,32,128]{2,1,0:T(8,128)S(1)}, f32[24,32,128]{2,1,0:T(8,128)S(1)}, bf16[272,128]{1,0:T(8,128)(2,1)S(1)}, bf16[272,128]{1,0:T(8,128)(2,1)S(1)}, f32[8,128]{1,0:T(8,128)S(1)}) custom-call(s32[1]{0:T(128)} %bitcast.2.place_ref, s32[1]{0:T(128)} %bitcast.3.lane_ref, s32[1]{0:T(128)S(6)} %copy.40.live_ref, s32[4,32]{1,0:T(4,128)S(1)} %bitcast.56, ...), custom_call_target="tpu_custom_call" | custom-call | tf_op jit(solution)/shard_map/step0/pallas_call | solution.py:390
  15.1 2.5 %collective-permute-start.4 = (bf16[272,128]{1,0:T(8,128)(2,1)S(1)}, bf16[272,128]{1,0:T(8,128)(2,1)S(1)}, u32[]{:S(2)}, u32[]{:S(2)}) collective-permute-start(bf16[272,128]{1,0:T(8,128)(2,1)S(1)} %get-tuple-element.258), channel_id=1, source_target_pairs={{0,4},{4,8},{8,12},{12,16},{16,20},{20,24},{24,28},{28,29},{29,25}... | collective-permute-start | bytes 208904 | tf_op jit(solution)/shard_map/ppermute | solution.py:356
  17.6 0.0 collective-permute-start.5
  17.6 1.9 %collective-permute-done.4.onward_in_ref = bf16[272,128]{1,0:T(8,128)(2,1)S(1)} collective-permute-done((bf16[272,128]{1,0:T(8,128)(2,1)S(1)}, bf16[272,128]{1,0:T(8,128)(2,1)S(1)}, u32[]{:S(2)}, u32[]{:S(2)}) %collective-permute-start.4) | collective-permute-done | bytes 69664 | tf_op jit(solution)/shard_map/ppermute | solution.py:356
  19.6 2.4 %collective-permute-done.5.return_in_ref = bf16[272,128]{1,0:T(8,128)(2,1)S(1)} collective-permute-done((bf16[272,128]{1,0:T(8,128)(2,1)S(1)}, bf16[272,128]{1,0:T(8,128)(2,1)S(1)}, u32[]{:S(2)}, u32[]{:S(2)}) %collective-permute-start.5) | collective-permute-done | bytes 69664 | tf_op jit(solution)/shard_map/ppermute | solution.py:356
  21.9 2.6 %step1.1 = (f32[24,32,128]{2,1,0:T(8,128)S(1)}, f32[24,32,128]{2,1,0:T(8,128)S(1)}, bf16[272,128]{1,0:T(8,128)(2,1)S(1)}, bf16[272,128]{1,0:T(8,128)(2,1)S(1)}, f32[8,128]{1,0:T(8,128)S(1)}) custom-call(s32[1]{0:T(128)} %bitcast.2.place_ref, s32[1]{0:T(128)} %bitcast.3.lane_ref, s32[1]{0:T(128)S(6)} %copy.40.live_ref, s32[4,32]{1,0:T(4,128)S(1)} %bitcast.57, ...), custom_call_target="tpu_custom_call" | custom-call | tf_op jit(solution)/shard_map/step1/pallas_call | solution.py:390
  24.5 2.5 %collective-permute-start.6 = (bf16[272,128]{1,0:T(8,128)(2,1)S(1)}, bf16[272,128]{1,0:T(8,128)(2,1)S(1)}, u32[]{:S(2)}, u32[]{:S(2)}) collective-permute-start(bf16[272,128]{1,0:T(8,128)(2,1)S(1)} %get-tuple-element.262), channel_id=1, source_target_pairs={{0,4},{4,8},{8,12},{12,16},{16,20},{20,24},{24,28},{28,29},{29,25}... | collective-permute-start | bytes 208904 | tf_op jit(solution)/shard_map/ppermute | solution.py:356
  27.0 0.0 collective-permute-start.7
  27.0 1.9 %collective-permute-done.6.onward_in_ref = bf16[272,128]{1,0:T(8,128)(2,1)S(1)} collective-permute-done((bf16[272,128]{1,0:T(8,128)(2,1)S(1)}, bf16[272,128]{1,0:T(8,128)(2,1)S(1)}, u32[]{:S(2)}, u32[]{:S(2)}) %collective-permute-start.6) | collective-permute-done | bytes 69664 | tf_op jit(solution)/shard_map/ppermute | solution.py:356
  28.9 2.4 %collective-permute-done.7.return_in_ref = bf16[272,128]{1,0:T(8,128)(2,1)S(1)} collective-permute-done((bf16[272,128]{1,0:T(8,128)(2,1)S(1)}, bf16[272,128]{1,0:T(8,128)(2,1)S(1)}, u32[]{:S(2)}, u32[]{:S(2)}) %collective-permute-start.7) | collective-permute-done | bytes 69664 | tf_op jit(solution)/shard_map/ppermute | solution.py:356
  31.3 3.0 %step2.1 = (f32[24,32,128]{2,1,0:T(8,128)S(1)}, f32[24,32,128]{2,1,0:T(8,128)S(1)}, bf16[144,128]{1,0:T(8,128)(2,1)S(1)}, bf16[144,128]{1,0:T(8,128)(2,1)S(1)}, f32[32,1,128]{2,1,0:T(1,128)}) custom-call(s32[1]{0:T(128)} %bitcast.2.place_ref, s32[1]{0:T(128)} %bitcast.3.lane_ref, s32[1]{0:T(128)S(6)} %copy.40.live_ref, s32[4,32]{1,0:T(4,128)S(1)} %bitcast.58, ...), custom_call_target="tpu_custom_call" | custom-call | tf_op jit(solution)/shard_map/step2/pallas_call | solution.py:390
  34.3 1.7 %collective-permute-start.8 = (bf16[144,128]{1,0:T(8,128)(2,1)S(1)}, bf16[144,128]{1,0:T(8,128)(2,1)S(1)}, u32[]{:S(2)}, u32[]{:S(2)}) collective-permute-start(bf16[144,128]{1,0:T(8,128)(2,1)S(1)} %get-tuple-element.270), channel_id=1, source_target_pairs={{0,4},{4,8},{8,12},{12,16},{16,20},{20,24},{24,28},{28,29},{29,25}... | collective-permute-start | bytes 110600 | tf_op jit(solution)/shard_map/ppermute | solution.py:356
  35.9 0.0 collective-permute-start.9
  35.9 5.1 %all-to-all-start = ((f32[32,1,128]{2,1,0:T(1,128)}), f32[32,1,128]{2,1,0:T(1,128)S(1)}, u32[]{:S(2)}, u32[]{:S(2)}) async-start(f32[32,1,128]{2,1,0:T(1,128)} %get-tuple-element.265), calls=%async_computation | async-start | bytes 32768 | tf_op jit(solution)/shard_map/all_to_all | solution.py:401
  41.1 7.1 %all-to-all-done.moments_ref = f32[32,1,128]{2,1,0:T(1,128)S(1)} async-done(((f32[32,1,128]{2,1,0:T(1,128)}), f32[32,1,128]{2,1,0:T(1,128)S(1)}, u32[]{:S(2)}, u32[]{:S(2)}) %all-to-all-start) | async-done | bytes 16416 | tf_op jit(solution)/shard_map/all_to_all | solution.py:401
  48.2 0.0 collective-permute-done.8.onward_in_ref
  48.2 0.0 collective-permute-done.9.return_in_ref
  48.2 1.9 %combine.1 = (f32[32,16,128]{2,1,0:T(8,128)}, f32[32,16,128]{2,1,0:T(8,128)}, s32[1]{0:T(128)}) custom-call(s32[1]{0:T(128)} %bitcast.2.place_ref, s32[1]{0:T(128)} %bitcast.3.lane_ref, f32[32,1,128]{2,1,0:T(1,128)S(1)} %all-to-all-done.moments_ref, f32[24,32,128]{2,1,0:T(8,128)S(1)} %get-tuple-element.266.first_ref, ...), custom_call_target="tpu_custom_call" | custom-call | tf_op jit(solution)/shard_map/combine/pallas_call | solution.py:403
  50.7 0.2 conditional.1
  (1 shorter events, 0.0 us)
Async XLA Ops:
  0.6 11.9 %copy-start = (s32[1,32,4]{1,2,0:T(4,128)S(1)}, s32[1,32,4]{1,2,0:T(4,128)}, u32[]{:S(2)}) copy-start(s32[1,32,4]{1,2,0:T(4,128)} %param.14) | copy-start | bytes 1540
  5.2 5.4 %collective-permute-start.2 = (bf16[272,128]{1,0:T(8,128)(2,1)S(1)}, bf16[272,128]{1,0:T(8,128)(2,1)S(1)}, u32[]{:S(2)}, u32[]{:S(2)}) collective-permute-start(bf16[272,128]{1,0:T(8,128)(2,1)S(1)} %get-tuple-element.253), channel_id=1, source_target_pairs={{0,4},{4,8},{8,12},{12,16},{16,20},{20,24},{24,28},{28,29},{29,25}... | collective-permute-start | bytes 208904 | tf_op jit(solution)/shard_map/ppermute | solution.py:356
  8.2 4.3 %collective-permute-start.3 = (bf16[272,128]{1,0:T(8,128)(2,1)S(1)}, bf16[272,128]{1,0:T(8,128)(2,1)S(1)}, u32[]{:S(2)}, u32[]{:S(2)}) collective-permute-start(bf16[272,128]{1,0:T(8,128)(2,1)S(1)} %get-tuple-element.254), channel_id=1, source_target_pairs={{4,0},{8,4},{12,8},{16,12},{20,16},{24,20},{28,24},{29,28},{25,29}... | collective-permute-start | bytes 208904 | tf_op jit(solution)/shard_map/ppermute | solution.py:356
  15.1 4.5 %collective-permute-start.4 = (bf16[272,128]{1,0:T(8,128)(2,1)S(1)}, bf16[272,128]{1,0:T(8,128)(2,1)S(1)}, u32[]{:S(2)}, u32[]{:S(2)}) collective-permute-start(bf16[272,128]{1,0:T(8,128)(2,1)S(1)} %get-tuple-element.258), channel_id=1, source_target_pairs={{0,4},{4,8},{8,12},{12,16},{16,20},{20,24},{24,28},{28,29},{29,25}... | collective-permute-start | bytes 208904 | tf_op jit(solution)/shard_map/ppermute | solution.py:356
  17.6 4.3 %collective-permute-start.5 = (bf16[272,128]{1,0:T(8,128)(2,1)S(1)}, bf16[272,128]{1,0:T(8,128)(2,1)S(1)}, u32[]{:S(2)}, u32[]{:S(2)}) collective-permute-start(bf16[272,128]{1,0:T(8,128)(2,1)S(1)} %get-tuple-element.259), channel_id=1, source_target_pairs={{4,0},{8,4},{12,8},{16,12},{20,16},{24,20},{28,24},{29,28},{25,29}... | collective-permute-start | bytes 208904 | tf_op jit(solution)/shard_map/ppermute | solution.py:356
  24.5 4.4 %collective-permute-start.6 = (bf16[272,128]{1,0:T(8,128)(2,1)S(1)}, bf16[272,128]{1,0:T(8,128)(2,1)S(1)}, u32[]{:S(2)}, u32[]{:S(2)}) collective-permute-start(bf16[272,128]{1,0:T(8,128)(2,1)S(1)} %get-tuple-element.262), channel_id=1, source_target_pairs={{0,4},{4,8},{8,12},{12,16},{16,20},{20,24},{24,28},{28,29},{29,25}... | collective-permute-start | bytes 208904 | tf_op jit(solution)/shard_map/ppermute | solution.py:356
  27.0 4.3 %collective-permute-start.7 = (bf16[272,128]{1,0:T(8,128)(2,1)S(1)}, bf16[272,128]{1,0:T(8,128)(2,1)S(1)}, u32[]{:S(2)}, u32[]{:S(2)}) collective-permute-start(bf16[272,128]{1,0:T(8,128)(2,1)S(1)} %get-tuple-element.263), channel_id=1, source_target_pairs={{4,0},{8,4},{12,8},{16,12},{20,16},{24,20},{28,24},{29,28},{25,29}... | collective-permute-start | bytes 208904 | tf_op jit(solution)/shard_map/ppermute | solution.py:356
  34.3 13.9 %collective-permute-start.8 = (bf16[144,128]{1,0:T(8,128)(2,1)S(1)}, bf16[144,128]{1,0:T(8,128)(2,1)S(1)}, u32[]{:S(2)}, u32[]{:S(2)}) collective-permute-start(bf16[144,128]{1,0:T(8,128)(2,1)S(1)} %get-tuple-element.270), channel_id=1, source_target_pairs={{0,4},{4,8},{8,12},{12,16},{16,20},{20,24},{24,28},{28,29},{29,25}... | collective-permute-start | bytes 110600 | tf_op jit(solution)/shard_map/ppermute | solution.py:356
  35.9 12.2 %collective-permute-start.9 = (bf16[144,128]{1,0:T(8,128)(2,1)S(1)}, bf16[144,128]{1,0:T(8,128)(2,1)S(1)}, u32[]{:S(2)}, u32[]{:S(2)}) collective-permute-start(bf16[144,128]{1,0:T(8,128)(2,1)S(1)} %get-tuple-element.271), channel_id=1, source_target_pairs={{4,0},{8,4},{12,8},{16,12},{20,16},{24,20},{28,24},{29,28},{25,29}... | collective-permute-start | bytes 110600 | tf_op jit(solution)/shard_map/ppermute | solution.py:356
  35.9 12.2 %all-to-all-start = ((f32[32,1,128]{2,1,0:T(1,128)}), f32[32,1,128]{2,1,0:T(1,128)S(1)}, u32[]{:S(2)}, u32[]{:S(2)}) async-start(f32[32,1,128]{2,1,0:T(1,128)} %get-tuple-element.265), calls=%async_computation | async-start | bytes 32768 | tf_op jit(solution)/shard_map/all_to_all | solution.py:401
